TPU v7x, 256 devices: a whole 4x4x8 slice. The times are simulated.
256 devices in a mesh: dp: 32 (over z_lo, x, core), group: 8 (over y, z_hi).
Axes of the slice: x: 4, y: 4, z: 8 (z_hi: 2, z_lo: 4; z = z_hi * 4 + z_lo), core: 2. Of those that a mesh axis runs over, the one named last changes fastest.
Arguments:
- tokens: bfloat16 [32768, 7168], P('dp', 'group'), may hold values from -6 to 6
- proj_in: bfloat16 [32, 1024, 2, 7168], P(None, 'dp', None, 'group'), may hold values from -0.0625 to 0.0625
- proj_out: bfloat16 [32, 1024, 7168], P(None, 'dp', 'group'), may hold values from -0.1875 to 0.1875
- expert_list: int32 [32, 2], replicated, may hold values from 0 to 31, as said below
- block_pattern: int32 [32, 2, 8], replicated, may hold values from 0 to 1, as said below
- route_weight: float32 [32768, 2], P('dp'), may hold values from 0.1 to 1
Outputs:
- mixed: bfloat16 [32768, 7168], P('dp', 'group')
Inputs may be any that keep to these rules, and one draw needn't show every extreme that they name: `expert_list`: each row names 2 different experts of the window. `block_pattern`: 1 where the list slot's expert acts on that block of 128 tokens, else 0; the share of ones differs from token group to token group, and in every draw some token group has every block of every slot set.
All inputs are finite; a program needn't handle non-finite values.
Results may differ from a plain program's by a relative error of at most 0.025.
Values may be sent and summed in bfloat16 or wider, within the bound.
A program may use at most 128 MiB of HBM per device.

v0:
```python
import jax
import jax.numpy as jnp
from jax import lax
from jax.experimental import pallas as pl
from jax.experimental.pallas import tpu as pltpu
from jax.sharding import PartitionSpec as P


Y_PARTS = 4


def _perm(size, fn):
    return [(j, fn(j)) for j in range(size)]


def _y_shift(size, dy):
    z_parts = size // Y_PARTS
    return _perm(size, lambda j: ((j // z_parts + dy) % Y_PARTS) * z_parts + j % z_parts)


def _z_flip(size):
    return _perm(size, lambda j: j ^ 1)


def _rs_kernel(x_ref, out_ref, ybuf, own, zsend, zrecv, send_sem, recv_sem, local_sem):
    size = lax.axis_size("group")
    z_parts = size // Y_PARTS
    j = lax.axis_index("group")
    y, zh = j // z_parts, j % z_parts
    rows = x_ref.shape[0] // Y_PARTS
    half = rows // 2

    def peer(dy):
        return ((y + dy) % Y_PARTS) * z_parts + zh

    partner = y * z_parts + (1 - zh)
    shifts = (1, Y_PARTS - 1, 2)
    barrier = pltpu.get_barrier_semaphore()
    for dy in shifts:
        pl.semaphore_signal(barrier, inc=1, device_id={"group": peer(dy)},
                            device_id_type=pl.DeviceIdType.MESH)
    pl.semaphore_signal(barrier, inc=1, device_id={"group": partner},
                        device_id_type=pl.DeviceIdType.MESH)
    pl.semaphore_wait(barrier, len(shifts) + 1)

    copies = []
    for k, dy in enumerate(shifts):
        start = pl.multiple_of(((y + dy) % Y_PARTS) * rows, rows)
        c = pltpu.make_async_remote_copy(
            src_ref=x_ref.at[pl.ds(start, rows)],
            dst_ref=ybuf.at[k],
            send_sem=send_sem.at[k],
            recv_sem=recv_sem.at[k],
            device_id={"group": peer(dy)},
            device_id_type=pl.DeviceIdType.MESH,
        )
        c.start()
        copies.append(c)
    mine_start = pl.multiple_of(y * rows, rows)
    local = pltpu.make_async_copy(x_ref.at[pl.ds(mine_start, rows)], own, local_sem.at[0])
    local.start()
    local.wait()
    for c in copies:
        c.wait()

    f32 = jnp.float32

    def y_sum(lo):
        sl = pl.ds(lo, half)
        total = own[sl, :].astype(f32)
        for k in range(len(shifts)):
            total = total + ybuf[k, sl, :].astype(f32)
        return total

    other_lo = pl.multiple_of((1 - zh) * half, half)
    mine_lo = pl.multiple_of(zh * half, half)
    zsend[...] = y_sum(other_lo).astype(zsend.dtype)
    zc = pltpu.make_async_remote_copy(
        src_ref=zsend, dst_ref=zrecv, send_sem=send_sem.at[3], recv_sem=recv_sem.at[3],
        device_id={"group": partner}, device_id_type=pl.DeviceIdType.MESH,
    )
    zc.start()
    out_ref[...] = y_sum(mine_lo)
    zc.wait()
    out_ref[...] += zrecv[...].astype(f32)


def group_reduce_scatter(x, collective_id=0):
    size = lax.axis_size("group")
    r, c = x.shape
    rows = r // Y_PARTS
    half = rows // 2
    return pl.pallas_call(
        _rs_kernel,
        out_shape=jax.ShapeDtypeStruct((r // size, c), jnp.float32),
        in_specs=[pl.BlockSpec(memory_space=pl.ANY)],
        out_specs=pl.BlockSpec(memory_space=pltpu.VMEM),
        scratch_shapes=[
            pltpu.VMEM((3, rows, c), x.dtype),
            pltpu.VMEM((rows, c), x.dtype),
            pltpu.VMEM((half, c), x.dtype),
            pltpu.VMEM((half, c), x.dtype),
            pltpu.SemaphoreType.DMA((4,)),
            pltpu.SemaphoreType.DMA((4,)),
            pltpu.SemaphoreType.DMA((1,)),
        ],
        compiler_params=pltpu.CompilerParams(
            collective_id=collective_id, has_side_effects=True, vmem_limit_bytes=48 * 1024 * 1024
        ),
    )(x)


def group_all_gather(h):
    size = lax.axis_size("group")
    j = lax.axis_index("group")
    y, zh = j // 2, j % 2
    n = h.shape[0]
    partner = lax.ppermute(h, "group", _z_flip(size))
    pair = jnp.where(zh == 0, jnp.concatenate([h, partner]), jnp.concatenate([partner, h]))
    from_down = lax.ppermute(pair, "group", _y_shift(size, 1))
    from_up = lax.ppermute(pair, "group", _y_shift(size, -1))
    far_a = lax.ppermute(from_down[:n], "group", _y_shift(size, 1))
    far_b = lax.ppermute(from_up[n:], "group", _y_shift(size, -1))
    out = jnp.zeros((Y_PARTS * 2 * n,) + h.shape[1:], h.dtype)
    for dy, piece in ((0, pair), (-1, from_down), (1, from_up),
                      (2, jnp.concatenate([far_a, far_b]))):
        out = lax.dynamic_update_slice_in_dim(out, piece, ((y + dy) % Y_PARTS) * 2 * n, 0)
    return out


def on_device(tokens, proj_in, proj_out, expert_list, block_pattern, route_weight):
    group_size = lax.axis_size("group")
    n_dp = lax.axis_size("dp")
    dp_index = lax.axis_index("dp")
    row_count, width_here = tokens.shape
    slots = expert_list.shape[1]
    ff_here = proj_in.shape[1]
    block_rows = row_count // block_pattern.shape[2]

    own_pattern = lax.dynamic_index_in_dim(block_pattern, dp_index, 0, keepdims=False)
    block_mask = jnp.repeat(own_pattern, block_rows, axis=1).astype(jnp.float32)
    token_scale = route_weight.T * block_mask

    send_in = jnp.take(proj_in, expert_list, axis=0, mode="clip").transpose(0, 1, 3, 2, 4)
    send_out = jnp.take(proj_out, expert_list, axis=0, mode="clip")

    hiddens = []
    weights_out = []
    pending = tokens
    for slot in range(slots):
        pending, piece = lax.optimization_barrier((pending, send_in[:, slot]))
        weight_in = lax.all_to_all(piece, "dp", 0, 0, tiled=True).reshape(-1, width_here)
        if hiddens:
            weight_in, hiddens[-1] = lax.optimization_barrier((weight_in, hiddens[-1]))
        partial_here = jnp.dot(weight_in, tokens.T, preferred_element_type=jnp.float32)
        partial_here = partial_here.astype(jnp.bfloat16)
        shares = group_reduce_scatter(partial_here, collective_id=slot)
        shares = shares.reshape(n_dp // group_size, 2, ff_here, row_count)
        hidden = (token_scale[slot] * jax.nn.silu(shares[:, 0]) * shares[:, 1]).astype(jnp.bfloat16)
        hiddens.append(group_all_gather(hidden.reshape(-1, row_count)))
        pending = partial_here
    for slot in range(slots):
        pending, piece = lax.optimization_barrier((pending, send_out[:, slot]))
        weight_out = lax.all_to_all(piece, "dp", 0, 0, tiled=True)
        weights_out.append(weight_out.reshape(-1, width_here))
        pending = weight_out

    combined = None
    for slot in range(slots):
        term = lax.dot_general(
            hiddens[slot], weights_out[slot], (((0,), (0,)), ((), ())),
            preferred_element_type=jnp.float32,
        )
        combined = term if combined is None else combined + term
    return combined.astype(jnp.bfloat16)


def solution(mesh):
    return jax.shard_map(
        on_device,
        mesh=mesh,
        in_specs=(
            P("dp", "group"),
            P(None, "dp", None, "group"),
            P(None, "dp", "group"),
            P(),
            P(),
            P("dp", None),
        ),
        out_specs=P("dp", "group"),
        check_vma=False,
    )
```

profile of v0, /device:TPU:24, one launch (start us, length us, event | category | flops | bytes accessed | tf_op | source)
XLA Modules:
  0.0 455.0 jit_solution(3269773153401134461)
XLA Ops:
  0.0 0.9 copy.10
  0.9 0.1 reshape.37
  1.0 19.4 %gather_fusion = bf16[64,32,2,896]{3,2,1,0:T(2,128)(2,1)} fusion(bf16[32,32,2,896]{3,2,1,0:T(2,128)(2,1)} %param.7, s32[1024]{0:T(1024)S(1)} %pad_clamp_fusion), kind=kCustom, calls=%fused_computation | custom fusion | bytes 14680320 | tf_op jit(solution)/shard_map/jit(_take)/gather | solution.py:144
  20.5 4.7 %copy.11 = bf16[64,32,2,896]{3,1,2,0:T(8,128)(2,1)S(1)} copy(bf16[64,32,2,896]{3,2,1,0:T(2,128)(2,1)} %gather_fusion) | data formatting | bytes 14680064 | tf_op jit(solution)/shard_map/jit(_take)/gather | solution.py:144
  25.2 2.6 slice_bitcast_fusion
  27.8 91.8 %all_to_all.20 = bf16[32,2,32,896]{3,2,1,0:T(8,128)(2,1)S(1)} all-to-all(bf16[32,2,32,896]{3,2,1,0:T(8,128)(2,1)S(1)} %get-tuple-element.11), channel_id=1, replica_groups=mesh['dp'=32,'group'=8] {'dp'}, dimensions={0} | all-to-all | bytes 7340032 | tf_op jit(solution)/shard_map/all_to_all | solution.py:152
  119.6 6.3 %convolution_convert_fusion.1.x_ref = bf16[2048,1024]{1,0:T(8,128)(2,1)} fusion(bf16[2048,896]{1,0:T(8,128)(2,1)S(1)} %bitcast.76, bf16[1024,896]{1,0:T(8,128)(2,1)S(1)} %copy-done), kind=kOutput, calls=%fused_computation.3 | convolution fusion | flops 3760193536 | bytes 9699328 | tf_op jit(solution)/shard_map/dot_general | solution.py:155
  125.9 5.0 %all-to-all-start.1 = ((bf16[32,2,32,896]{3,2,1,0:T(8,128)(2,1)}), bf16[32,2,32,896]{3,2,1,0:T(8,128)(2,1)}, u32[]{:S(2)}, u32[]{:S(2)}) async-start(bf16[32,2,32,896]{3,2,1,0:T(8,128)(2,1)} %get-tuple-element.12), calls=%async_computation.1 | async-start | bytes 7340032 | tf_op jit(solution)/shard_map/all_to_all | solution.py:152
  130.9 0.2 convert_reduce_fusion
  131.2 2.2 copy-done.2
  133.3 87.2 %shard_map.64 = f32[256,1024]{1,0:T(8,128)S(1)} custom-call(bf16[2048,1024]{1,0:T(8,128)(2,1)S(1)} %copy-done.2), custom_call_target="tpu_custom_call" | custom-call | tf_op jit(solution)/shard_map/pallas_call | solution.py:93
  220.6 0.1 fusion.11
  220.7 0.2 fusion.5
  220.9 1.6 collective-permute-start
  222.5 12.2 %collective-permute-done = bf16[128,1024]{1,0:T(8,128)(2,1)S(1)} collective-permute-done((bf16[128,1024]{1,0:T(8,128)(2,1)S(1)}, bf16[128,1024]{1,0:T(8,128)(2,1)S(1)}, u32[]{:S(2)}, u32[]{:S(2)}) %collective-permute-start) | collective-permute-done | bytes 262176 | tf_op jit(solution)/shard_map/ppermute | solution.py:118
  234.7 1.7 broadcast.19.clone
  236.4 1.0 constant_dynamic-update-slice_fusion.5
  237.4 0.8 collective-permute-start.2
  238.2 2.4 collective-permute-start.1
  240.6 4.2 gather_fusion.1
  244.9 7.5 %collective-permute-done.2 = bf16[256,1024]{1,0:T(8,128)(2,1)S(1)} collective-permute-done((bf16[256,1024]{1,0:T(8,128)(2,1)S(1)}, bf16[256,1024]{1,0:T(8,128)(2,1)S(1)}, u32[]{:S(2)}, u32[]{:S(2)}) %collective-permute-start.2) | collective-permute-done | bytes 524320 | tf_op jit(solution)/shard_map/ppermute | solution.py:121
  252.4 0.7 slice.66
  253.1 3.3 collective-permute-start.3
  256.4 4.2 slice_bitcast_fusion.2
  260.6 0.9 constant_dynamic-update-slice_fusion.4
  261.5 0.8 constant_dynamic-update-slice_fusion.3
  262.3 1.8 maximum_dynamic-update-slice_fusion
  264.1 8.3 %convolution_convert_fusion.x_ref = bf16[2048,1024]{1,0:T(8,128)(2,1)} fusion(bf16[2048,896]{1,0:T(8,128)(2,1)} %bitcast.6, bf16[1024,896]{1,0:T(8,128)(2,1)S(1)} %copy-done), kind=kOutput, calls=%fused_computation.2 | convolution fusion | flops 3760193536 | bytes 9699328 | tf_op jit(solution)/shard_map/dot_general | solution.py:155
  272.5 51.5 %all_to_all.21 = bf16[32,32,896]{2,1,0:T(8,128)(2,1)} all-to-all(bf16[32,32,896]{2,1,0:T(8,128)(2,1)S(1)} %copy-done.4), channel_id=1, replica_groups=mesh['dp'=32,'group'=8] {'dp'}, dimensions={0} | all-to-all | bytes 3670016 | tf_op jit(solution)/shard_map/all_to_all | solution.py:164
  324.0 5.7 %all-to-all-start.3 = ((bf16[32,32,896]{2,1,0:T(8,128)(2,1)}), bf16[32,32,896]{2,1,0:T(8,128)(2,1)}, u32[]{:S(2)}, u32[]{:S(2)}) async-start(bf16[32,32,896]{2,1,0:T(8,128)(2,1)} %get-tuple-element.16), calls=%async_computation.3 | async-start | bytes 3670016 | tf_op jit(solution)/shard_map/all_to_all | solution.py:164
  329.7 2.2 copy-done.3
  331.9 65.5 %shard_map.65 = f32[256,1024]{1,0:T(8,128)S(1)} custom-call(bf16[2048,1024]{1,0:T(8,128)(2,1)S(1)} %copy-done.3), custom_call_target="tpu_custom_call" | custom-call | tf_op jit(solution)/shard_map/pallas_call | solution.py:93
  397.3 0.1 fusion.10
  397.4 0.2 fusion
  397.6 1.9 collective-permute-start.5
  399.5 15.6 %collective-permute-done.5 = bf16[128,1024]{1,0:T(8,128)(2,1)S(1)} collective-permute-done((bf16[128,1024]{1,0:T(8,128)(2,1)S(1)}, bf16[128,1024]{1,0:T(8,128)(2,1)S(1)}, u32[]{:S(2)}, u32[]{:S(2)}) %collective-permute-start.5) | collective-permute-done | bytes 262176 | tf_op jit(solution)/shard_map/ppermute | solution.py:118
  415.1 1.6 broadcast.19
  416.7 1.0 constant_dynamic-update-slice_fusion.2
  417.7 0.6 collective-permute-start.7
  418.2 2.7 collective-permute-start.6
  420.9 11.8 %collective-permute-done.7 = bf16[256,1024]{1,0:T(8,128)(2,1)S(1)} collective-permute-done((bf16[256,1024]{1,0:T(8,128)(2,1)S(1)}, bf16[256,1024]{1,0:T(8,128)(2,1)S(1)}, u32[]{:S(2)}, u32[]{:S(2)}) %collective-permute-start.7) | collective-permute-done | bytes 524320 | tf_op jit(solution)/shard_map/ppermute | solution.py:121
  432.9 3.5 collective-permute-start.8
  436.4 0.8 constant_dynamic-update-slice_fusion.1
  437.2 0.8 constant_dynamic-update-slice_fusion
  438.0 3.4 collective-permute-done.9
  441.4 0.8 maximum_dynamic-update-slice_fusion.1
  442.2 5.8 %fusion.13 = f32[1024,896]{1,0:T(8,128)} fusion(bf16[1024,1024]{1,0:T(8,128)(2,1)} %maximum_dynamic-update-slice_fusion, bf16[1024,896]{1,0:T(8,128)(2,1)S(1)} %bitcast.77), kind=kOutput, calls=%fused_computation.42 | convolution fusion | flops 1879048192 | bytes 7602176 | tf_op jit(solution)/shard_map/dot_general | solution.py:170
  448.0 7.0 %add_convert_fusion = bf16[1024,896]{1,0:T(8,128)(2,1)} fusion(f32[1024,896]{1,0:T(8,128)} %fusion.13, bf16[1024,1024]{1,0:T(8,128)(2,1)} %maximum_dynamic-update-slice_fusion.1, bf16[1024,896]{1,0:T(8,128)(2,1)} %bitcast.20), kind=kOutput, calls=%fused_computation.6 | convolution fusion | flops 1880883200 | bytes 9437184 | tf_op jit(solution)/shard_map/dot_general | solution.py:170
  (30 shorter events, 0.3 us)
Async XLA Ops:
  0.0 119.6 %copy-start = (bf16[1024,896]{1,0:T(8,128)(2,1)S(1)}, bf16[1024,896]{1,0:T(8,128)(2,1)}, u32[]{:S(2)}) copy-start(bf16[1024,896]{1,0:T(8,128)(2,1)} %param.6) | copy-start | bytes 5505028
  125.9 5.0 %copy-start.7 = (s32[32,2,8]{0,2,1:T(8,128)S(1)}, s32[32,2,8]{0,2,1:T(8,128)}, u32[]{:S(2)}) copy-start(s32[32,2,8]{0,2,1:T(8,128)} %param.10) | copy-start | bytes 6148
  125.9 5.3 %copy-start.6 = (f32[1024,2]{0,1:T(2,128)S(1)}, f32[1024,2]{0,1:T(2,128)}, u32[]{:S(2)}) copy-start(f32[1024,2]{0,1:T(2,128)} %param.11) | copy-start | bytes 24580
  125.9 138.3 %all-to-all-start.1 = ((bf16[32,2,32,896]{3,2,1,0:T(8,128)(2,1)}), bf16[32,2,32,896]{3,2,1,0:T(8,128)(2,1)}, u32[]{:S(2)}, u32[]{:S(2)}) async-start(bf16[32,2,32,896]{3,2,1,0:T(8,128)(2,1)} %get-tuple-element.12), calls=%async_computation.1 | async-start | bytes 7340032 | tf_op jit(solution)/shard_map/all_to_all | solution.py:152
  131.2 2.2 copy-start.2
  220.9 13.8 %collective-permute-start = (bf16[128,1024]{1,0:T(8,128)(2,1)S(1)}, bf16[128,1024]{1,0:T(8,128)(2,1)S(1)}, u32[]{:S(2)}, u32[]{:S(2)}) collective-permute-start(bf16[128,1024]{1,0:T(8,128)(2,1)S(1)} %fusion.5), channel_id=1, source_target_pairs={{0,1},{1,0},{2,3},{3,2},{4,5},{5,4},{6,7},{7,6},{8,9},{9,8},{10,11... | collective-permute-start | bytes 786440 | tf_op jit(solution)/shard_map/ppermute | solution.py:118
  237.4 15.0 %collective-permute-start.2 = (bf16[256,1024]{1,0:T(8,128)(2,1)S(1)}, bf16[256,1024]{1,0:T(8,128)(2,1)S(1)}, u32[]{:S(2)}, u32[]{:S(2)}) collective-permute-start(bf16[256,1024]{1,0:T(8,128)(2,1)S(1)} %get-tuple-element.20), channel_id=1, source_target_pairs={{0,6},{1,7},{2,0},{3,1},{4,2},{5,3},{6,4},{7,5},{8,14},{9,15},{10,... | collective-permute-start | bytes 1572872 | tf_op jit(solution)/shard_map/ppermute | solution.py:121
  238.2 14.9 %collective-permute-start.1 = (bf16[256,1024]{1,0:T(8,128)(2,1)S(1)}, bf16[256,1024]{1,0:T(8,128)(2,1)S(1)}, u32[]{:S(2)}, u32[]{:S(2)}) collective-permute-start(bf16[256,1024]{1,0:T(8,128)(2,1)S(1)} %get-tuple-element.20), channel_id=1, source_target_pairs={{0,2},{1,3},{2,4},{3,5},{4,6},{5,7},{6,0},{7,1},{8,10},{9,11},{10,... | collective-permute-start | bytes 1572872 | tf_op jit(solution)/shard_map/ppermute | solution.py:120
  253.1 9.2 %collective-permute-start.4 = (bf16[128,1024]{1,0:T(8,128)(2,1)}, bf16[128,1024]{1,0:T(8,128)(2,1)}, u32[]{:S(2)}, u32[]{:S(2)}) collective-permute-start(bf16[128,1024]{1,0:T(8,128)(2,1)} %slice.66), channel_id=1, source_target_pairs={{0,6},{1,7},{2,0},{3,1},{4,2},{5,3},{6,4},{7,5},{8,14},{9,15},{10,... | collective-permute-start | bytes 786440 | tf_op jit(solution)/shard_map/ppermute | solution.py:123
  253.1 9.2 %collective-permute-start.3 = (bf16[128,1024]{1,0:T(8,128)(2,1)S(1)}, bf16[128,1024]{1,0:T(8,128)(2,1)S(1)}, u32[]{:S(2)}, u32[]{:S(2)}) collective-permute-start(bf16[128,1024]{1,0:T(8,128)(2,1)S(1)} %slice.65), channel_id=1, source_target_pairs={{0,2},{1,3},{2,4},{3,5},{4,6},{5,7},{6,0},{7,1},{8,10},{9,11},{10,... | collective-permute-start | bytes 786440 | tf_op jit(solution)/shard_map/ppermute | solution.py:122
  264.1 8.3 %copy-start.4 = (bf16[32,32,896]{2,1,0:T(8,128)(2,1)S(1)}, bf16[32,32,896]{2,1,0:T(8,128)(2,1)}, u32[]{:S(2)}) copy-start(bf16[32,32,896]{2,1,0:T(8,128)(2,1)} %get-tuple-element.15) | copy-start | bytes 5505028
  324.0 124.0 %all-to-all-start.3 = ((bf16[32,32,896]{2,1,0:T(8,128)(2,1)}), bf16[32,32,896]{2,1,0:T(8,128)(2,1)}, u32[]{:S(2)}, u32[]{:S(2)}) async-start(bf16[32,32,896]{2,1,0:T(8,128)(2,1)} %get-tuple-element.16), calls=%async_computation.3 | async-start | bytes 3670016 | tf_op jit(solution)/shard_map/all_to_all | solution.py:164
  329.7 2.2 copy-start.3
  397.6 17.5 %collective-permute-start.5 = (bf16[128,1024]{1,0:T(8,128)(2,1)S(1)}, bf16[128,1024]{1,0:T(8,128)(2,1)S(1)}, u32[]{:S(2)}, u32[]{:S(2)}) collective-permute-start(bf16[128,1024]{1,0:T(8,128)(2,1)S(1)} %fusion), channel_id=1, source_target_pairs={{0,1},{1,0},{2,3},{3,2},{4,5},{5,4},{6,7},{7,6},{8,9},{9,8},{10,11... | collective-permute-start | bytes 786440 | tf_op jit(solution)/shard_map/ppermute | solution.py:118
  417.7 24.6 %copy-start.5 = (bf16[32,32,896]{2,1,0:T(8,128)(2,1)S(1)}, bf16[32,32,896]{2,1,0:T(8,128)(2,1)}, u32[]{:S(2)}) copy-start(bf16[32,32,896]{2,1,0:T(8,128)(2,1)} %all_to_all.21) | copy-start | bytes 5505028
  417.7 15.1 %collective-permute-start.7 = (bf16[256,1024]{1,0:T(8,128)(2,1)S(1)}, bf16[256,1024]{1,0:T(8,128)(2,1)S(1)}, u32[]{:S(2)}, u32[]{:S(2)}) collective-permute-start(bf16[256,1024]{1,0:T(8,128)(2,1)S(1)} %get-tuple-element.18), channel_id=1, source_target_pairs={{0,6},{1,7},{2,0},{3,1},{4,2},{5,3},{6,4},{7,5},{8,14},{9,15},{10,... | collective-permute-start | bytes 1572872 | tf_op jit(solution)/shard_map/ppermute | solution.py:121
  418.2 14.6 %collective-permute-start.6 = (bf16[256,1024]{1,0:T(8,128)(2,1)S(1)}, bf16[256,1024]{1,0:T(8,128)(2,1)S(1)}, u32[]{:S(2)}, u32[]{:S(2)}) collective-permute-start(bf16[256,1024]{1,0:T(8,128)(2,1)S(1)} %get-tuple-element.18), channel_id=1, source_target_pairs={{0,2},{1,3},{2,4},{3,5},{4,6},{5,7},{6,0},{7,1},{8,10},{9,11},{10,... | collective-permute-start | bytes 1572872 | tf_op jit(solution)/shard_map/ppermute | solution.py:120
  432.7 8.7 %collective-permute-start.9 = (bf16[128,1024]{1,0:T(8,128)(2,1)S(1)}, bf16[128,1024]{1,0:T(8,128)(2,1)S(1)}, u32[]{:S(2)}, u32[]{:S(2)}) collective-permute-start(bf16[128,1024]{1,0:T(8,128)(2,1)S(1)} %slice.72), channel_id=1, source_target_pairs={{0,6},{1,7},{2,0},{3,1},{4,2},{5,3},{6,4},{7,5},{8,14},{9,15},{10,... | collective-permute-start | bytes 786440 | tf_op jit(solution)/shard_map/ppermute | solution.py:123
  432.9 8.5 %collective-permute-start.8 = (bf16[128,1024]{1,0:T(8,128)(2,1)S(1)}, bf16[128,1024]{1,0:T(8,128)(2,1)S(1)}, u32[]{:S(2)}, u32[]{:S(2)}) collective-permute-start(bf16[128,1024]{1,0:T(8,128)(2,1)S(1)} %slice.71), channel_id=1, source_target_pairs={{0,2},{1,3},{2,4},{3,5},{4,6},{5,7},{6,0},{7,1},{8,10},{9,11},{10,... | collective-permute-start | bytes 786440 | tf_op jit(solution)/shard_map/ppermute | solution.py:122
  448.0 7.0 %copy-start.1 = (bf16[1024,896]{1,0:T(8,128)(2,1)S(1)}, bf16[1024,896]{1,0:T(8,128)(2,1)}, u32[]{:S(2)}) copy-start(bf16[1024,896]{1,0:T(8,128)(2,1)} %param.6) | copy-start | bytes 5505028
where the time goes:
time: 462 us; the launch traced here: 455 us
  Pallas kernels  153 us (33%)
  blocking collectives  143 us (31%)
  waiting for transfers between devices  50.5 us (11%)
  local copies, waits for them, and re-layouts  48.3 us (10%)
  starting transfers between devices  27.6 us (6%)
  matrix products  27.3 us (6%)
  other arithmetic  5.09 us (1%)
    pallas_call x2, Pallas kernels, group_reduce_scatter(): pl.pallas_call(_rs_kernel, out_shape=jax.ShapeDtypeStruct((r // size, c),...  153 us
    all_to_all x1, blocking collectives, on_device(): lax.all_to_all(piece, 'dp', 0, 0, tiled=True).reshape(-1, width_here)  91.8 us
    all_to_all x1, blocking collectives, on_device(): weight_out = lax.all_to_all(piece, 'dp', 0, 0, tiled=True)  51.5 us
    ppermute x2, waiting for transfers between devices, group_all_gather(): partner = lax.ppermute(h, 'group', _z_flip(size))  27.8 us
    gather x2, local copies, waits for them, and re-layouts, on_device(): jnp.take(proj_in, expert_list, axis=0, mode='clip').transpose(0, 1, 3, 2, 4)  24.2 us
    ppermute x2, waiting for transfers between devices, group_all_gather(): from_up = lax.ppermute(pair, 'group', _y_shift(size, -1))  19.3 us
    dot_general x2, matrix products, on_device(): jnp.dot(weight_in, tokens.T, preferred_element_type=jnp.float32)  14.6 us
    dot_general x2, matrix products, on_device(): lax.dot_general(hiddens[slot], weights_out[slot], (((0,), (0,)), ((), ())...  12.7 us
  transfers between devices with their start and end apart: 12, of which 5 were waited for; matrix products, arithmetic and copies ran while one was open for 6% of the time, Pallas kernels for 34%

commit v1 on v0

--- a/solution.py
+++ b/solution.py
@@ -141,14 +141,13 @@
     block_mask = jnp.repeat(own_pattern, block_rows, axis=1).astype(jnp.float32)
     token_scale = route_weight.T * block_mask
 
-    send_in = jnp.take(proj_in, expert_list, axis=0, mode="clip").transpose(0, 1, 3, 2, 4)
     send_out = jnp.take(proj_out, expert_list, axis=0, mode="clip")
 
     hiddens = []
-    weights_out = []
     pending = tokens
     for slot in range(slots):
-        pending, piece = lax.optimization_barrier((pending, send_in[:, slot]))
+        piece = jnp.take(proj_in, expert_list[:, slot], axis=0, mode="clip").transpose(0, 2, 1, 3)
+        pending, piece = lax.optimization_barrier((pending, piece))
         weight_in = lax.all_to_all(piece, "dp", 0, 0, tiled=True).reshape(-1, width_here)
         if hiddens:
             weight_in, hiddens[-1] = lax.optimization_barrier((weight_in, hiddens[-1]))
@@ -159,16 +158,13 @@
         hidden = (token_scale[slot] * jax.nn.silu(shares[:, 0]) * shares[:, 1]).astype(jnp.bfloat16)
         hiddens.append(group_all_gather(hidden.reshape(-1, row_count)))
         pending = partial_here
-    for slot in range(slots):
-        pending, piece = lax.optimization_barrier((pending, send_out[:, slot]))
-        weight_out = lax.all_to_all(piece, "dp", 0, 0, tiled=True)
-        weights_out.append(weight_out.reshape(-1, width_here))
-        pending = weight_out
+    pending, send_out = lax.optimization_barrier((pending, send_out))
+    weights_out = lax.all_to_all(send_out, "dp", 0, 0, tiled=True)
 
     combined = None
     for slot in range(slots):
         term = lax.dot_general(
-            hiddens[slot], weights_out[slot], (((0,), (0,)), ((), ())),
+            hiddens[slot], weights_out[:, slot].reshape(-1, width_here), (((0,), (0,)), ((), ())),
             preferred_element_type=jnp.float32,
         )
         combined = term if combined is None else combined + term

time: 462 us -> 411 us (0.89); the launches traced: 455 us -> 411 us
  blocking collectives: 143 us -> 0 us
  waiting for transfers between devices: 50.5 us -> 125 us
  Pallas kernels: 153 us -> 171 us
  starting transfers between devices: 27.6 us -> 39.1 us
  matrix products: 27.3 us -> 22 us
    all_to_all x2 -> x0, blocking collectives: 143 us -> none  [the longest x1 91.8 us: on_device(): lax.all_to_all(piece, 'dp', 0, 0, tiled=True).reshape(-1, width_here)]
    all_to_all x1 -> x2, waiting for transfers between devices: 0.01 us -> 70.8 us  [on_device(): lax.all_to_all(piece, 'dp', 0, 0, tiled=True).reshape(-1, width_here)]
    ppermute x2, waiting for transfers between devices: 0.01 us -> 23.1 us  [group_all_gather(): from_down = lax.ppermute(pair, 'group', _y_shift(size, 1))]
    ppermute x2, waiting for transfers between devices: 19.3 us -> 0.01 us  [group_all_gather(): from_up = lax.ppermute(pair, 'group', _y_shift(size, -1))]
    pallas_call x2, Pallas kernels: 153 us -> 171 us  [group_reduce_scatter(): pl.pallas_call(_rs_kernel, out_shape=jax.ShapeDtypeStruct((r // size, c),...]
    all_to_all x1 -> x2, starting transfers between devices: 5.01 us -> 15.2 us  [on_device(): lax.all_to_all(piece, 'dp', 0, 0, tiled=True).reshape(-1, width_here)]
    squeeze x2 -> x0, local copies, waits for them, and re-layouts: 6.77 us -> none  [the longest x1 4.19 us: on_device(): pending, piece = lax.optimization_barrier((pending, send_out[:, slot]))]
    all_to_all x0 -> x2, local copies, waits for them, and re-layouts: none -> 5.44 us  [on_device(): lax.all_to_all(piece, 'dp', 0, 0, tiled=True).reshape(-1, width_here)]
  transfers between devices with their start and end apart: 12 -> 13, of which waited for: 5 -> 8; matrix products, arithmetic and copies ran while one was open for 6% -> 7% of each run, Pallas kernels for 34% -> 42%
where the time goes in v1:
time: 411 us
  Pallas kernels  171 us (42%)
  waiting for transfers between devices  125 us (30%)
  local copies, waits for them, and re-layouts  48.6 us (12%)
  starting transfers between devices  39.1 us (10%)
  matrix products  22 us (5%)
  other arithmetic  5.1 us (1%)
    pallas_call x2, Pallas kernels, group_reduce_scatter(): pl.pallas_call(_rs_kernel, out_shape=jax.ShapeDtypeStruct((r // size, c),...  171 us
    all_to_all x2, waiting for transfers between devices, on_device(): lax.all_to_all(piece, 'dp', 0, 0, tiled=True).reshape(-1, width_here)  70.8 us
    gather x2, local copies, waits for them, and re-layouts, on_device(): jnp.take(proj_in, expert_list[:, slot], axis=0, mode='clip')  23.5 us
    ppermute x2, waiting for transfers between devices, group_all_gather(): partner = lax.ppermute(h, 'group', _z_flip(size))  23.1 us
    ppermute x2, waiting for transfers between devices, group_all_gather(): from_down = lax.ppermute(pair, 'group', _y_shift(size, 1))  23.1 us
    all_to_all x2, starting transfers between devices, on_device(): lax.all_to_all(piece, 'dp', 0, 0, tiled=True).reshape(-1, width_here)  15.2 us
    dot_general x2, matrix products, on_device(): jnp.dot(weight_in, tokens.T, preferred_element_type=jnp.float32)  12.5 us
    dot_general x2, matrix products, on_device(): lax.dot_general(hiddens[slot], weights_out[:, slot].reshape(-1, width_her...  9.45 us
  transfers between devices with their start and end apart: 13, of which 8 were waited for; matrix products, arithmetic and copies ran while one was open for 7% of the time, Pallas kernels for 42%

profile of v1, /device:TPU:24, one launch (start us, length us, event | category | flops | bytes accessed | tf_op | source)
XLA Modules:
  0.0 410.9 jit_solution(7082124845997792603)
XLA Ops:
  0.0 0.8 slice_bitcast_fusion
  0.8 11.8 %gather_fusion = bf16[32,32,2,896]{3,2,1,0:T(2,128)(2,1)} fusion(bf16[32,32,2,896]{3,2,1,0:T(2,128)(2,1)} %param.7, s32[1024]{0:T(1024)S(1)} %get-tuple-element.30), kind=kCustom, calls=%fused_computation | custom fusion | bytes 7340160 | tf_op jit(solution)/shard_map/jit(_take)/gather | solution.py:149
  12.6 8.9 %all-to-all-start = ((bf16[32,2,32,896]{3,1,2,0:T(2,128)(2,1)}), bf16[32,2,32,896]{3,1,2,0:T(2,128)(2,1)}, u32[]{:S(2)}, u32[]{:S(2)}) async-start(bf16[32,2,32,896]{3,1,2,0:T(2,128)(2,1)} %bitcast.71), calls=%async_computation | async-start | bytes 7340032 | tf_op jit(solution)/shard_map/all_to_all | solution.py:151
  21.5 11.7 %gather_fusion.1 = bf16[32,32,2,896]{3,2,1,0:T(2,128)(2,1)} fusion(bf16[32,32,2,896]{3,2,1,0:T(2,128)(2,1)} %param.7, s32[1024]{0:T(1024)S(1)} %get-tuple-element.29), kind=kCustom, calls=%fused_computation.1 | custom fusion | bytes 7340160 | tf_op jit(solution)/shard_map/jit(_take)/gather | solution.py:149
  33.2 70.8 %all-to-all-done = bf16[32,2,32,896]{3,1,2,0:T(2,128)(2,1)} async-done(((bf16[32,2,32,896]{3,1,2,0:T(2,128)(2,1)}), bf16[32,2,32,896]{3,1,2,0:T(2,128)(2,1)}, u32[]{:S(2)}, u32[]{:S(2)}) %all-to-all-start) | async-done | bytes 3670048 | tf_op jit(solution)/shard_map/all_to_all | solution.py:151
  104.0 2.7 copy.9
  106.7 6.3 %convolution_convert_fusion.1.x_ref = bf16[2048,1024]{1,0:T(8,128)(2,1)} fusion(bf16[2048,896]{1,0:T(8,128)(2,1)S(1)} %bitcast.72, bf16[1024,896]{1,0:T(8,128)(2,1)S(1)} %copy-done), kind=kOutput, calls=%fused_computation.4 | convolution fusion | flops 3760193536 | bytes 9699328 | tf_op jit(solution)/shard_map/dot_general | solution.py:154
  113.0 6.3 %all-to-all-start.1 = ((bf16[32,2,32,896]{3,1,2,0:T(2,128)(2,1)}), bf16[32,2,32,896]{3,1,2,0:T(2,128)(2,1)}, u32[]{:S(2)}, u32[]{:S(2)}) async-start(bf16[32,2,32,896]{3,1,2,0:T(2,128)(2,1)} %bitcast.70), calls=%async_computation.1 | async-start | bytes 7340032 | tf_op jit(solution)/shard_map/all_to_all | solution.py:151
  119.7 2.2 copy-done.2
  121.9 86.5 %shard_map.64 = f32[256,1024]{1,0:T(8,128)S(1)} custom-call(bf16[2048,1024]{1,0:T(8,128)(2,1)S(1)} %copy-done.2), custom_call_target="tpu_custom_call" | custom-call | tf_op jit(solution)/shard_map/pallas_call | solution.py:93
  208.5 0.2 fusion.5
  208.7 1.5 collective-permute-start
  210.2 12.2 %collective-permute-done = bf16[128,1024]{1,0:T(8,128)(2,1)S(1)} collective-permute-done((bf16[128,1024]{1,0:T(8,128)(2,1)S(1)}, bf16[128,1024]{1,0:T(8,128)(2,1)S(1)}, u32[]{:S(2)}, u32[]{:S(2)}) %collective-permute-start) | collective-permute-done | bytes 262176 | tf_op jit(solution)/shard_map/ppermute | solution.py:118
  222.4 1.6 broadcast.19.clone
  224.0 1.0 constant_dynamic-update-slice_fusion.5
  225.0 0.3 collective-permute-start.1
  225.3 1.7 collective-permute-start.2
  227.2 11.5 %collective-permute-done.1 = bf16[256,1024]{1,0:T(8,128)(2,1)S(1)} collective-permute-done((bf16[256,1024]{1,0:T(8,128)(2,1)S(1)}, bf16[256,1024]{1,0:T(8,128)(2,1)S(1)}, u32[]{:S(2)}, u32[]{:S(2)}) %collective-permute-start.1) | collective-permute-done | bytes 524320 | tf_op jit(solution)/shard_map/ppermute | solution.py:120
  238.7 0.7 slice.65
  239.4 1.5 collective-permute-start.3
  241.0 0.6 collective-permute-start.4
  241.6 4.3 %gather_fusion.2 = bf16[64,32,896]{2,1,0:T(8,128)(2,1)} fusion(bf16[32,32,896]{2,1,0:T(8,128)(2,1)} %param.8, s32[1024]{0:T(1024)S(1)} %pad_clamp_fusion), kind=kCustom, calls=%fused_computation.2 | custom fusion | bytes 7340288 | tf_op jit(solution)/shard_map/jit(_take)/gather | solution.py:144
  245.9 0.8 constant_dynamic-update-slice_fusion.4
  246.7 0.8 constant_dynamic-update-slice_fusion.3
  247.6 1.7 collective-permute-done.4
  249.3 1.8 maximum_dynamic-update-slice_fusion
  251.1 2.7 copy.10
  253.8 6.2 %convolution_convert_fusion.x_ref = bf16[2048,1024]{1,0:T(8,128)(2,1)} fusion(bf16[2048,896]{1,0:T(8,128)(2,1)S(1)} %bitcast.73, bf16[1024,896]{1,0:T(8,128)(2,1)S(1)} %copy-done), kind=kOutput, calls=%fused_computation.3 | convolution fusion | flops 3760193536 | bytes 9699328 | tf_op jit(solution)/shard_map/dot_general | solution.py:154
  260.0 8.7 %all-to-all-start.2 = ((bf16[32,2,32,896]{3,2,1,0:T(8,128)(2,1)}), bf16[32,2,32,896]{3,2,1,0:T(8,128)(2,1)}, u32[]{:S(2)}, u32[]{:S(2)}) async-start(bf16[32,2,32,896]{3,2,1,0:T(8,128)(2,1)} %bitcast.69), calls=%async_computation.2 | async-start | bytes 7340032 | tf_op jit(solution)/shard_map/all_to_all | solution.py:162
  268.7 2.2 copy-done.3
  270.9 84.2 %shard_map.65 = f32[256,1024]{1,0:T(8,128)S(1)} custom-call(bf16[2048,1024]{1,0:T(8,128)(2,1)S(1)} %copy-done.3), custom_call_target="tpu_custom_call" | custom-call | tf_op jit(solution)/shard_map/pallas_call | solution.py:93
  355.3 0.2 fusion
  355.4 4.5 %collective-permute-start.5 = (bf16[128,1024]{1,0:T(8,128)(2,1)S(1)}, bf16[128,1024]{1,0:T(8,128)(2,1)S(1)}, u32[]{:S(2)}, u32[]{:S(2)}) collective-permute-start(bf16[128,1024]{1,0:T(8,128)(2,1)S(1)} %fusion), channel_id=1, source_target_pairs={{0,1},{1,0},{2,3},{3,2},{4,5},{5,4},{6,7},{7,6},{8,9},{9,8},{10,11... | collective-permute-start | bytes 786440 | tf_op jit(solution)/shard_map/ppermute | solution.py:118
  359.9 11.0 %collective-permute-done.5 = bf16[128,1024]{1,0:T(8,128)(2,1)S(1)} collective-permute-done((bf16[128,1024]{1,0:T(8,128)(2,1)S(1)}, bf16[128,1024]{1,0:T(8,128)(2,1)S(1)}, u32[]{:S(2)}, u32[]{:S(2)}) %collective-permute-start.5) | collective-permute-done | bytes 262176 | tf_op jit(solution)/shard_map/ppermute | solution.py:118
  370.9 1.6 broadcast.19
  372.4 1.0 constant_dynamic-update-slice_fusion.2
  373.4 1.6 collective-permute-start.6
  375.1 0.4 collective-permute-start.7
  375.4 11.6 %collective-permute-done.6 = bf16[256,1024]{1,0:T(8,128)(2,1)S(1)} collective-permute-done((bf16[256,1024]{1,0:T(8,128)(2,1)S(1)}, bf16[256,1024]{1,0:T(8,128)(2,1)S(1)}, u32[]{:S(2)}, u32[]{:S(2)}) %collective-permute-start.6) | collective-permute-done | bytes 524320 | tf_op jit(solution)/shard_map/ppermute | solution.py:120
  387.1 2.9 collective-permute-start.8
  390.1 0.8 constant_dynamic-update-slice_fusion.1
  391.0 0.8 constant_dynamic-update-slice_fusion
  391.8 2.9 collective-permute-done.8
  394.7 3.5 collective-permute-done.9
  398.2 0.8 maximum_dynamic-update-slice_fusion.1
  399.0 2.4 fusion.10
  401.4 4.0 fusion.14
  405.4 5.5 %add_convert_fusion = bf16[1024,896]{1,0:T(8,128)(2,1)} fusion(f32[1024,896]{1,0:T(8,128)S(1)} %fusion.14, bf16[1024,1024]{1,0:T(8,128)(2,1)} %maximum_dynamic-update-slice_fusion.1, bf16[1024,896]{1,0:T(8,128)(2,1)S(1)} %bitcast.74), kind=kOutput, calls=%fused_computation.5 | convolution fusion | flops 1880883200 | bytes 9437184 | tf_op jit(solution)/shard_map/dot_general | solution.py:166
  (31 shorter events, 0.8 us)
Async XLA Ops:
  0.0 106.7 %copy-start = (bf16[1024,896]{1,0:T(8,128)(2,1)S(1)}, bf16[1024,896]{1,0:T(8,128)(2,1)}, u32[]{:S(2)}) copy-start(bf16[1024,896]{1,0:T(8,128)(2,1)} %param.6) | copy-start | bytes 5505028
  12.6 91.4 %all-to-all-start = ((bf16[32,2,32,896]{3,1,2,0:T(2,128)(2,1)}), bf16[32,2,32,896]{3,1,2,0:T(2,128)(2,1)}, u32[]{:S(2)}, u32[]{:S(2)}) async-start(bf16[32,2,32,896]{3,1,2,0:T(2,128)(2,1)} %bitcast.71), calls=%async_computation | async-start | bytes 7340032 | tf_op jit(solution)/shard_map/all_to_all | solution.py:151
  113.0 6.4 %copy-start.5 = (s32[32,2,8]{0,2,1:T(8,128)S(1)}, s32[32,2,8]{0,2,1:T(8,128)}, u32[]{:S(2)}) copy-start(s32[32,2,8]{0,2,1:T(8,128)} %param.10) | copy-start | bytes 6148
  113.0 6.6 %copy-start.4 = (f32[1024,2]{0,1:T(2,128)S(1)}, f32[1024,2]{0,1:T(2,128)}, u32[]{:S(2)}) copy-start(f32[1024,2]{0,1:T(2,128)} %param.11) | copy-start | bytes 24580
  113.0 138.0 %all-to-all-start.1 = ((bf16[32,2,32,896]{3,1,2,0:T(2,128)(2,1)}), bf16[32,2,32,896]{3,1,2,0:T(2,128)(2,1)}, u32[]{:S(2)}, u32[]{:S(2)}) async-start(bf16[32,2,32,896]{3,1,2,0:T(2,128)(2,1)} %bitcast.70), calls=%async_computation.1 | async-start | bytes 7340032 | tf_op jit(solution)/shard_map/all_to_all | solution.py:151
  119.7 2.2 copy-start.2
  208.7 18.4 %copy-start.6 = (s32[32,2]{0,1:T(2,128)S(1)}, s32[32,2]{0,1:T(2,128)}, u32[]{:S(2)}) copy-start(s32[32,2]{0,1:T(2,128)} %param.9) | copy-start | bytes 772
  208.7 13.7 %collective-permute-start = (bf16[128,1024]{1,0:T(8,128)(2,1)S(1)}, bf16[128,1024]{1,0:T(8,128)(2,1)S(1)}, u32[]{:S(2)}, u32[]{:S(2)}) collective-permute-start(bf16[128,1024]{1,0:T(8,128)(2,1)S(1)} %fusion.5), channel_id=1, source_target_pairs={{0,1},{1,0},{2,3},{3,2},{4,5},{5,4},{6,7},{7,6},{8,9},{9,8},{10,11... | collective-permute-start | bytes 786440 | tf_op jit(solution)/shard_map/ppermute | solution.py:118
  225.0 13.7 %collective-permute-start.1 = (bf16[256,1024]{1,0:T(8,128)(2,1)S(1)}, bf16[256,1024]{1,0:T(8,128)(2,1)S(1)}, u32[]{:S(2)}, u32[]{:S(2)}) collective-permute-start(bf16[256,1024]{1,0:T(8,128)(2,1)S(1)} %get-tuple-element.18), channel_id=1, source_target_pairs={{0,2},{1,3},{2,4},{3,5},{4,6},{5,7},{6,0},{7,1},{8,10},{9,11},{10,... | collective-permute-start | bytes 1572872 | tf_op jit(solution)/shard_map/ppermute | solution.py:120
  225.3 15.7 %collective-permute-start.2 = (bf16[256,1024]{1,0:T(8,128)(2,1)S(1)}, bf16[256,1024]{1,0:T(8,128)(2,1)S(1)}, u32[]{:S(2)}, u32[]{:S(2)}) collective-permute-start(bf16[256,1024]{1,0:T(8,128)(2,1)S(1)} %get-tuple-element.18), channel_id=1, source_target_pairs={{0,6},{1,7},{2,0},{3,1},{4,2},{5,3},{6,4},{7,5},{8,14},{9,15},{10,... | collective-permute-start | bytes 1572872 | tf_op jit(solution)/shard_map/ppermute | solution.py:121
  239.4 8.1 %collective-permute-start.3 = (bf16[128,1024]{1,0:T(8,128)(2,1)}, bf16[128,1024]{1,0:T(8,128)(2,1)}, u32[]{:S(2)}, u32[]{:S(2)}) collective-permute-start(bf16[128,1024]{1,0:T(8,128)(2,1)} %slice.65), channel_id=1, source_target_pairs={{0,2},{1,3},{2,4},{3,5},{4,6},{5,7},{6,0},{7,1},{8,10},{9,11},{10,... | collective-permute-start | bytes 786440 | tf_op jit(solution)/shard_map/ppermute | solution.py:122
  241.0 8.2 %collective-permute-start.4 = (bf16[128,1024]{1,0:T(8,128)(2,1)S(1)}, bf16[128,1024]{1,0:T(8,128)(2,1)S(1)}, u32[]{:S(2)}, u32[]{:S(2)}) collective-permute-start(bf16[128,1024]{1,0:T(8,128)(2,1)S(1)} %slice.66), channel_id=1, source_target_pairs={{0,6},{1,7},{2,0},{3,1},{4,2},{5,3},{6,4},{7,5},{8,14},{9,15},{10,... | collective-permute-start | bytes 786440 | tf_op jit(solution)/shard_map/ppermute | solution.py:123
  260.0 139.0 %all-to-all-start.2 = ((bf16[32,2,32,896]{3,2,1,0:T(8,128)(2,1)}), bf16[32,2,32,896]{3,2,1,0:T(8,128)(2,1)}, u32[]{:S(2)}, u32[]{:S(2)}) async-start(bf16[32,2,32,896]{3,2,1,0:T(8,128)(2,1)} %bitcast.69), calls=%async_computation.2 | async-start | bytes 7340032 | tf_op jit(solution)/shard_map/all_to_all | solution.py:162
  268.7 2.2 copy-start.3
  355.4 15.4 %collective-permute-start.5 = (bf16[128,1024]{1,0:T(8,128)(2,1)S(1)}, bf16[128,1024]{1,0:T(8,128)(2,1)S(1)}, u32[]{:S(2)}, u32[]{:S(2)}) collective-permute-start(bf16[128,1024]{1,0:T(8,128)(2,1)S(1)} %fusion), channel_id=1, source_target_pairs={{0,1},{1,0},{2,3},{3,2},{4,5},{5,4},{6,7},{7,6},{8,9},{9,8},{10,11... | collective-permute-start | bytes 786440 | tf_op jit(solution)/shard_map/ppermute | solution.py:118
  373.4 13.6 %collective-permute-start.6 = (bf16[256,1024]{1,0:T(8,128)(2,1)S(1)}, bf16[256,1024]{1,0:T(8,128)(2,1)S(1)}, u32[]{:S(2)}, u32[]{:S(2)}) collective-permute-start(bf16[256,1024]{1,0:T(8,128)(2,1)S(1)} %get-tuple-element.16), channel_id=1, source_target_pairs={{0,2},{1,3},{2,4},{3,5},{4,6},{5,7},{6,0},{7,1},{8,10},{9,11},{10,... | collective-permute-start | bytes 1572872 | tf_op jit(solution)/shard_map/ppermute | solution.py:120
  375.1 14.9 %collective-permute-start.7 = (bf16[256,1024]{1,0:T(8,128)(2,1)S(1)}, bf16[256,1024]{1,0:T(8,128)(2,1)S(1)}, u32[]{:S(2)}, u32[]{:S(2)}) collective-permute-start(bf16[256,1024]{1,0:T(8,128)(2,1)S(1)} %get-tuple-element.16), channel_id=1, source_target_pairs={{0,6},{1,7},{2,0},{3,1},{4,2},{5,3},{6,4},{7,5},{8,14},{9,15},{10,... | collective-permute-start | bytes 1572872 | tf_op jit(solution)/shard_map/ppermute | solution.py:121
  387.1 7.6 %collective-permute-start.8 = (bf16[128,1024]{1,0:T(8,128)(2,1)S(1)}, bf16[128,1024]{1,0:T(8,128)(2,1)S(1)}, u32[]{:S(2)}, u32[]{:S(2)}) collective-permute-start(bf16[128,1024]{1,0:T(8,128)(2,1)S(1)} %slice.71), channel_id=1, source_target_pairs={{0,2},{1,3},{2,4},{3,5},{4,6},{5,7},{6,0},{7,1},{8,10},{9,11},{10,... | collective-permute-start | bytes 786440 | tf_op jit(solution)/shard_map/ppermute | solution.py:122
  390.0 8.1 %collective-permute-start.9 = (bf16[128,1024]{1,0:T(8,128)(2,1)S(1)}, bf16[128,1024]{1,0:T(8,128)(2,1)S(1)}, u32[]{:S(2)}, u32[]{:S(2)}) collective-permute-start(bf16[128,1024]{1,0:T(8,128)(2,1)S(1)} %slice.72), channel_id=1, source_target_pairs={{0,6},{1,7},{2,0},{3,1},{4,2},{5,3},{6,4},{7,5},{8,14},{9,15},{10,... | collective-permute-start | bytes 786440 | tf_op jit(solution)/shard_map/ppermute | solution.py:123
  405.4 5.5 %copy-start.1 = (bf16[1024,896]{1,0:T(8,128)(2,1)S(1)}, bf16[1024,896]{1,0:T(8,128)(2,1)}, u32[]{:S(2)}) copy-start(bf16[1024,896]{1,0:T(8,128)(2,1)} %param.6) | copy-start | bytes 5505028

commit v2 on v1

--- a/solution.py
+++ b/solution.py
@@ -22,65 +22,67 @@
     return _perm(size, lambda j: j ^ 1)
 
 
-def _rs_kernel(x_ref, out_ref, ybuf, own, zsend, zrecv, send_sem, recv_sem, local_sem):
+def _rs_kernel(x_ref, out_ref, ybuf, fwd, relay, own, zsend, zrecv, send_sem, recv_sem, local_sem):
     size = lax.axis_size("group")
     z_parts = size // Y_PARTS
     j = lax.axis_index("group")
     y, zh = j // z_parts, j % z_parts
     rows = x_ref.shape[0] // Y_PARTS
     half = rows // 2
+    mesh_id = pl.DeviceIdType.MESH
 
     def peer(dy):
-        return ((y + dy) % Y_PARTS) * z_parts + zh
+        return {"group": ((y + dy) % Y_PARTS) * z_parts + zh}
 
-    partner = y * z_parts + (1 - zh)
-    shifts = (1, Y_PARTS - 1, 2)
+    def block_at(dy):
+        return pl.multiple_of(((y + dy) % Y_PARTS) * rows, rows)
+
+    partner = {"group": y * z_parts + (1 - zh)}
+    up, down = peer(1), peer(Y_PARTS - 1)
     barrier = pltpu.get_barrier_semaphore()
-    for dy in shifts:
-        pl.semaphore_signal(barrier, inc=1, device_id={"group": peer(dy)},
-                            device_id_type=pl.DeviceIdType.MESH)
-    pl.semaphore_signal(barrier, inc=1, device_id={"group": partner},
-                        device_id_type=pl.DeviceIdType.MESH)
-    pl.semaphore_wait(barrier, len(shifts) + 1)
+    for dev in (up, down, partner):
+        pl.semaphore_signal(barrier, inc=1, device_id=dev, device_id_type=mesh_id)
+    pl.semaphore_wait(barrier, 3)
 
-    copies = []
-    for k, dy in enumerate(shifts):
-        start = pl.multiple_of(((y + dy) % Y_PARTS) * rows, rows)
+    def remote(src, dst, k, dev):
         c = pltpu.make_async_remote_copy(
-            src_ref=x_ref.at[pl.ds(start, rows)],
-            dst_ref=ybuf.at[k],
-            send_sem=send_sem.at[k],
-            recv_sem=recv_sem.at[k],
-            device_id={"group": peer(dy)},
-            device_id_type=pl.DeviceIdType.MESH,
+            src_ref=src, dst_ref=dst, send_sem=send_sem.at[k], recv_sem=recv_sem.at[k],
+            device_id=dev, device_id_type=mesh_id,
         )
         c.start()
-        copies.append(c)
-    mine_start = pl.multiple_of(y * rows, rows)
-    local = pltpu.make_async_copy(x_ref.at[pl.ds(mine_start, rows)], own, local_sem.at[0])
+        return c
+
+    far = block_at(2)
+    first = [
+        remote(x_ref.at[pl.ds(block_at(1), rows)], ybuf.at[0], 0, up),
+        remote(x_ref.at[pl.ds(block_at(-1), rows)], ybuf.at[1], 1, down),
+        remote(x_ref.at[pl.ds(far, half)], fwd.at[0], 2, up),
+        remote(x_ref.at[pl.ds(far + half, half)], fwd.at[1], 3, down),
+    ]
+    local = pltpu.make_async_copy(x_ref.at[pl.ds(block_at(0), rows)], own, local_sem.at[0])
     local.start()
+    for c in first:
+        c.wait()
+    second = [
+        remote(fwd.at[0], relay.at[pl.ds(0, half)], 4, up),
+        remote(fwd.at[1], relay.at[pl.ds(half, half)], 5, down),
+    ]
     local.wait()
-    for c in copies:
-        c.wait()
 
     f32 = jnp.float32
 
-    def y_sum(lo):
+    def near_sum(lo):
         sl = pl.ds(lo, half)
-        total = own[sl, :].astype(f32)
-        for k in range(len(shifts)):
-            total = total + ybuf[k, sl, :].astype(f32)
-        return total
+        return own[sl, :].astype(f32) + ybuf[0, sl, :].astype(f32) + ybuf[1, sl, :].astype(f32)
 
     other_lo = pl.multiple_of((1 - zh) * half, half)
     mine_lo = pl.multiple_of(zh * half, half)
-    zsend[...] = y_sum(other_lo).astype(zsend.dtype)
-    zc = pltpu.make_async_remote_copy(
-        src_ref=zsend, dst_ref=zrecv, send_sem=send_sem.at[3], recv_sem=recv_sem.at[3],
-        device_id={"group": partner}, device_id_type=pl.DeviceIdType.MESH,
-    )
-    zc.start()
-    out_ref[...] = y_sum(mine_lo)
+    out_ref[...] = near_sum(other_lo)
+    for c in second:
+        c.wait()
+    zsend[...] = (out_ref[...] + relay[pl.ds(other_lo, half), :].astype(f32)).astype(zsend.dtype)
+    zc = remote(zsend, zrecv, 6, partner)
+    out_ref[...] = near_sum(mine_lo) + relay[pl.ds(mine_lo, half), :].astype(f32)
     zc.wait()
     out_ref[...] += zrecv[...].astype(f32)
 
@@ -96,12 +98,14 @@
         in_specs=[pl.BlockSpec(memory_space=pl.ANY)],
         out_specs=pl.BlockSpec(memory_space=pltpu.VMEM),
         scratch_shapes=[
-            pltpu.VMEM((3, rows, c), x.dtype),
+            pltpu.VMEM((2, rows, c), x.dtype),
+            pltpu.VMEM((2, half, c), x.dtype),
+            pltpu.VMEM((rows, c), x.dtype),
             pltpu.VMEM((rows, c), x.dtype),
             pltpu.VMEM((half, c), x.dtype),
             pltpu.VMEM((half, c), x.dtype),
-            pltpu.SemaphoreType.DMA((4,)),
-            pltpu.SemaphoreType.DMA((4,)),
+            pltpu.SemaphoreType.DMA((7,)),
+            pltpu.SemaphoreType.DMA((7,)),
             pltpu.SemaphoreType.DMA((1,)),
         ],
         compiler_params=pltpu.CompilerParams(

time: 411 us -> 410 us (level)
  no operation moved by 1% of the time
where the time goes in v2:
time: 410 us; the launch traced here: 409 us
  Pallas kernels  171 us (42%)
  waiting for transfers between devices  125 us (30%)
  local copies, waits for them, and re-layouts  48.6 us (12%)
  starting transfers between devices  36.6 us (9%)
  matrix products  22 us (5%)
  other arithmetic  5.1 us (1%)
    pallas_call x2, Pallas kernels, group_reduce_scatter(): pl.pallas_call(_rs_kernel, out_shape=jax.ShapeDtypeStruct((r // size, c),...  171 us
    all_to_all x2, waiting for transfers between devices, on_device(): lax.all_to_all(piece, 'dp', 0, 0, tiled=True).reshape(-1, width_here)  70.8 us
    gather x2, local copies, waits for them, and re-layouts, on_device(): jnp.take(proj_in, expert_list[:, slot], axis=0, mode='clip')  23.5 us
    ppermute x2, waiting for transfers between devices, group_all_gather(): partner = lax.ppermute(h, 'group', _z_flip(size))  23.2 us
    ppermute x2, waiting for transfers between devices, group_all_gather(): from_down = lax.ppermute(pair, 'group', _y_shift(size, 1))  23.1 us
    all_to_all x2, starting transfers between devices, on_device(): lax.all_to_all(piece, 'dp', 0, 0, tiled=True).reshape(-1, width_here)  15.2 us
    dot_general x2, matrix products, on_device(): jnp.dot(weight_in, tokens.T, preferred_element_type=jnp.float32)  12.5 us
    dot_general x2, matrix products, on_device(): lax.dot_general(hiddens[slot], weights_out[:, slot].reshape(-1, width_her...  9.44 us
  transfers between devices with their start and end apart: 13, of which 8 were waited for; matrix products, arithmetic and copies ran while one was open for 7% of the time, Pallas kernels for 42%

profile of v2, /device:TPU:24, one launch (start us, length us, event | category | flops | bytes accessed | tf_op | source)
XLA Modules:
  0.0 409.0 jit_solution(13660110598993561408)
XLA Ops:
  0.0 0.8 slice_bitcast_fusion
  0.8 11.8 %gather_fusion = bf16[32,32,2,896]{3,2,1,0:T(2,128)(2,1)} fusion(bf16[32,32,2,896]{3,2,1,0:T(2,128)(2,1)} %param.7, s32[1024]{0:T(1024)S(1)} %get-tuple-element.30), kind=kCustom, calls=%fused_computation | custom fusion | bytes 7340160 | tf_op jit(solution)/shard_map/jit(_take)/gather | solution.py:153
  12.6 8.9 %all-to-all-start = ((bf16[32,2,32,896]{3,1,2,0:T(2,128)(2,1)}), bf16[32,2,32,896]{3,1,2,0:T(2,128)(2,1)}, u32[]{:S(2)}, u32[]{:S(2)}) async-start(bf16[32,2,32,896]{3,1,2,0:T(2,128)(2,1)} %bitcast.71), calls=%async_computation | async-start | bytes 7340032 | tf_op jit(solution)/shard_map/all_to_all | solution.py:155
  21.5 11.7 %gather_fusion.1 = bf16[32,32,2,896]{3,2,1,0:T(2,128)(2,1)} fusion(bf16[32,32,2,896]{3,2,1,0:T(2,128)(2,1)} %param.7, s32[1024]{0:T(1024)S(1)} %get-tuple-element.29), kind=kCustom, calls=%fused_computation.1 | custom fusion | bytes 7340160 | tf_op jit(solution)/shard_map/jit(_take)/gather | solution.py:153
  33.2 70.8 %all-to-all-done = bf16[32,2,32,896]{3,1,2,0:T(2,128)(2,1)} async-done(((bf16[32,2,32,896]{3,1,2,0:T(2,128)(2,1)}), bf16[32,2,32,896]{3,1,2,0:T(2,128)(2,1)}, u32[]{:S(2)}, u32[]{:S(2)}) %all-to-all-start) | async-done | bytes 3670048 | tf_op jit(solution)/shard_map/all_to_all | solution.py:155
  104.0 2.7 copy.9
  106.7 6.3 %convolution_convert_fusion.1.x_ref = bf16[2048,1024]{1,0:T(8,128)(2,1)} fusion(bf16[2048,896]{1,0:T(8,128)(2,1)S(1)} %bitcast.72, bf16[1024,896]{1,0:T(8,128)(2,1)S(1)} %copy-done), kind=kOutput, calls=%fused_computation.4 | convolution fusion | flops 3760193536 | bytes 9699328 | tf_op jit(solution)/shard_map/dot_general | solution.py:158
  113.0 6.3 %all-to-all-start.1 = ((bf16[32,2,32,896]{3,1,2,0:T(2,128)(2,1)}), bf16[32,2,32,896]{3,1,2,0:T(2,128)(2,1)}, u32[]{:S(2)}, u32[]{:S(2)}) async-start(bf16[32,2,32,896]{3,1,2,0:T(2,128)(2,1)} %bitcast.70), calls=%async_computation.1 | async-start | bytes 7340032 | tf_op jit(solution)/shard_map/all_to_all | solution.py:155
  119.7 2.2 copy-done.2
  121.9 86.6 %shard_map.64 = f32[256,1024]{1,0:T(8,128)S(1)} custom-call(bf16[2048,1024]{1,0:T(8,128)(2,1)S(1)} %copy-done.2), custom_call_target="tpu_custom_call" | custom-call | tf_op jit(solution)/shard_map/pallas_call | solution.py:95
  208.6 0.2 fusion.5
  208.8 1.5 collective-permute-start
  210.3 12.1 %collective-permute-done = bf16[128,1024]{1,0:T(8,128)(2,1)S(1)} collective-permute-done((bf16[128,1024]{1,0:T(8,128)(2,1)S(1)}, bf16[128,1024]{1,0:T(8,128)(2,1)S(1)}, u32[]{:S(2)}, u32[]{:S(2)}) %collective-permute-start) | collective-permute-done | bytes 262176 | tf_op jit(solution)/shard_map/ppermute | solution.py:122
  222.4 1.6 broadcast.19.clone
  224.0 1.0 constant_dynamic-update-slice_fusion.5
  225.0 0.3 collective-permute-start.1
  225.3 1.7 collective-permute-start.2
  227.2 11.5 %collective-permute-done.1 = bf16[256,1024]{1,0:T(8,128)(2,1)S(1)} collective-permute-done((bf16[256,1024]{1,0:T(8,128)(2,1)S(1)}, bf16[256,1024]{1,0:T(8,128)(2,1)S(1)}, u32[]{:S(2)}, u32[]{:S(2)}) %collective-permute-start.1) | collective-permute-done | bytes 524320 | tf_op jit(solution)/shard_map/ppermute | solution.py:124
  238.7 0.7 slice.65
  239.4 1.5 collective-permute-start.3
  241.0 0.6 collective-permute-start.4
  241.6 4.3 %gather_fusion.2 = bf16[64,32,896]{2,1,0:T(8,128)(2,1)} fusion(bf16[32,32,896]{2,1,0:T(8,128)(2,1)} %param.8, s32[1024]{0:T(1024)S(1)} %pad_clamp_fusion), kind=kCustom, calls=%fused_computation.2 | custom fusion | bytes 7340288 | tf_op jit(solution)/shard_map/jit(_take)/gather | solution.py:148
  245.9 0.8 constant_dynamic-update-slice_fusion.4
  246.7 0.8 constant_dynamic-update-slice_fusion.3
  247.6 1.7 collective-permute-done.4
  249.2 1.8 maximum_dynamic-update-slice_fusion
  251.0 2.7 copy.10
  253.8 6.2 %convolution_convert_fusion.x_ref = bf16[2048,1024]{1,0:T(8,128)(2,1)} fusion(bf16[2048,896]{1,0:T(8,128)(2,1)S(1)} %bitcast.73, bf16[1024,896]{1,0:T(8,128)(2,1)S(1)} %copy-done), kind=kOutput, calls=%fused_computation.3 | convolution fusion | flops 3760193536 | bytes 9699328 | tf_op jit(solution)/shard_map/dot_general | solution.py:158
  260.0 6.8 %all-to-all-start.2 = ((bf16[32,2,32,896]{3,2,1,0:T(8,128)(2,1)}), bf16[32,2,32,896]{3,2,1,0:T(8,128)(2,1)}, u32[]{:S(2)}, u32[]{:S(2)}) async-start(bf16[32,2,32,896]{3,2,1,0:T(8,128)(2,1)} %bitcast.69), calls=%async_computation.2 | async-start | bytes 7340032 | tf_op jit(solution)/shard_map/all_to_all | solution.py:166
  266.8 2.2 copy-done.3
  269.0 84.7 %shard_map.65 = f32[256,1024]{1,0:T(8,128)S(1)} custom-call(bf16[2048,1024]{1,0:T(8,128)(2,1)S(1)} %copy-done.3), custom_call_target="tpu_custom_call" | custom-call | tf_op jit(solution)/shard_map/pallas_call | solution.py:95
  353.8 0.2 fusion
  353.9 4.1 collective-permute-start.5
  358.0 11.1 %collective-permute-done.5 = bf16[128,1024]{1,0:T(8,128)(2,1)S(1)} collective-permute-done((bf16[128,1024]{1,0:T(8,128)(2,1)S(1)}, bf16[128,1024]{1,0:T(8,128)(2,1)S(1)}, u32[]{:S(2)}, u32[]{:S(2)}) %collective-permute-start.5) | collective-permute-done | bytes 262176 | tf_op jit(solution)/shard_map/ppermute | solution.py:122
  369.1 1.6 broadcast.19
  370.7 1.0 constant_dynamic-update-slice_fusion.2
  371.7 1.4 collective-permute-start.6
  373.1 0.6 collective-permute-start.7
  373.7 11.6 %collective-permute-done.6 = bf16[256,1024]{1,0:T(8,128)(2,1)S(1)} collective-permute-done((bf16[256,1024]{1,0:T(8,128)(2,1)S(1)}, bf16[256,1024]{1,0:T(8,128)(2,1)S(1)}, u32[]{:S(2)}, u32[]{:S(2)}) %collective-permute-start.6) | collective-permute-done | bytes 524320 | tf_op jit(solution)/shard_map/ppermute | solution.py:124
  385.3 2.8 collective-permute-start.8
  388.2 0.8 constant_dynamic-update-slice_fusion.1
  389.1 0.8 constant_dynamic-update-slice_fusion
  389.9 2.9 collective-permute-done.8
  392.8 3.5 collective-permute-done.9
  396.3 0.8 maximum_dynamic-update-slice_fusion.1
  397.2 2.4 fusion.10
  399.5 4.0 fusion.14
  403.6 5.5 %add_convert_fusion = bf16[1024,896]{1,0:T(8,128)(2,1)} fusion(f32[1024,896]{1,0:T(8,128)S(1)} %fusion.14, bf16[1024,1024]{1,0:T(8,128)(2,1)} %maximum_dynamic-update-slice_fusion.1, bf16[1024,896]{1,0:T(8,128)(2,1)S(1)} %bitcast.74), kind=kOutput, calls=%fused_computation.5 | convolution fusion | flops 1880883200 | bytes 9437184 | tf_op jit(solution)/shard_map/dot_general | solution.py:170
  (31 shorter events, 0.8 us)
Async XLA Ops:
  0.0 106.7 %copy-start = (bf16[1024,896]{1,0:T(8,128)(2,1)S(1)}, bf16[1024,896]{1,0:T(8,128)(2,1)}, u32[]{:S(2)}) copy-start(bf16[1024,896]{1,0:T(8,128)(2,1)} %param.6) | copy-start | bytes 5505028
  12.6 91.4 %all-to-all-start = ((bf16[32,2,32,896]{3,1,2,0:T(2,128)(2,1)}), bf16[32,2,32,896]{3,1,2,0:T(2,128)(2,1)}, u32[]{:S(2)}, u32[]{:S(2)}) async-start(bf16[32,2,32,896]{3,1,2,0:T(2,128)(2,1)} %bitcast.71), calls=%async_computation | async-start | bytes 7340032 | tf_op jit(solution)/shard_map/all_to_all | solution.py:155
  113.0 6.4 %copy-start.5 = (s32[32,2,8]{0,2,1:T(8,128)S(1)}, s32[32,2,8]{0,2,1:T(8,128)}, u32[]{:S(2)}) copy-start(s32[32,2,8]{0,2,1:T(8,128)} %param.10) | copy-start | bytes 6148
  113.0 6.6 %copy-start.4 = (f32[1024,2]{0,1:T(2,128)S(1)}, f32[1024,2]{0,1:T(2,128)}, u32[]{:S(2)}) copy-start(f32[1024,2]{0,1:T(2,128)} %param.11) | copy-start | bytes 24580
  113.0 138.0 %all-to-all-start.1 = ((bf16[32,2,32,896]{3,1,2,0:T(2,128)(2,1)}), bf16[32,2,32,896]{3,1,2,0:T(2,128)(2,1)}, u32[]{:S(2)}, u32[]{:S(2)}) async-start(bf16[32,2,32,896]{3,1,2,0:T(2,128)(2,1)} %bitcast.70), calls=%async_computation.1 | async-start | bytes 7340032 | tf_op jit(solution)/shard_map/all_to_all | solution.py:155
  119.7 2.2 copy-start.2
  208.8 18.2 %copy-start.6 = (s32[32,2]{0,1:T(2,128)S(1)}, s32[32,2]{0,1:T(2,128)}, u32[]{:S(2)}) copy-start(s32[32,2]{0,1:T(2,128)} %param.9) | copy-start | bytes 772
  208.8 13.6 %collective-permute-start = (bf16[128,1024]{1,0:T(8,128)(2,1)S(1)}, bf16[128,1024]{1,0:T(8,128)(2,1)S(1)}, u32[]{:S(2)}, u32[]{:S(2)}) collective-permute-start(bf16[128,1024]{1,0:T(8,128)(2,1)S(1)} %fusion.5), channel_id=1, source_target_pairs={{0,1},{1,0},{2,3},{3,2},{4,5},{5,4},{6,7},{7,6},{8,9},{9,8},{10,11... | collective-permute-start | bytes 786440 | tf_op jit(solution)/shard_map/ppermute | solution.py:122
  225.0 13.7 %collective-permute-start.1 = (bf16[256,1024]{1,0:T(8,128)(2,1)S(1)}, bf16[256,1024]{1,0:T(8,128)(2,1)S(1)}, u32[]{:S(2)}, u32[]{:S(2)}) collective-permute-start(bf16[256,1024]{1,0:T(8,128)(2,1)S(1)} %get-tuple-element.18), channel_id=1, source_target_pairs={{0,2},{1,3},{2,4},{3,5},{4,6},{5,7},{6,0},{7,1},{8,10},{9,11},{10,... | collective-permute-start | bytes 1572872 | tf_op jit(solution)/shard_map/ppermute | solution.py:124
  225.3 15.7 %collective-permute-start.2 = (bf16[256,1024]{1,0:T(8,128)(2,1)S(1)}, bf16[256,1024]{1,0:T(8,128)(2,1)S(1)}, u32[]{:S(2)}, u32[]{:S(2)}) collective-permute-start(bf16[256,1024]{1,0:T(8,128)(2,1)S(1)} %get-tuple-element.18), channel_id=1, source_target_pairs={{0,6},{1,7},{2,0},{3,1},{4,2},{5,3},{6,4},{7,5},{8,14},{9,15},{10,... | collective-permute-start | bytes 1572872 | tf_op jit(solution)/shard_map/ppermute | solution.py:125
  239.4 8.1 %collective-permute-start.3 = (bf16[128,1024]{1,0:T(8,128)(2,1)}, bf16[128,1024]{1,0:T(8,128)(2,1)}, u32[]{:S(2)}, u32[]{:S(2)}) collective-permute-start(bf16[128,1024]{1,0:T(8,128)(2,1)} %slice.65), channel_id=1, source_target_pairs={{0,2},{1,3},{2,4},{3,5},{4,6},{5,7},{6,0},{7,1},{8,10},{9,11},{10,... | collective-permute-start | bytes 786440 | tf_op jit(solution)/shard_map/ppermute | solution.py:126
  241.0 8.2 %collective-permute-start.4 = (bf16[128,1024]{1,0:T(8,128)(2,1)S(1)}, bf16[128,1024]{1,0:T(8,128)(2,1)S(1)}, u32[]{:S(2)}, u32[]{:S(2)}) collective-permute-start(bf16[128,1024]{1,0:T(8,128)(2,1)S(1)} %slice.66), channel_id=1, source_target_pairs={{0,6},{1,7},{2,0},{3,1},{4,2},{5,3},{6,4},{7,5},{8,14},{9,15},{10,... | collective-permute-start | bytes 786440 | tf_op jit(solution)/shard_map/ppermute | solution.py:127
  260.0 137.2 %all-to-all-start.2 = ((bf16[32,2,32,896]{3,2,1,0:T(8,128)(2,1)}), bf16[32,2,32,896]{3,2,1,0:T(8,128)(2,1)}, u32[]{:S(2)}, u32[]{:S(2)}) async-start(bf16[32,2,32,896]{3,2,1,0:T(8,128)(2,1)} %bitcast.69), calls=%async_computation.2 | async-start | bytes 7340032 | tf_op jit(solution)/shard_map/all_to_all | solution.py:166
  266.8 2.2 copy-start.3
  353.9 15.2 %collective-permute-start.5 = (bf16[128,1024]{1,0:T(8,128)(2,1)S(1)}, bf16[128,1024]{1,0:T(8,128)(2,1)S(1)}, u32[]{:S(2)}, u32[]{:S(2)}) collective-permute-start(bf16[128,1024]{1,0:T(8,128)(2,1)S(1)} %fusion), channel_id=1, source_target_pairs={{0,1},{1,0},{2,3},{3,2},{4,5},{5,4},{6,7},{7,6},{8,9},{9,8},{10,11... | collective-permute-start | bytes 786440 | tf_op jit(solution)/shard_map/ppermute | solution.py:122
  371.7 13.6 %collective-permute-start.6 = (bf16[256,1024]{1,0:T(8,128)(2,1)S(1)}, bf16[256,1024]{1,0:T(8,128)(2,1)S(1)}, u32[]{:S(2)}, u32[]{:S(2)}) collective-permute-start(bf16[256,1024]{1,0:T(8,128)(2,1)S(1)} %get-tuple-element.16), channel_id=1, source_target_pairs={{0,2},{1,3},{2,4},{3,5},{4,6},{5,7},{6,0},{7,1},{8,10},{9,11},{10,... | collective-permute-start | bytes 1572872 | tf_op jit(solution)/shard_map/ppermute | solution.py:124
  373.1 15.0 %collective-permute-start.7 = (bf16[256,1024]{1,0:T(8,128)(2,1)S(1)}, bf16[256,1024]{1,0:T(8,128)(2,1)S(1)}, u32[]{:S(2)}, u32[]{:S(2)}) collective-permute-start(bf16[256,1024]{1,0:T(8,128)(2,1)S(1)} %get-tuple-element.16), channel_id=1, source_target_pairs={{0,6},{1,7},{2,0},{3,1},{4,2},{5,3},{6,4},{7,5},{8,14},{9,15},{10,... | collective-permute-start | bytes 1572872 | tf_op jit(solution)/shard_map/ppermute | solution.py:125
  385.3 7.5 %collective-permute-start.8 = (bf16[128,1024]{1,0:T(8,128)(2,1)S(1)}, bf16[128,1024]{1,0:T(8,128)(2,1)S(1)}, u32[]{:S(2)}, u32[]{:S(2)}) collective-permute-start(bf16[128,1024]{1,0:T(8,128)(2,1)S(1)} %slice.71), channel_id=1, source_target_pairs={{0,2},{1,3},{2,4},{3,5},{4,6},{5,7},{6,0},{7,1},{8,10},{9,11},{10,... | collective-permute-start | bytes 786440 | tf_op jit(solution)/shard_map/ppermute | solution.py:126
  388.1 8.2 %collective-permute-start.9 = (bf16[128,1024]{1,0:T(8,128)(2,1)S(1)}, bf16[128,1024]{1,0:T(8,128)(2,1)S(1)}, u32[]{:S(2)}, u32[]{:S(2)}) collective-permute-start(bf16[128,1024]{1,0:T(8,128)(2,1)S(1)} %slice.72), channel_id=1, source_target_pairs={{0,6},{1,7},{2,0},{3,1},{4,2},{5,3},{6,4},{7,5},{8,14},{9,15},{10,... | collective-permute-start | bytes 786440 | tf_op jit(solution)/shard_map/ppermute | solution.py:127
  403.5 5.5 %copy-start.1 = (bf16[1024,896]{1,0:T(8,128)(2,1)S(1)}, bf16[1024,896]{1,0:T(8,128)(2,1)}, u32[]{:S(2)}) copy-start(bf16[1024,896]{1,0:T(8,128)(2,1)} %param.6) | copy-start | bytes 5505028

commit v3 on v2

--- a/solution.py
+++ b/solution.py
@@ -160,18 +160,18 @@
         shares = group_reduce_scatter(partial_here, collective_id=slot)
         shares = shares.reshape(n_dp // group_size, 2, ff_here, row_count)
         hidden = (token_scale[slot] * jax.nn.silu(shares[:, 0]) * shares[:, 1]).astype(jnp.bfloat16)
-        hiddens.append(group_all_gather(hidden.reshape(-1, row_count)))
+        hiddens.append(hidden.reshape(-1, row_count))
         pending = partial_here
     pending, send_out = lax.optimization_barrier((pending, send_out))
     weights_out = lax.all_to_all(send_out, "dp", 0, 0, tiled=True)
 
-    combined = None
-    for slot in range(slots):
-        term = lax.dot_general(
-            hiddens[slot], weights_out[:, slot].reshape(-1, width_here), (((0,), (0,)), ((), ())),
-            preferred_element_type=jnp.float32,
-        )
-        combined = term if combined is None else combined + term
+    hidden_all = group_all_gather(jnp.concatenate(hiddens, axis=0))
+    hidden_all = hidden_all.reshape(group_size, slots, n_dp // group_size, ff_here, row_count)
+    weights_out = weights_out.reshape(group_size, n_dp // group_size, slots, ff_here, width_here)
+    combined = lax.dot_general(
+        hidden_all, weights_out, (((0, 1, 2, 3), (0, 2, 1, 3)), ((), ())),
+        preferred_element_type=jnp.float32,
+    )
     return combined.astype(jnp.bfloat16)
 
 

time: 410 us -> 413 us (level)
  waiting for transfers between devices: 125 us -> 143 us
  starting transfers between devices: 36.6 us -> 26.9 us
    all_to_all x2, waiting for transfers between devices: 70.8 us -> 86.4 us  [on_device(): lax.all_to_all(piece, 'dp', 0, 0, tiled=True).reshape(-1, width_here)]
    dot_general x2 -> x1, matrix products: 9.44 us -> 9.12 us  [on_device(): lax.dot_general(hidden_all, weights_out, (((0, 1, 2, 3), (0, 2, 1, 3)), (...]
    ppermute x2 -> x1, waiting for transfers between devices: 23.2 us -> 23.4 us  [group_all_gather(): partner = lax.ppermute(h, 'group', _z_flip(size))]
    ppermute x2 -> x1, waiting for transfers between devices: 23.1 us -> 23 us  [group_all_gather(): from_down = lax.ppermute(pair, 'group', _y_shift(size, 1))]
  transfers between devices with their start and end apart: 13 -> 8, of which waited for: 8 -> 6; matrix products, arithmetic and copies ran while one was open for 7% -> 7% of each run, Pallas kernels for 42% -> 41%
where the time goes in v3:
time: 413 us; the launch traced here: 412 us
  Pallas kernels  169 us (41%)
  waiting for transfers between devices  143 us (35%)
  local copies, waits for them, and re-layouts  47.2 us (11%)
  starting transfers between devices  26.9 us (7%)
  matrix products  21.7 us (5%)
    pallas_call x2, Pallas kernels, group_reduce_scatter(): pl.pallas_call(_rs_kernel, out_shape=jax.ShapeDtypeStruct((r // size, c),...  169 us
    all_to_all x2, waiting for transfers between devices, on_device(): lax.all_to_all(piece, 'dp', 0, 0, tiled=True).reshape(-1, width_here)  86.4 us
    ppermute x1, waiting for transfers between devices, group_all_gather(): partner = lax.ppermute(h, 'group', _z_flip(size))  23.4 us
    gather x2, local copies, waits for them, and re-layouts, on_device(): jnp.take(proj_in, expert_list[:, slot], axis=0, mode='clip')  23.3 us
    ppermute x1, waiting for transfers between devices, group_all_gather(): from_down = lax.ppermute(pair, 'group', _y_shift(size, 1))  23 us
    all_to_all x2, starting transfers between devices, on_device(): lax.all_to_all(piece, 'dp', 0, 0, tiled=True).reshape(-1, width_here)  15.2 us
    dot_general x2, matrix products, on_device(): jnp.dot(weight_in, tokens.T, preferred_element_type=jnp.float32)  12.6 us
    dot_general x1, matrix products, on_device(): lax.dot_general(hidden_all, weights_out, (((0, 1, 2, 3), (0, 2, 1, 3)), (...  9.12 us
  transfers between devices with their start and end apart: 8, of which 6 were waited for; matrix products, arithmetic and copies ran while one was open for 7% of the time, Pallas kernels for 41%

profile of v3, /device:TPU:24, one launch (start us, length us, event | category | flops | bytes accessed | tf_op | source)
XLA Modules:
  0.0 412.3 jit_solution(6141802176771352564)
XLA Ops:
  0.0 0.8 slice_bitcast_fusion
  0.8 11.7 %gather_fusion = bf16[32,32,2,896]{3,2,1,0:T(2,128)(2,1)} fusion(bf16[32,32,2,896]{3,2,1,0:T(2,128)(2,1)} %param.7, s32[1024]{0:T(1024)S(1)} %get-tuple-element.26), kind=kCustom, calls=%fused_computation | custom fusion | bytes 7340160 | tf_op jit(solution)/shard_map/jit(_take)/gather | solution.py:153
  12.5 8.9 %all-to-all-start = ((bf16[32,2,32,896]{3,1,2,0:T(2,128)(2,1)}), bf16[32,2,32,896]{3,1,2,0:T(2,128)(2,1)}, u32[]{:S(2)}, u32[]{:S(2)}) async-start(bf16[32,2,32,896]{3,1,2,0:T(2,128)(2,1)} %bitcast.72), calls=%async_computation | async-start | bytes 7340032 | tf_op jit(solution)/shard_map/all_to_all | solution.py:155
  21.4 11.6 %gather_fusion.1 = bf16[32,32,2,896]{3,2,1,0:T(2,128)(2,1)} fusion(bf16[32,32,2,896]{3,2,1,0:T(2,128)(2,1)} %param.7, s32[1024]{0:T(1024)S(1)} %get-tuple-element.25), kind=kCustom, calls=%fused_computation.1 | custom fusion | bytes 7340160 | tf_op jit(solution)/shard_map/jit(_take)/gather | solution.py:153
  33.0 70.9 %all-to-all-done = bf16[32,2,32,896]{3,1,2,0:T(2,128)(2,1)} async-done(((bf16[32,2,32,896]{3,1,2,0:T(2,128)(2,1)}), bf16[32,2,32,896]{3,1,2,0:T(2,128)(2,1)}, u32[]{:S(2)}, u32[]{:S(2)}) %all-to-all-start) | async-done | bytes 3670048 | tf_op jit(solution)/shard_map/all_to_all | solution.py:155
  103.9 2.7 copy.10
  106.7 6.3 %convolution_convert_fusion.1.x_ref = bf16[2048,1024]{1,0:T(8,128)(2,1)} fusion(bf16[2048,896]{1,0:T(8,128)(2,1)S(1)} %bitcast.73, bf16[1024,896]{1,0:T(8,128)(2,1)S(1)} %copy-done), kind=kOutput, calls=%fused_computation.4 | convolution fusion | flops 3760193536 | bytes 9699328 | tf_op jit(solution)/shard_map/dot_general | solution.py:158
  113.0 6.3 %all-to-all-start.1 = ((bf16[32,2,32,896]{3,1,2,0:T(2,128)(2,1)}), bf16[32,2,32,896]{3,1,2,0:T(2,128)(2,1)}, u32[]{:S(2)}, u32[]{:S(2)}) async-start(bf16[32,2,32,896]{3,1,2,0:T(2,128)(2,1)} %bitcast.71), calls=%async_computation.1 | async-start | bytes 7340032 | tf_op jit(solution)/shard_map/all_to_all | solution.py:155
  119.3 0.0 copy-done.6
  119.3 0.1 copy.12
  119.4 0.1 reshape.53
  119.5 0.0 copy-start.5
  119.5 0.0 copy-start.4
  119.5 4.2 %gather_fusion.2 = bf16[64,32,896]{2,1,0:T(8,128)(2,1)} fusion(bf16[32,32,896]{2,1,0:T(8,128)(2,1)} %param.8, s32[1024]{0:T(1024)S(1)} %pad_clamp_fusion), kind=kCustom, calls=%fused_computation.2 | custom fusion | bytes 7340288 | tf_op jit(solution)/shard_map/jit(_take)/gather | solution.py:148
  123.8 0.2 convert_reduce_fusion
  124.0 0.1 broadcast_bitcast_fusion
  124.1 2.2 copy-done.1
  126.3 82.0 %shard_map.64 = f32[256,1024]{1,0:T(8,128)S(1)} custom-call(bf16[2048,1024]{1,0:T(8,128)(2,1)S(1)} %copy-done.1), custom_call_target="tpu_custom_call" | custom-call | tf_op jit(solution)/shard_map/pallas_call | solution.py:95
  208.3 0.1 fusion.15
  208.4 0.2 fusion.9
  208.6 15.5 %all-to-all-done.1 = bf16[32,2,32,896]{3,1,2,0:T(2,128)(2,1)} async-done(((bf16[32,2,32,896]{3,1,2,0:T(2,128)(2,1)}), bf16[32,2,32,896]{3,1,2,0:T(2,128)(2,1)}, u32[]{:S(2)}, u32[]{:S(2)}) %all-to-all-start.1) | async-done | bytes 3670048 | tf_op jit(solution)/shard_map/all_to_all | solution.py:155
  224.1 2.7 copy.11
  226.8 6.3 %convolution_convert_fusion.x_ref = bf16[2048,1024]{1,0:T(8,128)(2,1)} fusion(bf16[2048,896]{1,0:T(8,128)(2,1)S(1)} %bitcast.74, bf16[1024,896]{1,0:T(8,128)(2,1)S(1)} %copy-done), kind=kOutput, calls=%fused_computation.3 | convolution fusion | flops 3760193536 | bytes 9699328 | tf_op jit(solution)/shard_map/dot_general | solution.py:158
  233.1 6.0 %all-to-all-start.2 = ((bf16[32,2,32,896]{3,2,1,0:T(8,128)(2,1)}), bf16[32,2,32,896]{3,2,1,0:T(8,128)(2,1)}, u32[]{:S(2)}, u32[]{:S(2)}) async-start(bf16[32,2,32,896]{3,2,1,0:T(8,128)(2,1)} %bitcast.70), calls=%async_computation.2 | async-start | bytes 7340032 | tf_op jit(solution)/shard_map/all_to_all | solution.py:166
  239.2 2.2 copy-done.2
  241.3 87.2 %shard_map.65 = f32[256,1024]{1,0:T(8,128)S(1)} custom-call(bf16[2048,1024]{1,0:T(8,128)(2,1)S(1)} %copy-done.2), custom_call_target="tpu_custom_call" | custom-call | tf_op jit(solution)/shard_map/pallas_call | solution.py:95
  328.6 0.1 fusion.14
  328.7 0.2 fusion.4
  328.9 1.6 collective-permute-start
  330.5 23.4 %collective-permute-done = bf16[256,1024]{1,0:T(8,128)(2,1)S(1)} collective-permute-done((bf16[256,1024]{1,0:T(8,128)(2,1)S(1)}, bf16[256,1024]{1,0:T(8,128)(2,1)S(1)}, u32[]{:S(2)}, u32[]{:S(2)}) %collective-permute-start) | collective-permute-done | bytes 524320 | tf_op jit(solution)/shard_map/ppermute | solution.py:122
  353.8 2.5 broadcast_in_dim.13
  356.3 1.5 constant_dynamic-update-slice_fusion.2
  357.8 0.3 collective-permute-start.1
  358.0 1.7 collective-permute-start.2
  359.8 23.0 %collective-permute-done.1 = bf16[512,1024]{1,0:T(8,128)(2,1)S(1)} collective-permute-done((bf16[512,1024]{1,0:T(8,128)(2,1)S(1)}, bf16[512,1024]{1,0:T(8,128)(2,1)S(1)}, u32[]{:S(2)}, u32[]{:S(2)}) %collective-permute-start.1) | collective-permute-done | bytes 1048608 | tf_op jit(solution)/shard_map/ppermute | solution.py:124
  382.8 0.9 slice.52
  383.6 1.5 collective-permute-start.3
  385.1 0.0 collective-permute-done.2
  385.1 1.0 copy-done.3
  386.1 0.8 slice.53
  387.0 0.5 collective-permute-start.4
  387.5 1.0 constant_dynamic-update-slice_fusion.1
  388.5 2.3 constant_dynamic-update-slice_fusion
  390.8 5.9 %collective-permute-done.3 = bf16[256,1024]{1,0:T(8,128)(2,1)S(1)} collective-permute-done((bf16[256,1024]{1,0:T(8,128)(2,1)}, bf16[256,1024]{1,0:T(8,128)(2,1)S(1)}, u32[]{:S(2)}, u32[]{:S(2)}) %collective-permute-start.3) | collective-permute-done | bytes 524320 | tf_op jit(solution)/shard_map/ppermute | solution.py:126
  396.8 4.3 %collective-permute-done.4 = bf16[256,1024]{1,0:T(8,128)(2,1)} collective-permute-done((bf16[256,1024]{1,0:T(8,128)(2,1)}, bf16[256,1024]{1,0:T(8,128)(2,1)}, u32[]{:S(2)}, u32[]{:S(2)}) %collective-permute-start.4) | collective-permute-done | bytes 524320 | tf_op jit(solution)/shard_map/ppermute | solution.py:127
  401.1 2.1 maximum_dynamic-update-slice_fusion
  403.2 0.0 all-to-all-done.2
  403.2 9.1 %bitcast_convert_fusion = bf16[1024,896]{1,0:T(8,128)(2,1)} fusion(bf16[8,2,4,32,1024]{4,3,2,1,0:T(8,128)(2,1)} %bitcast.15, bf16[8,4,2,32,896]{4,3,2,1,0:T(8,128)(2,1)} %bitcast.17), kind=kOutput, calls=%fused_computation.5 | convolution fusion | flops 3759013888 | bytes 9699328 | tf_op jit(solution)/shard_map/dot_general | solution.py:171
  (13 shorter events, 0.1 us)
Async XLA Ops:
  0.0 106.7 %copy-start = (bf16[1024,896]{1,0:T(8,128)(2,1)S(1)}, bf16[1024,896]{1,0:T(8,128)(2,1)}, u32[]{:S(2)}) copy-start(bf16[1024,896]{1,0:T(8,128)(2,1)} %param.6) | copy-start | bytes 5505028
  12.5 91.4 %all-to-all-start = ((bf16[32,2,32,896]{3,1,2,0:T(2,128)(2,1)}), bf16[32,2,32,896]{3,1,2,0:T(2,128)(2,1)}, u32[]{:S(2)}, u32[]{:S(2)}) async-start(bf16[32,2,32,896]{3,1,2,0:T(2,128)(2,1)} %bitcast.72), calls=%async_computation | async-start | bytes 7340032 | tf_op jit(solution)/shard_map/all_to_all | solution.py:155
  112.9 6.4 %copy-start.6 = (s32[32,2]{0,1:T(2,128)S(1)}, s32[32,2]{0,1:T(2,128)}, u32[]{:S(2)}) copy-start(s32[32,2]{0,1:T(2,128)} %param.9) | copy-start | bytes 772
  113.0 111.2 %all-to-all-start.1 = ((bf16[32,2,32,896]{3,1,2,0:T(2,128)(2,1)}), bf16[32,2,32,896]{3,1,2,0:T(2,128)(2,1)}, u32[]{:S(2)}, u32[]{:S(2)}) async-start(bf16[32,2,32,896]{3,1,2,0:T(2,128)(2,1)} %bitcast.71), calls=%async_computation.1 | async-start | bytes 7340032 | tf_op jit(solution)/shard_map/all_to_all | solution.py:155
  119.5 4.3 %copy-start.5 = (s32[32,2,8]{0,2,1:T(8,128)S(1)}, s32[32,2,8]{0,2,1:T(8,128)}, u32[]{:S(2)}) copy-start(s32[32,2,8]{0,2,1:T(8,128)} %param.10) | copy-start | bytes 6148
  119.5 4.5 %copy-start.4 = (f32[1024,2]{0,1:T(2,128)S(1)}, f32[1024,2]{0,1:T(2,128)}, u32[]{:S(2)}) copy-start(f32[1024,2]{0,1:T(2,128)} %param.11) | copy-start | bytes 24580
  124.1 2.2 copy-start.1
  233.1 170.1 %all-to-all-start.2 = ((bf16[32,2,32,896]{3,2,1,0:T(8,128)(2,1)}), bf16[32,2,32,896]{3,2,1,0:T(8,128)(2,1)}, u32[]{:S(2)}, u32[]{:S(2)}) async-start(bf16[32,2,32,896]{3,2,1,0:T(8,128)(2,1)} %bitcast.70), calls=%async_computation.2 | async-start | bytes 7340032 | tf_op jit(solution)/shard_map/all_to_all | solution.py:166
  239.2 2.2 copy-start.2
  328.9 24.9 %collective-permute-start = (bf16[256,1024]{1,0:T(8,128)(2,1)S(1)}, bf16[256,1024]{1,0:T(8,128)(2,1)S(1)}, u32[]{:S(2)}, u32[]{:S(2)}) collective-permute-start(bf16[256,1024]{1,0:T(8,128)(2,1)S(1)} %pad_maximum_fusion), channel_id=1, source_target_pairs={{0,1},{1,0},{2,3},{3,2},{4,5},{5,4},{6,7},{7,6},{8,9},{9,8},{10,11... | collective-permute-start | bytes 1572872 | tf_op jit(solution)/shard_map/ppermute | solution.py:122
  357.8 25.0 %collective-permute-start.1 = (bf16[512,1024]{1,0:T(8,128)(2,1)S(1)}, bf16[512,1024]{1,0:T(8,128)(2,1)S(1)}, u32[]{:S(2)}, u32[]{:S(2)}) collective-permute-start(bf16[512,1024]{1,0:T(8,128)(2,1)S(1)} %get-tuple-element.16), channel_id=1, source_target_pairs={{0,2},{1,3},{2,4},{3,5},{4,6},{5,7},{6,0},{7,1},{8,10},{9,11},{10,... | collective-permute-start | bytes 3145736 | tf_op jit(solution)/shard_map/ppermute | solution.py:124
  358.0 27.1 %collective-permute-start.2 = (bf16[512,1024]{1,0:T(8,128)(2,1)S(1)}, bf16[512,1024]{1,0:T(8,128)(2,1)S(1)}, u32[]{:S(2)}, u32[]{:S(2)}) collective-permute-start(bf16[512,1024]{1,0:T(8,128)(2,1)S(1)} %get-tuple-element.16), channel_id=1, source_target_pairs={{0,6},{1,7},{2,0},{3,1},{4,2},{5,3},{6,4},{7,5},{8,14},{9,15},{10,... | collective-permute-start | bytes 3145736 | tf_op jit(solution)/shard_map/ppermute | solution.py:125
  383.6 13.1 %collective-permute-start.3 = (bf16[256,1024]{1,0:T(8,128)(2,1)}, bf16[256,1024]{1,0:T(8,128)(2,1)S(1)}, u32[]{:S(2)}, u32[]{:S(2)}) collective-permute-start(bf16[256,1024]{1,0:T(8,128)(2,1)} %slice.52), channel_id=1, source_target_pairs={{0,2},{1,3},{2,4},{3,5},{4,6},{5,7},{6,0},{7,1},{8,10},{9,11},{10,... | collective-permute-start | bytes 1572872 | tf_op jit(solution)/shard_map/ppermute | solution.py:126
  385.1 1.0 copy-start.3
  387.0 14.1 %collective-permute-start.4 = (bf16[256,1024]{1,0:T(8,128)(2,1)}, bf16[256,1024]{1,0:T(8,128)(2,1)}, u32[]{:S(2)}, u32[]{:S(2)}) collective-permute-start(bf16[256,1024]{1,0:T(8,128)(2,1)} %slice.53), channel_id=1, source_target_pairs={{0,6},{1,7},{2,0},{3,1},{4,2},{5,3},{6,4},{7,5},{8,14},{9,15},{10,... | collective-permute-start | bytes 1572872 | tf_op jit(solution)/shard_map/ppermute | solution.py:127

commit v4 on v3

--- a/solution.py
+++ b/solution.py
@@ -147,12 +147,15 @@
 
     send_out = jnp.take(proj_out, expert_list, axis=0, mode="clip")
 
-    hiddens = []
-    pending = tokens
+    weights_in = []
     for slot in range(slots):
         piece = jnp.take(proj_in, expert_list[:, slot], axis=0, mode="clip").transpose(0, 2, 1, 3)
-        pending, piece = lax.optimization_barrier((pending, piece))
-        weight_in = lax.all_to_all(piece, "dp", 0, 0, tiled=True).reshape(-1, width_here)
+        weights_in.append(lax.all_to_all(piece, "dp", 0, 0, tiled=True).reshape(-1, width_here))
+    weights_out = lax.all_to_all(send_out, "dp", 0, 0, tiled=True)
+
+    hiddens = []
+    for slot in range(slots):
+        weight_in = weights_in[slot]
         if hiddens:
             weight_in, hiddens[-1] = lax.optimization_barrier((weight_in, hiddens[-1]))
         partial_here = jnp.dot(weight_in, tokens.T, preferred_element_type=jnp.float32)
@@ -161,9 +164,6 @@
         shares = shares.reshape(n_dp // group_size, 2, ff_here, row_count)
         hidden = (token_scale[slot] * jax.nn.silu(shares[:, 0]) * shares[:, 1]).astype(jnp.bfloat16)
         hiddens.append(hidden.reshape(-1, row_count))
-        pending = partial_here
-    pending, send_out = lax.optimization_barrier((pending, send_out))
-    weights_out = lax.all_to_all(send_out, "dp", 0, 0, tiled=True)
 
     hidden_all = group_all_gather(jnp.concatenate(hiddens, axis=0))
     hidden_all = hidden_all.reshape(group_size, slots, n_dp // group_size, ff_here, row_count)

time: 413 us -> 457 us (1.11)
  waiting for transfers between devices: 143 us -> 206 us
  Pallas kernels: 169 us -> 157 us
    all_to_all x2, waiting for transfers between devices: 86.4 us -> 149 us  [on_device(): lax.all_to_all(piece, 'dp', 0, 0, tiled=True).reshape(-1, width_here)]
    pallas_call x2, Pallas kernels: 169 us -> 157 us  [group_reduce_scatter(): pl.pallas_call(_rs_kernel, out_shape=jax.ShapeDtypeStruct((r // size, c),...]
  transfers between devices with their start and end apart: 8 -> 8, of which waited for: 6 -> 6; matrix products, arithmetic and copies ran while one was open for 7% -> 10% of each run, Pallas kernels for 41% -> 34%
where the time goes in v4:
time: 457 us
  waiting for transfers between devices  206 us (45%)
  Pallas kernels  157 us (34%)
  local copies, waits for them, and re-layouts  43 us (9%)
  starting transfers between devices  27.2 us (6%)
  matrix products  18.9 us (4%)
    pallas_call x2, Pallas kernels, group_reduce_scatter(): pl.pallas_call(_rs_kernel, out_shape=jax.ShapeDtypeStruct((r // size, c),...  157 us
    all_to_all x2, waiting for transfers between devices, on_device(): lax.all_to_all(piece, 'dp', 0, 0, tiled=True).reshape(-1, width_here)  149 us
    ppermute x1, waiting for transfers between devices, group_all_gather(): partner = lax.ppermute(h, 'group', _z_flip(size))  24.3 us
    gather x2, local copies, waits for them, and re-layouts, on_device(): jnp.take(proj_in, expert_list[:, slot], axis=0, mode='clip')  23.3 us
    ppermute x1, waiting for transfers between devices, group_all_gather(): from_down = lax.ppermute(pair, 'group', _y_shift(size, 1))  22.2 us
    all_to_all x2, starting transfers between devices, on_device(): lax.all_to_all(piece, 'dp', 0, 0, tiled=True).reshape(-1, width_here)  15 us
    dot_general x2, matrix products, on_device(): jnp.dot(weight_in, tokens.T, preferred_element_type=jnp.float32)  9.76 us
  transfers between devices with their start and end apart: 8, of which 6 were waited for; matrix products, arithmetic and copies ran while one was open for 10% of the time, Pallas kernels for 34%

profile of v4, /device:TPU:24, one launch (start us, length us, event | category | flops | bytes accessed | tf_op | source)
XLA Modules:
  0.0 456.8 jit_solution(17439592160931582879)
XLA Ops:
  0.0 0.0 copy-start
  0.0 0.8 slice_bitcast_fusion
  0.8 11.6 %gather_fusion.1 = bf16[32,32,2,896]{3,2,1,0:T(2,128)(2,1)} fusion(bf16[32,32,2,896]{3,2,1,0:T(2,128)(2,1)} %param.7, s32[1024]{0:T(1024)S(1)} %get-tuple-element.19), kind=kCustom, calls=%fused_computation.1 | custom fusion | bytes 7340160 | tf_op jit(solution)/shard_map/jit(_take)/gather | solution.py:152
  12.5 8.9 %all-to-all-start.1 = ((bf16[32,2,32,896]{3,1,2,0:T(2,128)(2,1)}), bf16[32,2,32,896]{3,1,2,0:T(2,128)(2,1)}, u32[]{:S(2)}, u32[]{:S(2)}) async-start(bf16[32,2,32,896]{3,1,2,0:T(2,128)(2,1)} %bitcast.72), calls=%async_computation.1 | async-start | bytes 7340032 | tf_op jit(solution)/shard_map/all_to_all | solution.py:153
  21.3 11.7 %gather_fusion = bf16[32,32,2,896]{3,2,1,0:T(2,128)(2,1)} fusion(bf16[32,32,2,896]{3,2,1,0:T(2,128)(2,1)} %param.7, s32[1024]{0:T(1024)S(1)} %get-tuple-element.20), kind=kCustom, calls=%fused_computation | custom fusion | bytes 7340160 | tf_op jit(solution)/shard_map/jit(_take)/gather | solution.py:152
  33.0 70.8 %all-to-all-done.1 = bf16[32,2,32,896]{3,1,2,0:T(2,128)(2,1)} async-done(((bf16[32,2,32,896]{3,1,2,0:T(2,128)(2,1)}), bf16[32,2,32,896]{3,1,2,0:T(2,128)(2,1)}, u32[]{:S(2)}, u32[]{:S(2)}) %all-to-all-start.1) | async-done | bytes 3670048 | tf_op jit(solution)/shard_map/all_to_all | solution.py:153
  103.9 6.2 %all-to-all-start = ((bf16[32,2,32,896]{3,1,2,0:T(2,128)(2,1)}), bf16[32,2,32,896]{3,1,2,0:T(2,128)(2,1)}, u32[]{:S(2)}, u32[]{:S(2)}) async-start(bf16[32,2,32,896]{3,1,2,0:T(2,128)(2,1)} %bitcast.71), calls=%async_computation | async-start | bytes 7340032 | tf_op jit(solution)/shard_map/all_to_all | solution.py:153
  110.0 0.0 copy-done.4
  110.0 0.1 copy.12
  110.1 0.1 reshape.53
  110.3 4.2 gather_fusion.2
  114.5 78.1 %all-to-all-done = bf16[32,2,32,896]{3,1,2,0:T(2,128)(2,1)} async-done(((bf16[32,2,32,896]{3,1,2,0:T(2,128)(2,1)}), bf16[32,2,32,896]{3,1,2,0:T(2,128)(2,1)}, u32[]{:S(2)}, u32[]{:S(2)}) %all-to-all-start) | async-done | bytes 3670048 | tf_op jit(solution)/shard_map/all_to_all | solution.py:153
  192.6 6.3 %all-to-all-start.2 = ((bf16[32,2,32,896]{3,2,1,0:T(8,128)(2,1)}), bf16[32,2,32,896]{3,2,1,0:T(8,128)(2,1)}, u32[]{:S(2)}, u32[]{:S(2)}) async-start(bf16[32,2,32,896]{3,2,1,0:T(8,128)(2,1)} %bitcast.70), calls=%async_computation.2 | async-start | bytes 7340032 | tf_op jit(solution)/shard_map/all_to_all | solution.py:154
  198.9 0.0 copy-done.3
  198.9 0.2 convert_reduce_fusion
  199.1 0.1 broadcast_bitcast_fusion
  199.2 0.0 copy-done.2
  199.2 2.7 copy.11
  201.9 0.0 copy-done
  201.9 4.9 %convolution_convert_fusion.1.x_ref = bf16[2048,1024]{1,0:T(8,128)(2,1)S(1)} fusion(bf16[2048,896]{1,0:T(8,128)(2,1)S(1)} %bitcast.74, bf16[1024,896]{1,0:T(8,128)(2,1)S(1)} %copy-done), kind=kOutput, calls=%fused_computation.4 | convolution fusion | flops 3760193536 | bytes 9699328 | tf_op jit(solution)/shard_map/dot_general | solution.py:161
  206.8 81.1 %shard_map.64 = f32[256,1024]{1,0:T(8,128)S(1)} custom-call(bf16[2048,1024]{1,0:T(8,128)(2,1)S(1)} %convolution_convert_fusion.1.x_ref), custom_call_target="tpu_custom_call" | custom-call | tf_op jit(solution)/shard_map/pallas_call | solution.py:95
  287.9 2.7 copy.10
  290.6 0.1 fusion.15
  290.7 0.2 fusion.9
  290.9 4.9 %convolution_convert_fusion.x_ref = bf16[2048,1024]{1,0:T(8,128)(2,1)S(1)} fusion(bf16[2048,896]{1,0:T(8,128)(2,1)S(1)} %bitcast.73, bf16[1024,896]{1,0:T(8,128)(2,1)S(1)} %copy-done), kind=kOutput, calls=%fused_computation.3 | convolution fusion | flops 3760193536 | bytes 9699328 | tf_op jit(solution)/shard_map/dot_general | solution.py:161
  295.8 76.0 %shard_map.65 = f32[256,1024]{1,0:T(8,128)S(1)} custom-call(bf16[2048,1024]{1,0:T(8,128)(2,1)S(1)} %convolution_convert_fusion.x_ref), custom_call_target="tpu_custom_call" | custom-call | tf_op jit(solution)/shard_map/pallas_call | solution.py:95
  371.8 0.1 fusion.14
  371.9 0.2 fusion.4
  372.2 0.1 collective-permute-start
  372.3 24.3 %collective-permute-done = bf16[256,1024]{1,0:T(8,128)(2,1)S(1)} collective-permute-done((bf16[256,1024]{1,0:T(8,128)(2,1)S(1)}, bf16[256,1024]{1,0:T(8,128)(2,1)S(1)}, u32[]{:S(2)}, u32[]{:S(2)}) %collective-permute-start) | collective-permute-done | bytes 524320 | tf_op jit(solution)/shard_map/ppermute | solution.py:122
  396.6 2.6 broadcast_in_dim.13
  399.2 1.5 constant_dynamic-update-slice_fusion.2
  400.6 1.7 collective-permute-start.1
  402.3 0.4 collective-permute-start.2
  402.6 22.2 %collective-permute-done.1 = bf16[512,1024]{1,0:T(8,128)(2,1)S(1)} collective-permute-done((bf16[512,1024]{1,0:T(8,128)(2,1)S(1)}, bf16[512,1024]{1,0:T(8,128)(2,1)S(1)}, u32[]{:S(2)}, u32[]{:S(2)}) %collective-permute-start.1) | collective-permute-done | bytes 1048608 | tf_op jit(solution)/shard_map/ppermute | solution.py:124
  424.9 0.9 slice.52
  425.8 3.7 collective-permute-start.3
  429.4 0.0 collective-permute-done.2
  429.5 1.0 copy-done.1
  430.4 0.8 slice.53
  431.3 0.0 collective-permute-start.4
  431.3 1.1 constant_dynamic-update-slice_fusion.1
  432.3 2.3 constant_dynamic-update-slice_fusion
  434.7 5.6 %collective-permute-done.3 = bf16[256,1024]{1,0:T(8,128)(2,1)S(1)} collective-permute-done((bf16[256,1024]{1,0:T(8,128)(2,1)}, bf16[256,1024]{1,0:T(8,128)(2,1)S(1)}, u32[]{:S(2)}, u32[]{:S(2)}) %collective-permute-start.3) | collective-permute-done | bytes 524320 | tf_op jit(solution)/shard_map/ppermute | solution.py:126
  440.3 5.2 %collective-permute-done.4 = bf16[256,1024]{1,0:T(8,128)(2,1)} collective-permute-done((bf16[256,1024]{1,0:T(8,128)(2,1)}, bf16[256,1024]{1,0:T(8,128)(2,1)}, u32[]{:S(2)}, u32[]{:S(2)}) %collective-permute-start.4) | collective-permute-done | bytes 524320 | tf_op jit(solution)/shard_map/ppermute | solution.py:127
  445.5 2.2 maximum_dynamic-update-slice_fusion
  447.7 0.0 all-to-all-done.2
  447.7 9.1 %bitcast_convert_fusion = bf16[1024,896]{1,0:T(8,128)(2,1)} fusion(bf16[8,2,4,32,1024]{4,3,2,1,0:T(8,128)(2,1)} %bitcast.15, bf16[8,4,2,32,896]{4,3,2,1,0:T(8,128)(2,1)} %bitcast.17), kind=kOutput, calls=%fused_computation.5 | convolution fusion | flops 3759013888 | bytes 9699328 | tf_op jit(solution)/shard_map/dot_general | solution.py:171
  (9 shorter events, 0.1 us)
Async XLA Ops:
  0.0 201.9 %copy-start = (bf16[1024,896]{1,0:T(8,128)(2,1)S(1)}, bf16[1024,896]{1,0:T(8,128)(2,1)}, u32[]{:S(2)}) copy-start(bf16[1024,896]{1,0:T(8,128)(2,1)} %param.6) | copy-start | bytes 5505028
  12.5 91.4 %all-to-all-start.1 = ((bf16[32,2,32,896]{3,1,2,0:T(2,128)(2,1)}), bf16[32,2,32,896]{3,1,2,0:T(2,128)(2,1)}, u32[]{:S(2)}, u32[]{:S(2)}) async-start(bf16[32,2,32,896]{3,1,2,0:T(2,128)(2,1)} %bitcast.72), calls=%async_computation.1 | async-start | bytes 7340032 | tf_op jit(solution)/shard_map/all_to_all | solution.py:153
  103.9 6.2 %copy-start.4 = (s32[32,2]{0,1:T(2,128)S(1)}, s32[32,2]{0,1:T(2,128)}, u32[]{:S(2)}) copy-start(s32[32,2]{0,1:T(2,128)} %param.9) | copy-start | bytes 772
  103.9 88.7 %all-to-all-start = ((bf16[32,2,32,896]{3,1,2,0:T(2,128)(2,1)}), bf16[32,2,32,896]{3,1,2,0:T(2,128)(2,1)}, u32[]{:S(2)}, u32[]{:S(2)}) async-start(bf16[32,2,32,896]{3,1,2,0:T(2,128)(2,1)} %bitcast.71), calls=%async_computation | async-start | bytes 7340032 | tf_op jit(solution)/shard_map/all_to_all | solution.py:153
  192.6 6.4 %copy-start.3 = (s32[32,2,8]{0,2,1:T(8,128)S(1)}, s32[32,2,8]{0,2,1:T(8,128)}, u32[]{:S(2)}) copy-start(s32[32,2,8]{0,2,1:T(8,128)} %param.10) | copy-start | bytes 6148
  192.6 6.6 %copy-start.2 = (f32[1024,2]{0,1:T(2,128)S(1)}, f32[1024,2]{0,1:T(2,128)}, u32[]{:S(2)}) copy-start(f32[1024,2]{0,1:T(2,128)} %param.11) | copy-start | bytes 24580
  192.6 255.1 %all-to-all-start.2 = ((bf16[32,2,32,896]{3,2,1,0:T(8,128)(2,1)}), bf16[32,2,32,896]{3,2,1,0:T(8,128)(2,1)}, u32[]{:S(2)}, u32[]{:S(2)}) async-start(bf16[32,2,32,896]{3,2,1,0:T(8,128)(2,1)} %bitcast.70), calls=%async_computation.2 | async-start | bytes 7340032 | tf_op jit(solution)/shard_map/all_to_all | solution.py:154
  372.2 24.4 %collective-permute-start = (bf16[256,1024]{1,0:T(8,128)(2,1)S(1)}, bf16[256,1024]{1,0:T(8,128)(2,1)S(1)}, u32[]{:S(2)}, u32[]{:S(2)}) collective-permute-start(bf16[256,1024]{1,0:T(8,128)(2,1)S(1)} %pad_maximum_fusion), channel_id=1, source_target_pairs={{0,1},{1,0},{2,3},{3,2},{4,5},{5,4},{6,7},{7,6},{8,9},{9,8},{10,11... | collective-permute-start | bytes 1572872 | tf_op jit(solution)/shard_map/ppermute | solution.py:122
  400.6 24.3 %collective-permute-start.1 = (bf16[512,1024]{1,0:T(8,128)(2,1)S(1)}, bf16[512,1024]{1,0:T(8,128)(2,1)S(1)}, u32[]{:S(2)}, u32[]{:S(2)}) collective-permute-start(bf16[512,1024]{1,0:T(8,128)(2,1)S(1)} %get-tuple-element.10), channel_id=1, source_target_pairs={{0,2},{1,3},{2,4},{3,5},{4,6},{5,7},{6,0},{7,1},{8,10},{9,11},{10,... | collective-permute-start | bytes 3145736 | tf_op jit(solution)/shard_map/ppermute | solution.py:124
  402.3 27.2 %collective-permute-start.2 = (bf16[512,1024]{1,0:T(8,128)(2,1)S(1)}, bf16[512,1024]{1,0:T(8,128)(2,1)S(1)}, u32[]{:S(2)}, u32[]{:S(2)}) collective-permute-start(bf16[512,1024]{1,0:T(8,128)(2,1)S(1)} %get-tuple-element.10), channel_id=1, source_target_pairs={{0,6},{1,7},{2,0},{3,1},{4,2},{5,3},{6,4},{7,5},{8,14},{9,15},{10,... | collective-permute-start | bytes 3145736 | tf_op jit(solution)/shard_map/ppermute | solution.py:125
  425.8 14.5 %collective-permute-start.3 = (bf16[256,1024]{1,0:T(8,128)(2,1)}, bf16[256,1024]{1,0:T(8,128)(2,1)S(1)}, u32[]{:S(2)}, u32[]{:S(2)}) collective-permute-start(bf16[256,1024]{1,0:T(8,128)(2,1)} %slice.52), channel_id=1, source_target_pairs={{0,2},{1,3},{2,4},{3,5},{4,6},{5,7},{6,0},{7,1},{8,10},{9,11},{10,... | collective-permute-start | bytes 1572872 | tf_op jit(solution)/shard_map/ppermute | solution.py:126
  429.4 1.0 copy-start.1
  431.3 14.2 %collective-permute-start.4 = (bf16[256,1024]{1,0:T(8,128)(2,1)}, bf16[256,1024]{1,0:T(8,128)(2,1)}, u32[]{:S(2)}, u32[]{:S(2)}) collective-permute-start(bf16[256,1024]{1,0:T(8,128)(2,1)} %slice.53), channel_id=1, source_target_pairs={{0,6},{1,7},{2,0},{3,1},{4,2},{5,3},{6,4},{7,5},{8,14},{9,15},{10,... | collective-permute-start | bytes 1572872 | tf_op jit(solution)/shard_map/ppermute | solution.py:127

commit v5 on v2

--- a/solution.py
+++ b/solution.py
@@ -7,6 +7,7 @@
 
 
 Y_PARTS = 4
+COL_PARTS = 2
 
 
 def _perm(size, fn):
@@ -29,7 +30,9 @@
     y, zh = j // z_parts, j % z_parts
     rows = x_ref.shape[0] // Y_PARTS
     half = rows // 2
+    width = x_ref.shape[1] // COL_PARTS
     mesh_id = pl.DeviceIdType.MESH
+    f32 = jnp.float32
 
     def peer(dy):
         return {"group": ((y + dy) % Y_PARTS) * z_parts + zh}
@@ -44,47 +47,60 @@
         pl.semaphore_signal(barrier, inc=1, device_id=dev, device_id_type=mesh_id)
     pl.semaphore_wait(barrier, 3)
 
-    def remote(src, dst, k, dev):
+    def remote(src, dst, p, k, dev):
         c = pltpu.make_async_remote_copy(
-            src_ref=src, dst_ref=dst, send_sem=send_sem.at[k], recv_sem=recv_sem.at[k],
+            src_ref=src, dst_ref=dst, send_sem=send_sem.at[p, k], recv_sem=recv_sem.at[p, k],
             device_id=dev, device_id_type=mesh_id,
         )
         c.start()
         return c
 
     far = block_at(2)
-    first = [
-        remote(x_ref.at[pl.ds(block_at(1), rows)], ybuf.at[0], 0, up),
-        remote(x_ref.at[pl.ds(block_at(-1), rows)], ybuf.at[1], 1, down),
-        remote(x_ref.at[pl.ds(far, half)], fwd.at[0], 2, up),
-        remote(x_ref.at[pl.ds(far + half, half)], fwd.at[1], 3, down),
-    ]
-    local = pltpu.make_async_copy(x_ref.at[pl.ds(block_at(0), rows)], own, local_sem.at[0])
-    local.start()
-    for c in first:
-        c.wait()
-    second = [
-        remote(fwd.at[0], relay.at[pl.ds(0, half)], 4, up),
-        remote(fwd.at[1], relay.at[pl.ds(half, half)], 5, down),
-    ]
-    local.wait()
-
-    f32 = jnp.float32
-
-    def near_sum(lo):
-        sl = pl.ds(lo, half)
-        return own[sl, :].astype(f32) + ybuf[0, sl, :].astype(f32) + ybuf[1, sl, :].astype(f32)
-
     other_lo = pl.multiple_of((1 - zh) * half, half)
     mine_lo = pl.multiple_of(zh * half, half)
-    out_ref[...] = near_sum(other_lo)
-    for c in second:
-        c.wait()
-    zsend[...] = (out_ref[...] + relay[pl.ds(other_lo, half), :].astype(f32)).astype(zsend.dtype)
-    zc = remote(zsend, zrecv, 6, partner)
-    out_ref[...] = near_sum(mine_lo) + relay[pl.ds(mine_lo, half), :].astype(f32)
-    zc.wait()
-    out_ref[...] += zrecv[...].astype(f32)
+
+    def first_round(p):
+        cols = pl.ds(p * width, width)
+        copies = [
+            remote(x_ref.at[pl.ds(block_at(1), rows), cols], ybuf.at[p, 0], p, 0, up),
+            remote(x_ref.at[pl.ds(block_at(-1), rows), cols], ybuf.at[p, 1], p, 1, down),
+            remote(x_ref.at[pl.ds(far, half), cols], fwd.at[p, 0], p, 2, up),
+            remote(x_ref.at[pl.ds(far + half, half), cols], fwd.at[p, 1], p, 3, down),
+        ]
+        local = pltpu.make_async_copy(
+            x_ref.at[pl.ds(block_at(0), rows), cols], own.at[p], local_sem.at[p])
+        local.start()
+        return copies, local
+
+    def near_sum(p, lo):
+        sl = pl.ds(lo, half)
+        return (own[p, sl, :].astype(f32) + ybuf[p, 0, sl, :].astype(f32)
+                + ybuf[p, 1, sl, :].astype(f32))
+
+    pending = first_round(0)
+    z_copies = []
+    for p in range(COL_PARTS):
+        copies, local = pending
+        for c in copies:
+            c.wait()
+        second = [
+            remote(fwd.at[p, 0], relay.at[p, pl.ds(0, half)], p, 4, up),
+            remote(fwd.at[p, 1], relay.at[p, pl.ds(half, half)], p, 5, down),
+        ]
+        if p + 1 < COL_PARTS:
+            pending = first_round(p + 1)
+        local.wait()
+        cols = pl.ds(p * width, width)
+        out_ref[:, cols] = near_sum(p, other_lo)
+        for c in second:
+            c.wait()
+        zsend[p] = (out_ref[:, cols] + relay[p, pl.ds(other_lo, half), :].astype(f32)).astype(zsend.dtype)
+        z_copies.append(remote(zsend.at[p], zrecv.at[p], p, 6, partner))
+        out_ref[:, cols] = near_sum(p, mine_lo) + relay[p, pl.ds(mine_lo, half), :].astype(f32)
+    for p, zc in enumerate(z_copies):
+        zc.wait()
+        cols = pl.ds(p * width, width)
+        out_ref[:, cols] += zrecv[p].astype(f32)
 
 
 def group_reduce_scatter(x, collective_id=0):
@@ -92,21 +108,22 @@
     r, c = x.shape
     rows = r // Y_PARTS
     half = rows // 2
+    width = c // COL_PARTS
     return pl.pallas_call(
         _rs_kernel,
         out_shape=jax.ShapeDtypeStruct((r // size, c), jnp.float32),
         in_specs=[pl.BlockSpec(memory_space=pl.ANY)],
         out_specs=pl.BlockSpec(memory_space=pltpu.VMEM),
         scratch_shapes=[
-            pltpu.VMEM((2, rows, c), x.dtype),
-            pltpu.VMEM((2, half, c), x.dtype),
-            pltpu.VMEM((rows, c), x.dtype),
-            pltpu.VMEM((rows, c), x.dtype),
-            pltpu.VMEM((half, c), x.dtype),
-            pltpu.VMEM((half, c), x.dtype),
-            pltpu.SemaphoreType.DMA((7,)),
-            pltpu.SemaphoreType.DMA((7,)),
-            pltpu.SemaphoreType.DMA((1,)),
+            pltpu.VMEM((COL_PARTS, 2, rows, width), x.dtype),
+            pltpu.VMEM((COL_PARTS, 2, half, width), x.dtype),
+            pltpu.VMEM((COL_PARTS, rows, width), x.dtype),
+            pltpu.VMEM((COL_PARTS, rows, width), x.dtype),
+            pltpu.VMEM((COL_PARTS, half, width), x.dtype),
+            pltpu.VMEM((COL_PARTS, half, width), x.dtype),
+            pltpu.SemaphoreType.DMA((COL_PARTS, 7)),
+            pltpu.SemaphoreType.DMA((COL_PARTS, 7)),
+            pltpu.SemaphoreType.DMA((COL_PARTS,)),
         ],
         compiler_params=pltpu.CompilerParams(
             collective_id=collective_id, has_side_effects=True, vmem_limit_bytes=48 * 1024 * 1024

time: 410 us -> 412 us (level)
  Pallas kernels: 171 us -> 182 us
  waiting for transfers between devices: 125 us -> 117 us
    pallas_call x2, Pallas kernels: 171 us -> 182 us  [group_reduce_scatter(): pl.pallas_call(_rs_kernel, out_shape=jax.ShapeDtypeStruct((r // size, c),...]
    ppermute x2, waiting for transfers between devices: 23.2 us -> 17.9 us  [group_all_gather(): partner = lax.ppermute(h, 'group', _z_flip(size))]
  transfers between devices with their start and end apart: 13 -> 13, of which waited for: 8 -> 8; matrix products, arithmetic and copies ran while one was open for 7% -> 7% of each run, Pallas kernels for 42% -> 44%
where the time goes in v5:
time: 412 us
  Pallas kernels  182 us (44%)
  waiting for transfers between devices  117 us (28%)
  local copies, waits for them, and re-layouts  48.6 us (12%)
  starting transfers between devices  37.3 us (9%)
  matrix products  22 us (5%)
  other arithmetic  5.1 us (1%)
    pallas_call x2, Pallas kernels, group_reduce_scatter(): pl.pallas_call(_rs_kernel, out_shape=jax.ShapeDtypeStruct((r // size, c),...  182 us
    all_to_all x2, waiting for transfers between devices, on_device(): lax.all_to_all(piece, 'dp', 0, 0, tiled=True).reshape(-1, width_here)  70.8 us
    gather x2, local copies, waits for them, and re-layouts, on_device(): jnp.take(proj_in, expert_list[:, slot], axis=0, mode='clip')  23.5 us
    ppermute x2, waiting for transfers between devices, group_all_gather(): from_down = lax.ppermute(pair, 'group', _y_shift(size, 1))  21 us
    ppermute x2, waiting for transfers between devices, group_all_gather(): partner = lax.ppermute(h, 'group', _z_flip(size))  17.9 us
    all_to_all x2, starting transfers between devices, on_device(): lax.all_to_all(piece, 'dp', 0, 0, tiled=True).reshape(-1, width_here)  15.2 us
    dot_general x2, matrix products, on_device(): jnp.dot(weight_in, tokens.T, preferred_element_type=jnp.float32)  12.5 us
    dot_general x2, matrix products, on_device(): lax.dot_general(hiddens[slot], weights_out[:, slot].reshape(-1, width_her...  9.45 us
  transfers between devices with their start and end apart: 13, of which 8 were waited for; matrix products, arithmetic and copies ran while one was open for 7% of the time, Pallas kernels for 44%

profile of v5, /device:TPU:24, one launch (start us, length us, event | category | flops | bytes accessed | tf_op | source)
XLA Modules:
  0.0 411.8 jit_solution(2561277423532505178)
XLA Ops:
  0.0 0.8 slice_bitcast_fusion
  0.8 11.8 %gather_fusion = bf16[32,32,2,896]{3,2,1,0:T(2,128)(2,1)} fusion(bf16[32,32,2,896]{3,2,1,0:T(2,128)(2,1)} %param.7, s32[1024]{0:T(1024)S(1)} %get-tuple-element.30), kind=kCustom, calls=%fused_computation | custom fusion | bytes 7340160 | tf_op jit(solution)/shard_map/jit(_take)/gather | solution.py:170
  12.6 8.9 %all-to-all-start = ((bf16[32,2,32,896]{3,1,2,0:T(2,128)(2,1)}), bf16[32,2,32,896]{3,1,2,0:T(2,128)(2,1)}, u32[]{:S(2)}, u32[]{:S(2)}) async-start(bf16[32,2,32,896]{3,1,2,0:T(2,128)(2,1)} %bitcast.71), calls=%async_computation | async-start | bytes 7340032 | tf_op jit(solution)/shard_map/all_to_all | solution.py:172
  21.5 11.8 %gather_fusion.1 = bf16[32,32,2,896]{3,2,1,0:T(2,128)(2,1)} fusion(bf16[32,32,2,896]{3,2,1,0:T(2,128)(2,1)} %param.7, s32[1024]{0:T(1024)S(1)} %get-tuple-element.29), kind=kCustom, calls=%fused_computation.1 | custom fusion | bytes 7340160 | tf_op jit(solution)/shard_map/jit(_take)/gather | solution.py:170
  33.2 70.8 %all-to-all-done = bf16[32,2,32,896]{3,1,2,0:T(2,128)(2,1)} async-done(((bf16[32,2,32,896]{3,1,2,0:T(2,128)(2,1)}), bf16[32,2,32,896]{3,1,2,0:T(2,128)(2,1)}, u32[]{:S(2)}, u32[]{:S(2)}) %all-to-all-start) | async-done | bytes 3670048 | tf_op jit(solution)/shard_map/all_to_all | solution.py:172
  104.0 2.7 copy.9
  106.7 6.3 %convolution_convert_fusion.1.x_ref = bf16[2048,1024]{1,0:T(8,128)(2,1)} fusion(bf16[2048,896]{1,0:T(8,128)(2,1)S(1)} %bitcast.72, bf16[1024,896]{1,0:T(8,128)(2,1)S(1)} %copy-done), kind=kOutput, calls=%fused_computation.4 | convolution fusion | flops 3760193536 | bytes 9699328 | tf_op jit(solution)/shard_map/dot_general | solution.py:175
  113.0 6.3 %all-to-all-start.1 = ((bf16[32,2,32,896]{3,1,2,0:T(2,128)(2,1)}), bf16[32,2,32,896]{3,1,2,0:T(2,128)(2,1)}, u32[]{:S(2)}, u32[]{:S(2)}) async-start(bf16[32,2,32,896]{3,1,2,0:T(2,128)(2,1)} %bitcast.70), calls=%async_computation.1 | async-start | bytes 7340032 | tf_op jit(solution)/shard_map/all_to_all | solution.py:172
  119.7 2.2 copy-done.2
  121.9 92.1 %shard_map.64 = f32[256,1024]{1,0:T(8,128)S(1)} custom-call(bf16[2048,1024]{1,0:T(8,128)(2,1)S(1)} %copy-done.2), custom_call_target="tpu_custom_call" | custom-call | tf_op jit(solution)/shard_map/pallas_call | solution.py:112
  214.1 0.2 fusion.5
  214.3 1.6 collective-permute-start
  215.9 10.4 %collective-permute-done = bf16[128,1024]{1,0:T(8,128)(2,1)S(1)} collective-permute-done((bf16[128,1024]{1,0:T(8,128)(2,1)S(1)}, bf16[128,1024]{1,0:T(8,128)(2,1)S(1)}, u32[]{:S(2)}, u32[]{:S(2)}) %collective-permute-start) | collective-permute-done | bytes 262176 | tf_op jit(solution)/shard_map/ppermute | solution.py:139
  226.3 1.6 broadcast.19.clone
  227.9 1.0 constant_dynamic-update-slice_fusion.5
  228.8 0.2 collective-permute-start.1
  229.1 1.8 collective-permute-start.2
  231.1 10.4 %collective-permute-done.1 = bf16[256,1024]{1,0:T(8,128)(2,1)S(1)} collective-permute-done((bf16[256,1024]{1,0:T(8,128)(2,1)S(1)}, bf16[256,1024]{1,0:T(8,128)(2,1)S(1)}, u32[]{:S(2)}, u32[]{:S(2)}) %collective-permute-start.1) | collective-permute-done | bytes 524320 | tf_op jit(solution)/shard_map/ppermute | solution.py:141
  241.4 0.7 slice.65
  242.1 1.5 collective-permute-start.3
  243.7 0.6 collective-permute-start.4
  244.3 4.3 %gather_fusion.2 = bf16[64,32,896]{2,1,0:T(8,128)(2,1)} fusion(bf16[32,32,896]{2,1,0:T(8,128)(2,1)} %param.8, s32[1024]{0:T(1024)S(1)} %pad_clamp_fusion), kind=kCustom, calls=%fused_computation.2 | custom fusion | bytes 7340288 | tf_op jit(solution)/shard_map/jit(_take)/gather | solution.py:165
  248.6 0.8 constant_dynamic-update-slice_fusion.4
  249.4 0.8 constant_dynamic-update-slice_fusion.3
  250.3 1.1 collective-permute-done.4
  251.3 1.8 maximum_dynamic-update-slice_fusion
  253.2 2.7 copy.10
  255.9 6.2 %convolution_convert_fusion.x_ref = bf16[2048,1024]{1,0:T(8,128)(2,1)} fusion(bf16[2048,896]{1,0:T(8,128)(2,1)S(1)} %bitcast.73, bf16[1024,896]{1,0:T(8,128)(2,1)S(1)} %copy-done), kind=kOutput, calls=%fused_computation.3 | convolution fusion | flops 3760193536 | bytes 9699328 | tf_op jit(solution)/shard_map/dot_general | solution.py:175
  262.1 6.7 %all-to-all-start.2 = ((bf16[32,2,32,896]{3,2,1,0:T(8,128)(2,1)}), bf16[32,2,32,896]{3,2,1,0:T(8,128)(2,1)}, u32[]{:S(2)}, u32[]{:S(2)}) async-start(bf16[32,2,32,896]{3,2,1,0:T(8,128)(2,1)} %bitcast.69), calls=%async_computation.2 | async-start | bytes 7340032 | tf_op jit(solution)/shard_map/all_to_all | solution.py:183
  268.9 2.2 copy-done.3
  271.1 89.8 %shard_map.65 = f32[256,1024]{1,0:T(8,128)S(1)} custom-call(bf16[2048,1024]{1,0:T(8,128)(2,1)S(1)} %copy-done.3), custom_call_target="tpu_custom_call" | custom-call | tf_op jit(solution)/shard_map/pallas_call | solution.py:112
  361.0 0.2 fusion
  361.1 4.5 %collective-permute-start.5 = (bf16[128,1024]{1,0:T(8,128)(2,1)S(1)}, bf16[128,1024]{1,0:T(8,128)(2,1)S(1)}, u32[]{:S(2)}, u32[]{:S(2)}) collective-permute-start(bf16[128,1024]{1,0:T(8,128)(2,1)S(1)} %fusion), channel_id=1, source_target_pairs={{0,1},{1,0},{2,3},{3,2},{4,5},{5,4},{6,7},{7,6},{8,9},{9,8},{10,11... | collective-permute-start | bytes 786440 | tf_op jit(solution)/shard_map/ppermute | solution.py:139
  365.7 7.5 %collective-permute-done.5 = bf16[128,1024]{1,0:T(8,128)(2,1)S(1)} collective-permute-done((bf16[128,1024]{1,0:T(8,128)(2,1)S(1)}, bf16[128,1024]{1,0:T(8,128)(2,1)S(1)}, u32[]{:S(2)}, u32[]{:S(2)}) %collective-permute-start.5) | collective-permute-done | bytes 262176 | tf_op jit(solution)/shard_map/ppermute | solution.py:139
  373.2 1.6 broadcast.19
  374.8 1.0 constant_dynamic-update-slice_fusion.2
  375.7 1.6 collective-permute-start.6
  377.4 0.4 collective-permute-start.7
  377.8 10.7 %collective-permute-done.6 = bf16[256,1024]{1,0:T(8,128)(2,1)S(1)} collective-permute-done((bf16[256,1024]{1,0:T(8,128)(2,1)S(1)}, bf16[256,1024]{1,0:T(8,128)(2,1)S(1)}, u32[]{:S(2)}, u32[]{:S(2)}) %collective-permute-start.6) | collective-permute-done | bytes 524320 | tf_op jit(solution)/shard_map/ppermute | solution.py:141
  388.5 2.9 collective-permute-start.8
  391.5 0.8 constant_dynamic-update-slice_fusion.1
  392.4 0.8 constant_dynamic-update-slice_fusion
  393.2 2.1 collective-permute-done.8
  395.3 3.8 collective-permute-done.9
  399.1 0.8 maximum_dynamic-update-slice_fusion.1
  399.9 2.4 fusion.10
  402.3 4.0 fusion.14
  406.3 5.5 %add_convert_fusion = bf16[1024,896]{1,0:T(8,128)(2,1)} fusion(f32[1024,896]{1,0:T(8,128)S(1)} %fusion.14, bf16[1024,1024]{1,0:T(8,128)(2,1)} %maximum_dynamic-update-slice_fusion.1, bf16[1024,896]{1,0:T(8,128)(2,1)S(1)} %bitcast.74), kind=kOutput, calls=%fused_computation.5 | convolution fusion | flops 1880883200 | bytes 9437184 | tf_op jit(solution)/shard_map/dot_general | solution.py:187
  (31 shorter events, 0.8 us)
Async XLA Ops:
  0.0 106.7 %copy-start = (bf16[1024,896]{1,0:T(8,128)(2,1)S(1)}, bf16[1024,896]{1,0:T(8,128)(2,1)}, u32[]{:S(2)}) copy-start(bf16[1024,896]{1,0:T(8,128)(2,1)} %param.6) | copy-start | bytes 5505028
  12.6 91.4 %all-to-all-start = ((bf16[32,2,32,896]{3,1,2,0:T(2,128)(2,1)}), bf16[32,2,32,896]{3,1,2,0:T(2,128)(2,1)}, u32[]{:S(2)}, u32[]{:S(2)}) async-start(bf16[32,2,32,896]{3,1,2,0:T(2,128)(2,1)} %bitcast.71), calls=%async_computation | async-start | bytes 7340032 | tf_op jit(solution)/shard_map/all_to_all | solution.py:172
  113.0 6.4 %copy-start.5 = (s32[32,2,8]{0,2,1:T(8,128)S(1)}, s32[32,2,8]{0,2,1:T(8,128)}, u32[]{:S(2)}) copy-start(s32[32,2,8]{0,2,1:T(8,128)} %param.10) | copy-start | bytes 6148
  113.0 6.6 %copy-start.4 = (f32[1024,2]{0,1:T(2,128)S(1)}, f32[1024,2]{0,1:T(2,128)}, u32[]{:S(2)}) copy-start(f32[1024,2]{0,1:T(2,128)} %param.11) | copy-start | bytes 24580
  113.0 140.1 %all-to-all-start.1 = ((bf16[32,2,32,896]{3,1,2,0:T(2,128)(2,1)}), bf16[32,2,32,896]{3,1,2,0:T(2,128)(2,1)}, u32[]{:S(2)}, u32[]{:S(2)}) async-start(bf16[32,2,32,896]{3,1,2,0:T(2,128)(2,1)} %bitcast.70), calls=%async_computation.1 | async-start | bytes 7340032 | tf_op jit(solution)/shard_map/all_to_all | solution.py:172
  119.7 2.2 copy-start.2
  214.3 16.6 %copy-start.6 = (s32[32,2]{0,1:T(2,128)S(1)}, s32[32,2]{0,1:T(2,128)}, u32[]{:S(2)}) copy-start(s32[32,2]{0,1:T(2,128)} %param.9) | copy-start | bytes 772
  214.3 12.0 %collective-permute-start = (bf16[128,1024]{1,0:T(8,128)(2,1)S(1)}, bf16[128,1024]{1,0:T(8,128)(2,1)S(1)}, u32[]{:S(2)}, u32[]{:S(2)}) collective-permute-start(bf16[128,1024]{1,0:T(8,128)(2,1)S(1)} %fusion.5), channel_id=1, source_target_pairs={{0,1},{1,0},{2,3},{3,2},{4,5},{5,4},{6,7},{7,6},{8,9},{9,8},{10,11... | collective-permute-start | bytes 786440 | tf_op jit(solution)/shard_map/ppermute | solution.py:139
  228.8 12.6 %collective-permute-start.1 = (bf16[256,1024]{1,0:T(8,128)(2,1)S(1)}, bf16[256,1024]{1,0:T(8,128)(2,1)S(1)}, u32[]{:S(2)}, u32[]{:S(2)}) collective-permute-start(bf16[256,1024]{1,0:T(8,128)(2,1)S(1)} %get-tuple-element.18), channel_id=1, source_target_pairs={{0,2},{1,3},{2,4},{3,5},{4,6},{5,7},{6,0},{7,1},{8,10},{9,11},{10,... | collective-permute-start | bytes 1572872 | tf_op jit(solution)/shard_map/ppermute | solution.py:141
  229.1 14.6 %collective-permute-start.2 = (bf16[256,1024]{1,0:T(8,128)(2,1)S(1)}, bf16[256,1024]{1,0:T(8,128)(2,1)S(1)}, u32[]{:S(2)}, u32[]{:S(2)}) collective-permute-start(bf16[256,1024]{1,0:T(8,128)(2,1)S(1)} %get-tuple-element.18), channel_id=1, source_target_pairs={{0,6},{1,7},{2,0},{3,1},{4,2},{5,3},{6,4},{7,5},{8,14},{9,15},{10,... | collective-permute-start | bytes 1572872 | tf_op jit(solution)/shard_map/ppermute | solution.py:142
  242.1 8.1 %collective-permute-start.3 = (bf16[128,1024]{1,0:T(8,128)(2,1)}, bf16[128,1024]{1,0:T(8,128)(2,1)}, u32[]{:S(2)}, u32[]{:S(2)}) collective-permute-start(bf16[128,1024]{1,0:T(8,128)(2,1)} %slice.65), channel_id=1, source_target_pairs={{0,2},{1,3},{2,4},{3,5},{4,6},{5,7},{6,0},{7,1},{8,10},{9,11},{10,... | collective-permute-start | bytes 786440 | tf_op jit(solution)/shard_map/ppermute | solution.py:143
  243.7 7.7 %collective-permute-start.4 = (bf16[128,1024]{1,0:T(8,128)(2,1)S(1)}, bf16[128,1024]{1,0:T(8,128)(2,1)S(1)}, u32[]{:S(2)}, u32[]{:S(2)}) collective-permute-start(bf16[128,1024]{1,0:T(8,128)(2,1)S(1)} %slice.66), channel_id=1, source_target_pairs={{0,6},{1,7},{2,0},{3,1},{4,2},{5,3},{6,4},{7,5},{8,14},{9,15},{10,... | collective-permute-start | bytes 786440 | tf_op jit(solution)/shard_map/ppermute | solution.py:144
  262.1 137.8 %all-to-all-start.2 = ((bf16[32,2,32,896]{3,2,1,0:T(8,128)(2,1)}), bf16[32,2,32,896]{3,2,1,0:T(8,128)(2,1)}, u32[]{:S(2)}, u32[]{:S(2)}) async-start(bf16[32,2,32,896]{3,2,1,0:T(8,128)(2,1)} %bitcast.69), calls=%async_computation.2 | async-start | bytes 7340032 | tf_op jit(solution)/shard_map/all_to_all | solution.py:183
  268.9 2.2 copy-start.3
  361.1 12.1 %collective-permute-start.5 = (bf16[128,1024]{1,0:T(8,128)(2,1)S(1)}, bf16[128,1024]{1,0:T(8,128)(2,1)S(1)}, u32[]{:S(2)}, u32[]{:S(2)}) collective-permute-start(bf16[128,1024]{1,0:T(8,128)(2,1)S(1)} %fusion), channel_id=1, source_target_pairs={{0,1},{1,0},{2,3},{3,2},{4,5},{5,4},{6,7},{7,6},{8,9},{9,8},{10,11... | collective-permute-start | bytes 786440 | tf_op jit(solution)/shard_map/ppermute | solution.py:139
  375.7 12.7 %collective-permute-start.6 = (bf16[256,1024]{1,0:T(8,128)(2,1)S(1)}, bf16[256,1024]{1,0:T(8,128)(2,1)S(1)}, u32[]{:S(2)}, u32[]{:S(2)}) collective-permute-start(bf16[256,1024]{1,0:T(8,128)(2,1)S(1)} %get-tuple-element.16), channel_id=1, source_target_pairs={{0,2},{1,3},{2,4},{3,5},{4,6},{5,7},{6,0},{7,1},{8,10},{9,11},{10,... | collective-permute-start | bytes 1572872 | tf_op jit(solution)/shard_map/ppermute | solution.py:141
  377.4 14.0 %collective-permute-start.7 = (bf16[256,1024]{1,0:T(8,128)(2,1)S(1)}, bf16[256,1024]{1,0:T(8,128)(2,1)S(1)}, u32[]{:S(2)}, u32[]{:S(2)}) collective-permute-start(bf16[256,1024]{1,0:T(8,128)(2,1)S(1)} %get-tuple-element.16), channel_id=1, source_target_pairs={{0,6},{1,7},{2,0},{3,1},{4,2},{5,3},{6,4},{7,5},{8,14},{9,15},{10,... | collective-permute-start | bytes 1572872 | tf_op jit(solution)/shard_map/ppermute | solution.py:142
  388.5 6.8 %collective-permute-start.8 = (bf16[128,1024]{1,0:T(8,128)(2,1)S(1)}, bf16[128,1024]{1,0:T(8,128)(2,1)S(1)}, u32[]{:S(2)}, u32[]{:S(2)}) collective-permute-start(bf16[128,1024]{1,0:T(8,128)(2,1)S(1)} %slice.71), channel_id=1, source_target_pairs={{0,2},{1,3},{2,4},{3,5},{4,6},{5,7},{6,0},{7,1},{8,10},{9,11},{10,... | collective-permute-start | bytes 786440 | tf_op jit(solution)/shard_map/ppermute | solution.py:143
  391.4 7.7 %collective-permute-start.9 = (bf16[128,1024]{1,0:T(8,128)(2,1)S(1)}, bf16[128,1024]{1,0:T(8,128)(2,1)S(1)}, u32[]{:S(2)}, u32[]{:S(2)}) collective-permute-start(bf16[128,1024]{1,0:T(8,128)(2,1)S(1)} %slice.72), channel_id=1, source_target_pairs={{0,6},{1,7},{2,0},{3,1},{4,2},{5,3},{6,4},{7,5},{8,14},{9,15},{10,... | collective-permute-start | bytes 786440 | tf_op jit(solution)/shard_map/ppermute | solution.py:144
  406.3 5.5 %copy-start.1 = (bf16[1024,896]{1,0:T(8,128)(2,1)S(1)}, bf16[1024,896]{1,0:T(8,128)(2,1)}, u32[]{:S(2)}) copy-start(bf16[1024,896]{1,0:T(8,128)(2,1)} %param.6) | copy-start | bytes 5505028

commit v6 on v2

--- a/solution.py
+++ b/solution.py
@@ -7,19 +7,6 @@
 
 
 Y_PARTS = 4
-
-
-def _perm(size, fn):
-    return [(j, fn(j)) for j in range(size)]
-
-
-def _y_shift(size, dy):
-    z_parts = size // Y_PARTS
-    return _perm(size, lambda j: ((j // z_parts + dy) % Y_PARTS) * z_parts + j % z_parts)
-
-
-def _z_flip(size):
-    return _perm(size, lambda j: j ^ 1)
 
 
 def _rs_kernel(x_ref, out_ref, ybuf, fwd, relay, own, zsend, zrecv, send_sem, recv_sem, local_sem):
@@ -114,22 +101,84 @@
     )(x)
 
 
-def group_all_gather(h):
-    size = lax.axis_size("group")
+def _ag_kernel(h_ref, out_ref, pbuf, ybuf, fbuf, send_sem, recv_sem):
+    size = lax.axis_size("group")
+    z_parts = size // Y_PARTS
     j = lax.axis_index("group")
-    y, zh = j // 2, j % 2
-    n = h.shape[0]
-    partner = lax.ppermute(h, "group", _z_flip(size))
-    pair = jnp.where(zh == 0, jnp.concatenate([h, partner]), jnp.concatenate([partner, h]))
-    from_down = lax.ppermute(pair, "group", _y_shift(size, 1))
-    from_up = lax.ppermute(pair, "group", _y_shift(size, -1))
-    far_a = lax.ppermute(from_down[:n], "group", _y_shift(size, 1))
-    far_b = lax.ppermute(from_up[n:], "group", _y_shift(size, -1))
-    out = jnp.zeros((Y_PARTS * 2 * n,) + h.shape[1:], h.dtype)
-    for dy, piece in ((0, pair), (-1, from_down), (1, from_up),
-                      (2, jnp.concatenate([far_a, far_b]))):
-        out = lax.dynamic_update_slice_in_dim(out, piece, ((y + dy) % Y_PARTS) * 2 * n, 0)
-    return out
+    y, zh = j // z_parts, j % z_parts
+    n = h_ref.shape[0]
+    mesh_id = pl.DeviceIdType.MESH
+
+    def peer(dy):
+        return {"group": ((y + dy) % Y_PARTS) * z_parts + zh}
+
+    partner = {"group": y * z_parts + (1 - zh)}
+    up, down = peer(1), peer(Y_PARTS - 1)
+    barrier = pltpu.get_barrier_semaphore()
+    for dev in (up, down, partner):
+        pl.semaphore_signal(barrier, inc=1, device_id=dev, device_id_type=mesh_id)
+    pl.semaphore_wait(barrier, 3)
+
+    def remote(src, dst, k, dev):
+        c = pltpu.make_async_remote_copy(
+            src_ref=src, dst_ref=dst, send_sem=send_sem.at[k], recv_sem=recv_sem.at[k],
+            device_id=dev, device_id_type=mesh_id,
+        )
+        c.start()
+        return c
+
+    own_lo = pl.multiple_of(zh * n, n)
+    other_lo = pl.multiple_of((1 - zh) * n, n)
+    zc = remote(h_ref, pbuf, 0, partner)
+    first = [
+        remote(h_ref, ybuf.at[0, pl.ds(own_lo, n)], 1, up),
+        remote(h_ref, ybuf.at[1, pl.ds(own_lo, n)], 2, down),
+    ]
+    zc.wait()
+    first += [
+        remote(pbuf, ybuf.at[0, pl.ds(other_lo, n)], 3, up),
+        remote(pbuf, ybuf.at[1, pl.ds(other_lo, n)], 4, down),
+    ]
+    for c in first:
+        c.wait()
+    second = [
+        remote(ybuf.at[0, pl.ds(0, n)], fbuf.at[0], 5, up),
+        remote(ybuf.at[1, pl.ds(n, n)], fbuf.at[1], 6, down),
+    ]
+    pair = 2 * n
+
+    def at(dy):
+        return pl.multiple_of(((y + dy) % Y_PARTS) * pair, pair)
+
+    out_ref[pl.ds(at(0) + own_lo, n), :] = h_ref[...]
+    out_ref[pl.ds(at(0) + other_lo, n), :] = pbuf[...]
+    out_ref[pl.ds(at(-1), pair), :] = ybuf[0]
+    out_ref[pl.ds(at(1), pair), :] = ybuf[1]
+    for c in second:
+        c.wait()
+    out_ref[pl.ds(at(2), n), :] = fbuf[0]
+    out_ref[pl.ds(at(2) + n, n), :] = fbuf[1]
+
+
+def group_all_gather(h, collective_id=0):
+    size = lax.axis_size("group")
+    n, c = h.shape
+    return pl.pallas_call(
+        _ag_kernel,
+        out_shape=jax.ShapeDtypeStruct((size * n, c), h.dtype),
+        in_specs=[pl.BlockSpec(memory_space=pltpu.VMEM)],
+        out_specs=pl.BlockSpec(memory_space=pltpu.VMEM),
+        scratch_shapes=[
+            pltpu.VMEM((n, c), h.dtype),
+            pltpu.VMEM((2, 2 * n, c), h.dtype),
+            pltpu.VMEM((2, n, c), h.dtype),
+            pltpu.SemaphoreType.DMA((7,)),
+            pltpu.SemaphoreType.DMA((7,)),
+        ],
+        compiler_params=pltpu.CompilerParams(
+            collective_id=collective_id, has_side_effects=True, vmem_limit_bytes=32 * 1024 * 1024
+        ),
+    )(h)
 
 
 def on_device(tokens, proj_in, proj_out, expert_list, block_pattern, route_weight):
@@ -160,7 +209,7 @@
         shares = group_reduce_scatter(partial_here, collective_id=slot)
         shares = shares.reshape(n_dp // group_size, 2, ff_here, row_count)
         hidden = (token_scale[slot] * jax.nn.silu(shares[:, 0]) * shares[:, 1]).astype(jnp.bfloat16)
-        hiddens.append(group_all_gather(hidden.reshape(-1, row_count)))
+        hiddens.append(group_all_gather(hidden.reshape(-1, row_count), collective_id=slots + slot))
         pending = partial_here
     pending, send_out = lax.optimization_barrier((pending, send_out))
     weights_out = lax.all_to_all(send_out, "dp", 0, 0, tiled=True)

time: 410 us -> 387 us (0.944)
  Pallas kernels: 171 us -> 228 us
  waiting for transfers between devices: 125 us -> 70.9 us
  starting transfers between devices: 36.6 us -> 24.3 us
  other arithmetic: 5.1 us -> 0.5 us
  local copies, waits for them, and re-layouts: 48.6 us -> 44.1 us
    pallas_call x0 -> x2, Pallas kernels: none -> 59.7 us  [group_all_gather(): pl.pallas_call(_ag_kernel, out_shape=jax.ShapeDtypeStruct((size * n, c),...]
    ppermute x10 -> x0, waiting for transfers between devices: 54.4 us -> none  [the longest x2 23.2 us: group_all_gather(): partner = lax.ppermute(h, 'group', _z_flip(size))]
    ppermute x10 -> x0, starting transfers between devices: 14.6 us -> none  [the longest x2 5.62 us: group_all_gather(): partner = lax.ppermute(h, 'group', _z_flip(size))]
    dynamic_update_slice x4 -> x0, other arithmetic: 4.6 us -> none  [group_all_gather(): lax.dynamic_update_slice_in_dim(out, piece, (y + dy) % Y_PARTS * 2 * n, 0)]
  transfers between devices with their start and end apart: 13 -> 3, of which waited for: 8 -> 1; matrix products, arithmetic and copies ran while one was open for 7% -> 4% of each run, Pallas kernels for 42% -> 59%
where the time goes in v6:
time: 387 us; the launch traced here: 386 us
  Pallas kernels  228 us (59%)
  waiting for transfers between devices  70.9 us (18%)
  local copies, waits for them, and re-layouts  44.1 us (11%)
  starting transfers between devices  24.3 us (6%)
  matrix products  18.6 us (5%)
    pallas_call x2, Pallas kernels, group_reduce_scatter(): pl.pallas_call(_rs_kernel, out_shape=jax.ShapeDtypeStruct((r // size, c),...  168 us
    all_to_all x2, waiting for transfers between devices, on_device(): lax.all_to_all(piece, 'dp', 0, 0, tiled=True).reshape(-1, width_here)  70.9 us
    pallas_call x2, Pallas kernels, group_all_gather(): pl.pallas_call(_ag_kernel, out_shape=jax.ShapeDtypeStruct((size * n, c),...  59.7 us
    gather x2, local copies, waits for them, and re-layouts, on_device(): jnp.take(proj_in, expert_list[:, slot], axis=0, mode='clip')  23.3 us
    all_to_all x2, starting transfers between devices, on_device(): lax.all_to_all(piece, 'dp', 0, 0, tiled=True).reshape(-1, width_here)  15.2 us
    dot_general x2, matrix products, on_device(): jnp.dot(weight_in, tokens.T, preferred_element_type=jnp.float32)  12.6 us
    all_to_all x1, starting transfers between devices, on_device(): weights_out = lax.all_to_all(send_out, 'dp', 0, 0, tiled=True)  9.09 us
  transfers between devices with their start and end apart: 3, of which 1 were waited for; matrix products, arithmetic and copies ran while one was open for 4% of the time, Pallas kernels for 59%

profile of v6, /device:TPU:24, one launch (start us, length us, event | category | flops | bytes accessed | tf_op | source)
XLA Modules:
  0.0 386.2 jit_solution(13249193976120874394)
XLA Ops:
  0.0 0.0 copy-start
  0.0 0.8 slice_bitcast_fusion
  0.8 11.7 %gather_fusion = bf16[32,32,2,896]{3,2,1,0:T(2,128)(2,1)} fusion(bf16[32,32,2,896]{3,2,1,0:T(2,128)(2,1)} %param.7, s32[1024]{0:T(1024)S(1)} %get-tuple-element.26), kind=kCustom, calls=%fused_computation | custom fusion | bytes 7340160 | tf_op jit(solution)/shard_map/jit(_take)/gather | solution.py:202
  12.5 8.9 %all-to-all-start = ((bf16[32,2,32,896]{3,1,2,0:T(2,128)(2,1)}), bf16[32,2,32,896]{3,1,2,0:T(2,128)(2,1)}, u32[]{:S(2)}, u32[]{:S(2)}) async-start(bf16[32,2,32,896]{3,1,2,0:T(2,128)(2,1)} %bitcast.79), calls=%async_computation | async-start | bytes 7340032 | tf_op jit(solution)/shard_map/all_to_all | solution.py:204
  21.4 11.7 %gather_fusion.1 = bf16[32,32,2,896]{3,2,1,0:T(2,128)(2,1)} fusion(bf16[32,32,2,896]{3,2,1,0:T(2,128)(2,1)} %param.7, s32[1024]{0:T(1024)S(1)} %get-tuple-element.25), kind=kCustom, calls=%fused_computation.1 | custom fusion | bytes 7340160 | tf_op jit(solution)/shard_map/jit(_take)/gather | solution.py:202
  33.0 70.9 %all-to-all-done = bf16[32,2,32,896]{3,1,2,0:T(2,128)(2,1)} async-done(((bf16[32,2,32,896]{3,1,2,0:T(2,128)(2,1)}), bf16[32,2,32,896]{3,1,2,0:T(2,128)(2,1)}, u32[]{:S(2)}, u32[]{:S(2)}) %all-to-all-start) | async-done | bytes 3670048 | tf_op jit(solution)/shard_map/all_to_all | solution.py:204
  103.9 2.7 copy.17
  106.6 0.0 copy-done
  106.6 6.3 %convolution_convert_fusion.1.x_ref = bf16[2048,1024]{1,0:T(8,128)(2,1)} fusion(bf16[2048,896]{1,0:T(8,128)(2,1)S(1)} %bitcast.80, bf16[1024,896]{1,0:T(8,128)(2,1)S(1)} %copy-done), kind=kOutput, calls=%fused_computation.4 | convolution fusion | flops 3760193536 | bytes 9699328 | tf_op jit(solution)/shard_map/dot_general | solution.py:207
  112.9 0.0 copy-start.9
  112.9 6.3 %all-to-all-start.1 = ((bf16[32,2,32,896]{3,1,2,0:T(2,128)(2,1)}), bf16[32,2,32,896]{3,1,2,0:T(2,128)(2,1)}, u32[]{:S(2)}, u32[]{:S(2)}) async-start(bf16[32,2,32,896]{3,1,2,0:T(2,128)(2,1)} %bitcast.78), calls=%async_computation.1 | async-start | bytes 7340032 | tf_op jit(solution)/shard_map/all_to_all | solution.py:204
  119.3 0.0 copy-done.9
  119.3 0.1 copy.21
  119.4 0.1 reshape.45
  119.5 0.0 copy-start.8
  119.5 0.0 copy-start.7
  119.5 4.2 %gather_fusion.2 = bf16[64,32,896]{2,1,0:T(8,128)(2,1)} fusion(bf16[32,32,896]{2,1,0:T(8,128)(2,1)} %param.8, s32[1024]{0:T(1024)S(1)} %pad_clamp_fusion), kind=kCustom, calls=%fused_computation.2 | custom fusion | bytes 7340288 | tf_op jit(solution)/shard_map/jit(_take)/gather | solution.py:197
  123.8 0.0 copy-done.8
  123.8 0.2 convert_reduce_fusion
  123.9 0.1 broadcast_bitcast_fusion
  124.0 0.0 copy-done.7
  124.0 0.0 copy-start.1
  124.0 2.2 copy-done.1
  126.2 82.2 %shard_map.64 = f32[256,1024]{1,0:T(8,128)S(1)} custom-call(bf16[2048,1024]{1,0:T(8,128)(2,1)S(1)} %copy-done.1), custom_call_target="tpu_custom_call" | custom-call | tf_op jit(solution)/shard_map/pallas_call | solution.py:82
  208.4 0.1 fusion.12
  208.5 0.2 fusion.5.h_ref
  208.7 29.3 %shard_map.65 = bf16[1024,1024]{1,0:T(8,128)(2,1)S(1)} custom-call(bf16[128,1024]{1,0:T(8,128)(2,1)S(1)} %fusion.5.h_ref), custom_call_target="tpu_custom_call" | custom-call | tf_op jit(solution)/shard_map/pallas_call | solution.py:166
  238.0 0.0 copy-start.3
  238.0 1.3 copy-done.3
  239.3 0.0 all-to-all-done.1
  239.3 2.7 copy.18
  242.0 6.3 %convolution_convert_fusion.x_ref = bf16[2048,1024]{1,0:T(8,128)(2,1)} fusion(bf16[2048,896]{1,0:T(8,128)(2,1)S(1)} %bitcast.81, bf16[1024,896]{1,0:T(8,128)(2,1)S(1)} %copy-done), kind=kOutput, calls=%fused_computation.3 | convolution fusion | flops 3760193536 | bytes 9699328 | tf_op jit(solution)/shard_map/dot_general | solution.py:207
  248.3 9.1 %all-to-all-start.2 = ((bf16[32,2,32,896]{3,2,1,0:T(8,128)(2,1)}), bf16[32,2,32,896]{3,2,1,0:T(8,128)(2,1)}, u32[]{:S(2)}, u32[]{:S(2)}) async-start(bf16[32,2,32,896]{3,2,1,0:T(8,128)(2,1)} %bitcast.77), calls=%async_computation.2 | async-start | bytes 7340032 | tf_op jit(solution)/shard_map/all_to_all | solution.py:215
  257.4 0.0 copy-start.2
  257.4 2.2 copy-done.2
  259.6 85.7 %shard_map.66 = f32[256,1024]{1,0:T(8,128)S(1)} custom-call(bf16[2048,1024]{1,0:T(8,128)(2,1)S(1)} %copy-done.2), custom_call_target="tpu_custom_call" | custom-call | tf_op jit(solution)/shard_map/pallas_call | solution.py:82
  345.3 0.1 fusion.11
  345.4 0.2 fusion.h_ref
  345.6 30.4 %shard_map.67 = bf16[1024,1024]{1,0:T(8,128)(2,1)S(1)} custom-call(bf16[128,1024]{1,0:T(8,128)(2,1)S(1)} %fusion.h_ref), custom_call_target="tpu_custom_call" | custom-call | tf_op jit(solution)/shard_map/pallas_call | solution.py:166
  376.0 0.0 copy-start.5
  376.0 1.4 copy-done.5
  377.4 0.0 all-to-all-done.2
  377.4 0.0 copy-start.4
  377.4 2.5 fusion.10
  379.9 0.2 copy-done.4
  380.1 2.4 fusion.14
  382.5 0.0 copy-done.6
  382.5 3.7 add_convert_fusion
  (5 shorter events, 0.0 us)
Async XLA Ops:
  0.0 106.6 %copy-start = (bf16[1024,896]{1,0:T(8,128)(2,1)S(1)}, bf16[1024,896]{1,0:T(8,128)(2,1)}, u32[]{:S(2)}) copy-start(bf16[1024,896]{1,0:T(8,128)(2,1)} %param.6) | copy-start | bytes 5505028
  12.5 91.4 %all-to-all-start = ((bf16[32,2,32,896]{3,1,2,0:T(2,128)(2,1)}), bf16[32,2,32,896]{3,1,2,0:T(2,128)(2,1)}, u32[]{:S(2)}, u32[]{:S(2)}) async-start(bf16[32,2,32,896]{3,1,2,0:T(2,128)(2,1)} %bitcast.79), calls=%async_computation | async-start | bytes 7340032 | tf_op jit(solution)/shard_map/all_to_all | solution.py:204
  112.9 6.4 %copy-start.9 = (s32[32,2]{0,1:T(2,128)S(1)}, s32[32,2]{0,1:T(2,128)}, u32[]{:S(2)}) copy-start(s32[32,2]{0,1:T(2,128)} %param.9) | copy-start | bytes 772
  112.9 126.4 %all-to-all-start.1 = ((bf16[32,2,32,896]{3,1,2,0:T(2,128)(2,1)}), bf16[32,2,32,896]{3,1,2,0:T(2,128)(2,1)}, u32[]{:S(2)}, u32[]{:S(2)}) async-start(bf16[32,2,32,896]{3,1,2,0:T(2,128)(2,1)} %bitcast.78), calls=%async_computation.1 | async-start | bytes 7340032 | tf_op jit(solution)/shard_map/all_to_all | solution.py:204
  119.5 4.3 %copy-start.8 = (s32[32,2,8]{0,2,1:T(8,128)S(1)}, s32[32,2,8]{0,2,1:T(8,128)}, u32[]{:S(2)}) copy-start(s32[32,2,8]{0,2,1:T(8,128)} %param.10) | copy-start | bytes 6148
  119.5 4.5 %copy-start.7 = (f32[1024,2]{0,1:T(2,128)S(1)}, f32[1024,2]{0,1:T(2,128)}, u32[]{:S(2)}) copy-start(f32[1024,2]{0,1:T(2,128)} %param.11) | copy-start | bytes 24580
  124.0 2.2 copy-start.1
  238.0 1.3 copy-start.3
  248.3 129.1 %all-to-all-start.2 = ((bf16[32,2,32,896]{3,2,1,0:T(8,128)(2,1)}), bf16[32,2,32,896]{3,2,1,0:T(8,128)(2,1)}, u32[]{:S(2)}, u32[]{:S(2)}) async-start(bf16[32,2,32,896]{3,2,1,0:T(8,128)(2,1)} %bitcast.77), calls=%async_computation.2 | async-start | bytes 7340032 | tf_op jit(solution)/shard_map/all_to_all | solution.py:215
  257.4 2.2 copy-start.2
  376.0 1.4 copy-start.5
  377.4 2.7 copy-start.4
  380.1 2.4 copy-start.6

commit v7 on v6

--- a/solution.py
+++ b/solution.py
@@ -199,7 +199,7 @@
     hiddens = []
     pending = tokens
     for slot in range(slots):
-        piece = jnp.take(proj_in, expert_list[:, slot], axis=0, mode="clip").transpose(0, 2, 1, 3)
+        piece = jnp.take(proj_in, expert_list[:, slot], axis=0, mode="clip")
         pending, piece = lax.optimization_barrier((pending, piece))
         weight_in = lax.all_to_all(piece, "dp", 0, 0, tiled=True).reshape(-1, width_here)
         if hiddens:
@@ -207,8 +207,8 @@
         partial_here = jnp.dot(weight_in, tokens.T, preferred_element_type=jnp.float32)
         partial_here = partial_here.astype(jnp.bfloat16)
         shares = group_reduce_scatter(partial_here, collective_id=slot)
-        shares = shares.reshape(n_dp // group_size, 2, ff_here, row_count)
-        hidden = (token_scale[slot] * jax.nn.silu(shares[:, 0]) * shares[:, 1]).astype(jnp.bfloat16)
+        shares = shares.reshape(n_dp // group_size, ff_here, 2, row_count)
+        hidden = (token_scale[slot] * jax.nn.silu(shares[:, :, 0]) * shares[:, :, 1]).astype(jnp.bfloat16)
         hiddens.append(group_all_gather(hidden.reshape(-1, row_count), collective_id=slots + slot))
         pending = partial_here
     pending, send_out = lax.optimization_barrier((pending, send_out))

time: 387 us -> 410 us (1.059)
  local copies, waits for them, and re-layouts: 44.1 us -> 61.8 us
  Pallas kernels: 228 us -> 221 us
  starting transfers between devices: 24.3 us -> 30.3 us
    reshape x0 -> x4, local copies, waits for them, and re-layouts: none -> 19.6 us  [the longest x2 17.4 us: on_device(): lax.all_to_all(piece, 'dp', 0, 0, tiled=True).reshape(-1, width_here)]
    all_to_all x1, starting transfers between devices: 9.09 us -> 14.8 us  [on_device(): weights_out = lax.all_to_all(send_out, 'dp', 0, 0, tiled=True)]
    pallas_call x2, Pallas kernels: 59.7 us -> 54 us  [group_all_gather(): pl.pallas_call(_ag_kernel, out_shape=jax.ShapeDtypeStruct((size * n, c),...]
    all_to_all x2 -> x0, local copies, waits for them, and re-layouts: 5.44 us -> none  [on_device(): lax.all_to_all(piece, 'dp', 0, 0, tiled=True).reshape(-1, width_here)]
  transfers between devices with their start and end apart: 3 -> 3, of which waited for: 1 -> 1; matrix products, arithmetic and copies ran while one was open for 4% -> 6% of each run, Pallas kernels for 59% -> 54%
where the time goes in v7:
time: 410 us; the launch traced here: 407 us
  Pallas kernels  221 us (54%)
  waiting for transfers between devices  70.7 us (17%)
  local copies, waits for them, and re-layouts  61.8 us (15%)
  starting transfers between devices  30.3 us (7%)
  matrix products  22.5 us (5%)
    pallas_call x2, Pallas kernels, group_reduce_scatter(): pl.pallas_call(_rs_kernel, out_shape=jax.ShapeDtypeStruct((r // size, c),...  167 us
    all_to_all x2, waiting for transfers between devices, on_device(): lax.all_to_all(piece, 'dp', 0, 0, tiled=True).reshape(-1, width_here)  70.7 us
    pallas_call x2, Pallas kernels, group_all_gather(): pl.pallas_call(_ag_kernel, out_shape=jax.ShapeDtypeStruct((size * n, c),...  54 us
    gather x2, local copies, waits for them, and re-layouts, on_device(): piece = jnp.take(proj_in, expert_list[:, slot], axis=0, mode='clip')  23.3 us
    reshape x2, local copies, waits for them, and re-layouts, on_device(): lax.all_to_all(piece, 'dp', 0, 0, tiled=True).reshape(-1, width_here)  17.4 us
    dot_general x2, matrix products, on_device(): jnp.dot(weight_in, tokens.T, preferred_element_type=jnp.float32)  16.4 us
    all_to_all x2, starting transfers between devices, on_device(): lax.all_to_all(piece, 'dp', 0, 0, tiled=True).reshape(-1, width_here)  15.4 us
    all_to_all x1, starting transfers between devices, on_device(): weights_out = lax.all_to_all(send_out, 'dp', 0, 0, tiled=True)  14.8 us
  transfers between devices with their start and end apart: 3, of which 1 were waited for; matrix products, arithmetic and copies ran while one was open for 6% of the time, Pallas kernels for 54%

profile of v7, /device:TPU:24, one launch (start us, length us, event | category | flops | bytes accessed | tf_op | source)
XLA Modules:
  0.0 407.1 jit_solution(7356474524699924445)
XLA Ops:
  0.0 0.0 copy-start
  0.0 0.8 slice_bitcast_fusion
  0.8 11.7 %gather_fusion = bf16[32,32,2,896]{3,2,1,0:T(2,128)(2,1)} fusion(bf16[32,32,2,896]{3,2,1,0:T(2,128)(2,1)} %param.7, s32[1024]{0:T(1024)S(1)} %pad_clamp_fusion.2), kind=kCustom, calls=%fused_computation | custom fusion | bytes 7340160 | tf_op jit(solution)/shard_map/jit(_take)/gather | solution.py:202
  12.5 9.0 %all-to-all-start = ((bf16[32,32,2,896]{3,2,1,0:T(2,128)(2,1)}), bf16[32,32,2,896]{3,2,1,0:T(2,128)(2,1)}, u32[]{:S(2)}, u32[]{:S(2)}) async-start(bf16[32,32,2,896]{3,2,1,0:T(2,128)(2,1)} %gather_fusion), calls=%async_computation | async-start | bytes 7340032 | tf_op jit(solution)/shard_map/all_to_all | solution.py:204
  21.6 11.7 %gather_fusion.1 = bf16[32,32,2,896]{3,2,1,0:T(2,128)(2,1)} fusion(bf16[32,32,2,896]{3,2,1,0:T(2,128)(2,1)} %param.7, s32[1024]{0:T(1024)S(1)} %pad_clamp_fusion.1), kind=kCustom, calls=%fused_computation.1 | custom fusion | bytes 7340160 | tf_op jit(solution)/shard_map/jit(_take)/gather | solution.py:202
  33.2 70.7 %all-to-all-done = bf16[32,32,2,896]{3,2,1,0:T(2,128)(2,1)} async-done(((bf16[32,32,2,896]{3,2,1,0:T(2,128)(2,1)}), bf16[32,32,2,896]{3,2,1,0:T(2,128)(2,1)}, u32[]{:S(2)}, u32[]{:S(2)}) %all-to-all-start) | async-done | bytes 3670048 | tf_op jit(solution)/shard_map/all_to_all | solution.py:204
  103.9 8.7 %reshape.23 = bf16[2048,896]{1,0:T(8,128)(2,1)} reshape(bf16[32,32,2,896]{3,2,1,0:T(2,128)(2,1)} %all-to-all-done) | data formatting | bytes 7340032 | tf_op jit(solution)/shard_map/reshape | solution.py:204
  112.6 0.0 copy-done
  112.6 8.2 %convolution_convert_fusion.1.x_ref = bf16[2048,1024]{1,0:T(8,128)(2,1)} fusion(bf16[2048,896]{1,0:T(8,128)(2,1)} %reshape.23, bf16[1024,896]{1,0:T(8,128)(2,1)S(1)} %copy-done), kind=kOutput, calls=%fused_computation.4 | convolution fusion | flops 3760193536 | bytes 9699328 | tf_op jit(solution)/shard_map/dot_general | solution.py:207
  120.8 6.4 %all-to-all-start.1 = ((bf16[32,32,2,896]{3,2,1,0:T(2,128)(2,1)}), bf16[32,32,2,896]{3,2,1,0:T(2,128)(2,1)}, u32[]{:S(2)}, u32[]{:S(2)}) async-start(bf16[32,32,2,896]{3,2,1,0:T(2,128)(2,1)} %gather_fusion.1), calls=%async_computation.1 | async-start | bytes 7340032 | tf_op jit(solution)/shard_map/all_to_all | solution.py:204
  127.2 0.0 copy-done.10
  127.2 0.1 copy.14
  127.3 0.1 reshape.45
  127.4 0.0 copy-start.9
  127.4 0.0 copy-start.8
  127.5 4.2 %gather_fusion.2 = bf16[64,32,896]{2,1,0:T(8,128)(2,1)} fusion(bf16[32,32,896]{2,1,0:T(8,128)(2,1)} %param.8, s32[1024]{0:T(1024)S(1)} %pad_clamp_fusion), kind=kCustom, calls=%fused_computation.2 | custom fusion | bytes 7340288 | tf_op jit(solution)/shard_map/jit(_take)/gather | solution.py:197
  131.7 0.0 copy-done.9
  131.7 0.2 convert_reduce_fusion
  131.9 0.1 broadcast_bitcast_fusion
  132.0 0.0 copy-start.2
  132.0 2.2 copy-done.2
  134.2 82.0 %shard_map.64 = f32[256,1024]{1,0:T(8,128)S(1)} custom-call(bf16[2048,1024]{1,0:T(8,128)(2,1)S(1)} %copy-done.2), custom_call_target="tpu_custom_call" | custom-call | tf_op jit(solution)/shard_map/pallas_call | solution.py:82
  216.2 1.6 reshape.25
  217.8 2.5 fusion.12
  220.3 0.1 copy.17
  220.4 0.1 copy.18
  220.5 0.2 fusion.5.h_ref
  220.7 24.9 %shard_map.65 = bf16[1024,1024]{1,0:T(8,128)(2,1)S(1)} custom-call(bf16[128,1024]{1,0:T(8,128)(2,1)S(1)} %fusion.5.h_ref), custom_call_target="tpu_custom_call" | custom-call | tf_op jit(solution)/shard_map/pallas_call | solution.py:166
  245.6 1.3 copy-done.4
  246.9 0.0 all-to-all-done.1
  246.9 8.7 %reshape.24 = bf16[2048,896]{1,0:T(8,128)(2,1)} reshape(bf16[32,32,2,896]{3,2,1,0:T(2,128)(2,1)} %all-to-all-done.1) | data formatting | bytes 7340032 | tf_op jit(solution)/shard_map/reshape | solution.py:204
  255.6 8.2 %convolution_convert_fusion.x_ref = bf16[2048,1024]{1,0:T(8,128)(2,1)} fusion(bf16[2048,896]{1,0:T(8,128)(2,1)} %reshape.24, bf16[1024,896]{1,0:T(8,128)(2,1)S(1)} %copy-done), kind=kOutput, calls=%fused_computation.3 | convolution fusion | flops 3760193536 | bytes 9699328 | tf_op jit(solution)/shard_map/dot_general | solution.py:207
  263.8 14.8 %all-to-all-start.2 = ((bf16[32,2,32,896]{3,2,1,0:T(8,128)(2,1)}), bf16[32,2,32,896]{3,2,1,0:T(8,128)(2,1)}, u32[]{:S(2)}, u32[]{:S(2)}) async-start(bf16[32,2,32,896]{3,2,1,0:T(8,128)(2,1)} %bitcast.61), calls=%async_computation.2 | async-start | bytes 7340032 | tf_op jit(solution)/shard_map/all_to_all | solution.py:215
  278.7 2.2 copy-done.3
  280.9 85.1 %shard_map.66 = f32[256,1024]{1,0:T(8,128)S(1)} custom-call(bf16[2048,1024]{1,0:T(8,128)(2,1)S(1)} %copy-done.3), custom_call_target="tpu_custom_call" | custom-call | tf_op jit(solution)/shard_map/pallas_call | solution.py:82
  366.0 0.6 reshape.26
  366.6 0.8 fusion.11
  367.4 0.1 copy.19
  367.5 0.1 copy.20
  367.6 0.2 fusion.h_ref
  367.8 29.0 %shard_map.67 = bf16[1024,1024]{1,0:T(8,128)(2,1)S(1)} custom-call(bf16[128,1024]{1,0:T(8,128)(2,1)S(1)} %fusion.h_ref), custom_call_target="tpu_custom_call" | custom-call | tf_op jit(solution)/shard_map/pallas_call | solution.py:166
  396.9 1.4 copy-done.6
  398.3 0.0 all-to-all-done.2
  398.3 2.5 fusion.10
  400.8 0.2 copy-done.5
  401.0 2.4 fusion.14
  403.4 0.0 copy-start.1
  403.4 3.7 add_convert_fusion
  (14 shorter events, 0.1 us)
Async XLA Ops:
  0.0 112.6 %copy-start = (bf16[1024,896]{1,0:T(8,128)(2,1)S(1)}, bf16[1024,896]{1,0:T(8,128)(2,1)}, u32[]{:S(2)}) copy-start(bf16[1024,896]{1,0:T(8,128)(2,1)} %param.6) | copy-start | bytes 5505028
  12.5 91.4 %all-to-all-start = ((bf16[32,32,2,896]{3,2,1,0:T(2,128)(2,1)}), bf16[32,32,2,896]{3,2,1,0:T(2,128)(2,1)}, u32[]{:S(2)}, u32[]{:S(2)}) async-start(bf16[32,32,2,896]{3,2,1,0:T(2,128)(2,1)} %gather_fusion), calls=%async_computation | async-start | bytes 7340032 | tf_op jit(solution)/shard_map/all_to_all | solution.py:204
  120.8 6.4 %copy-start.10 = (s32[32,2]{0,1:T(2,128)S(1)}, s32[32,2]{0,1:T(2,128)}, u32[]{:S(2)}) copy-start(s32[32,2]{0,1:T(2,128)} %param.9) | copy-start | bytes 772
  120.8 126.1 %all-to-all-start.1 = ((bf16[32,32,2,896]{3,2,1,0:T(2,128)(2,1)}), bf16[32,32,2,896]{3,2,1,0:T(2,128)(2,1)}, u32[]{:S(2)}, u32[]{:S(2)}) async-start(bf16[32,32,2,896]{3,2,1,0:T(2,128)(2,1)} %gather_fusion.1), calls=%async_computation.1 | async-start | bytes 7340032 | tf_op jit(solution)/shard_map/all_to_all | solution.py:204
  127.4 4.3 %copy-start.9 = (s32[32,2,8]{0,2,1:T(8,128)S(1)}, s32[32,2,8]{0,2,1:T(8,128)}, u32[]{:S(2)}) copy-start(s32[32,2,8]{0,2,1:T(8,128)} %param.10) | copy-start | bytes 6148
  127.4 4.5 %copy-start.8 = (f32[1024,2]{0,1:T(2,128)S(1)}, f32[1024,2]{0,1:T(2,128)}, u32[]{:S(2)}) copy-start(f32[1024,2]{0,1:T(2,128)} %param.11) | copy-start | bytes 24580
  132.0 2.2 copy-start.2
  245.6 1.3 copy-start.4
  263.8 134.5 %all-to-all-start.2 = ((bf16[32,2,32,896]{3,2,1,0:T(8,128)(2,1)}), bf16[32,2,32,896]{3,2,1,0:T(8,128)(2,1)}, u32[]{:S(2)}, u32[]{:S(2)}) async-start(bf16[32,2,32,896]{3,2,1,0:T(8,128)(2,1)} %bitcast.61), calls=%async_computation.2 | async-start | bytes 7340032 | tf_op jit(solution)/shard_map/all_to_all | solution.py:215
  278.7 2.2 copy-start.3
  396.8 1.4 copy-start.6
  398.3 2.7 copy-start.5
  401.0 2.4 copy-start.7
  403.4 3.7 copy-start.1

commit v8 on v6

--- a/solution.py
+++ b/solution.py
@@ -203,16 +203,22 @@
         pending, piece = lax.optimization_barrier((pending, piece))
         weight_in = lax.all_to_all(piece, "dp", 0, 0, tiled=True).reshape(-1, width_here)
         if hiddens:
-            weight_in, hiddens[-1] = lax.optimization_barrier((weight_in, hiddens[-1]))
+            previous = hiddens.pop()
+            if slot == slots - 1:
+                weight_in, previous, send_out = lax.optimization_barrier((weight_in, previous, send_out))
+                weights_out = lax.all_to_all(send_out, "dp", 0, 0, tiled=True)
+            gathered = group_all_gather(previous, collective_id=slots + slot - 1)
+            weight_in, gathered = lax.optimization_barrier((weight_in, gathered))
+            hiddens.append(gathered)
         partial_here = jnp.dot(weight_in, tokens.T, preferred_element_type=jnp.float32)
         partial_here = partial_here.astype(jnp.bfloat16)
         shares = group_reduce_scatter(partial_here, collective_id=slot)
         shares = shares.reshape(n_dp // group_size, 2, ff_here, row_count)
         hidden = (token_scale[slot] * jax.nn.silu(shares[:, 0]) * shares[:, 1]).astype(jnp.bfloat16)
-        hiddens.append(group_all_gather(hidden.reshape(-1, row_count), collective_id=slots + slot))
+        hiddens.append(hidden.reshape(-1, row_count))
         pending = partial_here
-    pending, send_out = lax.optimization_barrier((pending, send_out))
-    weights_out = lax.all_to_all(send_out, "dp", 0, 0, tiled=True)
+    hiddens[-1] = group_all_gather(hiddens[-1], collective_id=2 * slots - 1)
+    weights_out = weights_out.reshape(n_dp, slots, -1, width_here)
 
     combined = None
     for slot in range(slots):

time: 387 us -> 434 us (1.12)
  Pallas kernels: 228 us -> 262 us
  waiting for transfers between devices: 70.9 us -> 86.4 us
    pallas_call x2, Pallas kernels: 59.7 us -> 117 us  [group_all_gather(): pl.pallas_call(_ag_kernel, out_shape=jax.ShapeDtypeStruct((size * n, c),...]
    pallas_call x2, Pallas kernels: 168 us -> 145 us  [group_reduce_scatter(): pl.pallas_call(_rs_kernel, out_shape=jax.ShapeDtypeStruct((r // size, c),...]
    all_to_all x2, waiting for transfers between devices: 70.9 us -> 86.4 us  [on_device(): lax.all_to_all(piece, 'dp', 0, 0, tiled=True).reshape(-1, width_here)]
  transfers between devices with their start and end apart: 3 -> 3, of which waited for: 1 -> 2; matrix products, arithmetic and copies ran while one was open for 4% -> 5% of each run, Pallas kernels for 59% -> 60%
where the time goes in v8:
time: 434 us; the launch traced here: 433 us
  Pallas kernels  262 us (60%)
  waiting for transfers between devices  86.4 us (20%)
  local copies, waits for them, and re-layouts  44 us (10%)
  starting transfers between devices  21.2 us (5%)
  matrix products  19.2 us (4%)
    pallas_call x2, Pallas kernels, group_reduce_scatter(): pl.pallas_call(_rs_kernel, out_shape=jax.ShapeDtypeStruct((r // size, c),...  145 us
    pallas_call x2, Pallas kernels, group_all_gather(): pl.pallas_call(_ag_kernel, out_shape=jax.ShapeDtypeStruct((size * n, c),...  117 us
    all_to_all x2, waiting for transfers between devices, on_device(): lax.all_to_all(piece, 'dp', 0, 0, tiled=True).reshape(-1, width_here)  86.4 us
    gather x2, local copies, waits for them, and re-layouts, on_device(): jnp.take(proj_in, expert_list[:, slot], axis=0, mode='clip')  23.3 us
    all_to_all x2, starting transfers between devices, on_device(): lax.all_to_all(piece, 'dp', 0, 0, tiled=True).reshape(-1, width_here)  15.2 us
    dot_general x2, matrix products, on_device(): jnp.dot(weight_in, tokens.T, preferred_element_type=jnp.float32)  13.1 us
  transfers between devices with their start and end apart: 3, of which 2 were waited for; matrix products, arithmetic and copies ran while one was open for 5% of the time, Pallas kernels for 60%

profile of v8, /device:TPU:24, one launch (start us, length us, event | category | flops | bytes accessed | tf_op | source)
XLA Modules:
  0.0 433.0 jit_solution(5044314414937378261)
XLA Ops:
  0.0 0.0 copy-start
  0.0 0.8 slice_bitcast_fusion
  0.8 11.7 %gather_fusion = bf16[32,32,2,896]{3,2,1,0:T(2,128)(2,1)} fusion(bf16[32,32,2,896]{3,2,1,0:T(2,128)(2,1)} %param.7, s32[1024]{0:T(1024)S(1)} %get-tuple-element.30), kind=kCustom, calls=%fused_computation | custom fusion | bytes 7340160 | tf_op jit(solution)/shard_map/jit(_take)/gather | solution.py:202
  12.5 8.9 %all-to-all-start = ((bf16[32,2,32,896]{3,1,2,0:T(2,128)(2,1)}), bf16[32,2,32,896]{3,1,2,0:T(2,128)(2,1)}, u32[]{:S(2)}, u32[]{:S(2)}) async-start(bf16[32,2,32,896]{3,1,2,0:T(2,128)(2,1)} %bitcast.79), calls=%async_computation | async-start | bytes 7340032 | tf_op jit(solution)/shard_map/all_to_all | solution.py:204
  21.4 11.7 %gather_fusion.1 = bf16[32,32,2,896]{3,2,1,0:T(2,128)(2,1)} fusion(bf16[32,32,2,896]{3,2,1,0:T(2,128)(2,1)} %param.7, s32[1024]{0:T(1024)S(1)} %get-tuple-element.29), kind=kCustom, calls=%fused_computation.1 | custom fusion | bytes 7340160 | tf_op jit(solution)/shard_map/jit(_take)/gather | solution.py:202
  33.1 70.9 %all-to-all-done = bf16[32,2,32,896]{3,1,2,0:T(2,128)(2,1)} async-done(((bf16[32,2,32,896]{3,1,2,0:T(2,128)(2,1)}), bf16[32,2,32,896]{3,1,2,0:T(2,128)(2,1)}, u32[]{:S(2)}, u32[]{:S(2)}) %all-to-all-start) | async-done | bytes 3670048 | tf_op jit(solution)/shard_map/all_to_all | solution.py:204
  103.9 2.7 copy.17
  106.6 0.0 copy-done
  106.6 6.3 %convolution_convert_fusion.1.x_ref = bf16[2048,1024]{1,0:T(8,128)(2,1)} fusion(bf16[2048,896]{1,0:T(8,128)(2,1)S(1)} %bitcast.81, bf16[1024,896]{1,0:T(8,128)(2,1)S(1)} %copy-done), kind=kOutput, calls=%fused_computation.4 | convolution fusion | flops 3760193536 | bytes 9699328 | tf_op jit(solution)/shard_map/dot_general | solution.py:213
  112.9 0.0 copy-start.8
  112.9 6.3 %all-to-all-start.1 = ((bf16[32,2,32,896]{3,1,2,0:T(2,128)(2,1)}), bf16[32,2,32,896]{3,1,2,0:T(2,128)(2,1)}, u32[]{:S(2)}, u32[]{:S(2)}) async-start(bf16[32,2,32,896]{3,1,2,0:T(2,128)(2,1)} %bitcast.78), calls=%async_computation.1 | async-start | bytes 7340032 | tf_op jit(solution)/shard_map/all_to_all | solution.py:204
  119.3 0.0 copy-done.8
  119.3 0.1 copy.21
  119.4 0.1 reshape.45
  119.5 0.0 copy-start.7
  119.5 0.0 copy-start.6
  119.5 4.2 gather_fusion.2
  123.8 0.0 copy-done.7
  123.8 0.2 convert_reduce_fusion
  123.9 0.1 broadcast_bitcast_fusion
  124.0 0.0 copy-done.6
  124.0 0.0 copy-start.1
  124.1 2.2 copy-done.1
  126.2 82.0 %shard_map.64 = f32[256,1024]{1,0:T(8,128)S(1)} custom-call(bf16[2048,1024]{1,0:T(8,128)(2,1)S(1)} %copy-done.1), custom_call_target="tpu_custom_call" | custom-call | tf_op jit(solution)/shard_map/pallas_call | solution.py:82
  208.3 0.1 fusion.12
  208.4 0.2 fusion.5.h_ref
  208.6 15.5 %all-to-all-done.1 = bf16[32,2,32,896]{3,1,2,0:T(2,128)(2,1)} async-done(((bf16[32,2,32,896]{3,1,2,0:T(2,128)(2,1)}), bf16[32,2,32,896]{3,1,2,0:T(2,128)(2,1)}, u32[]{:S(2)}, u32[]{:S(2)}) %all-to-all-start.1) | async-done | bytes 3670048 | tf_op jit(solution)/shard_map/all_to_all | solution.py:204
  224.1 4.6 %copy.18 = bf16[32,2,32,896]{3,2,1,0:T(8,128)(2,1)} copy(bf16[32,2,32,896]{3,1,2,0:T(2,128)(2,1)} %all-to-all-done.1) | data formatting | bytes 7340032 | tf_op jit(solution)/shard_map/all_to_all | solution.py:204
  228.7 6.0 %all-to-all-start.2 = ((bf16[32,2,32,896]{3,2,1,0:T(8,128)(2,1)}), bf16[32,2,32,896]{3,2,1,0:T(8,128)(2,1)}, u32[]{:S(2)}, u32[]{:S(2)}) async-start(bf16[32,2,32,896]{3,2,1,0:T(8,128)(2,1)} %bitcast.77), calls=%async_computation.2 | async-start | bytes 7340032 | tf_op jit(solution)/shard_map/all_to_all | solution.py:209
  234.8 93.3 %shard_map.65 = bf16[1024,1024]{1,0:T(8,128)(2,1)S(1)} custom-call(bf16[128,1024]{1,0:T(8,128)(2,1)S(1)} %fusion.5.h_ref), custom_call_target="tpu_custom_call" | custom-call | tf_op jit(solution)/shard_map/pallas_call | solution.py:166
  328.0 0.0 copy-start.2
  328.1 1.4 copy-done.2
  329.5 6.8 %convolution_convert_fusion.x_ref = bf16[2048,1024]{1,0:T(8,128)(2,1)S(1)} fusion(bf16[2048,896]{1,0:T(8,128)(2,1)} %bitcast.80, bf16[1024,896]{1,0:T(8,128)(2,1)S(1)} %copy-done), kind=kOutput, calls=%fused_computation.3 | convolution fusion | flops 3760193536 | bytes 9699328 | tf_op jit(solution)/shard_map/dot_general | solution.py:213
  336.3 62.8 %shard_map.66 = f32[256,1024]{1,0:T(8,128)S(1)} custom-call(bf16[2048,1024]{1,0:T(8,128)(2,1)S(1)} %convolution_convert_fusion.x_ref), custom_call_target="tpu_custom_call" | custom-call | tf_op jit(solution)/shard_map/pallas_call | solution.py:82
  399.1 0.1 fusion.11
  399.2 0.2 fusion.h_ref
  399.4 23.5 %shard_map.67 = bf16[1024,1024]{1,0:T(8,128)(2,1)S(1)} custom-call(bf16[128,1024]{1,0:T(8,128)(2,1)S(1)} %fusion.h_ref), custom_call_target="tpu_custom_call" | custom-call | tf_op jit(solution)/shard_map/pallas_call | solution.py:166
  422.8 0.0 copy-start.4
  422.9 1.4 copy-done.4
  424.2 0.0 all-to-all-done.2
  424.2 0.0 copy-start.3
  424.3 2.5 fusion.10
  426.8 0.2 copy-done.3
  426.9 0.0 copy-start.5
  427.0 2.4 fusion.14
  429.3 0.0 copy-done.5
  429.3 3.7 add_convert_fusion
  (4 shorter events, 0.0 us)
Async XLA Ops:
  0.0 106.6 %copy-start = (bf16[1024,896]{1,0:T(8,128)(2,1)S(1)}, bf16[1024,896]{1,0:T(8,128)(2,1)}, u32[]{:S(2)}) copy-start(bf16[1024,896]{1,0:T(8,128)(2,1)} %param.6) | copy-start | bytes 5505028
  12.5 91.4 %all-to-all-start = ((bf16[32,2,32,896]{3,1,2,0:T(2,128)(2,1)}), bf16[32,2,32,896]{3,1,2,0:T(2,128)(2,1)}, u32[]{:S(2)}, u32[]{:S(2)}) async-start(bf16[32,2,32,896]{3,1,2,0:T(2,128)(2,1)} %bitcast.79), calls=%async_computation | async-start | bytes 7340032 | tf_op jit(solution)/shard_map/all_to_all | solution.py:204
  112.9 6.4 %copy-start.8 = (s32[32,2]{0,1:T(2,128)S(1)}, s32[32,2]{0,1:T(2,128)}, u32[]{:S(2)}) copy-start(s32[32,2]{0,1:T(2,128)} %param.9) | copy-start | bytes 772
  112.9 111.2 %all-to-all-start.1 = ((bf16[32,2,32,896]{3,1,2,0:T(2,128)(2,1)}), bf16[32,2,32,896]{3,1,2,0:T(2,128)(2,1)}, u32[]{:S(2)}, u32[]{:S(2)}) async-start(bf16[32,2,32,896]{3,1,2,0:T(2,128)(2,1)} %bitcast.78), calls=%async_computation.1 | async-start | bytes 7340032 | tf_op jit(solution)/shard_map/all_to_all | solution.py:204
  119.5 4.3 copy-start.7
  119.5 4.5 %copy-start.6 = (f32[1024,2]{0,1:T(2,128)S(1)}, f32[1024,2]{0,1:T(2,128)}, u32[]{:S(2)}) copy-start(f32[1024,2]{0,1:T(2,128)} %param.11) | copy-start | bytes 24580
  124.0 2.2 copy-start.1
  228.7 195.5 %all-to-all-start.2 = ((bf16[32,2,32,896]{3,2,1,0:T(8,128)(2,1)}), bf16[32,2,32,896]{3,2,1,0:T(8,128)(2,1)}, u32[]{:S(2)}, u32[]{:S(2)}) async-start(bf16[32,2,32,896]{3,2,1,0:T(8,128)(2,1)} %bitcast.77), calls=%async_computation.2 | async-start | bytes 7340032 | tf_op jit(solution)/shard_map/all_to_all | solution.py:209
  328.0 1.5 copy-start.2
  422.8 1.4 copy-start.4
  424.2 2.7 copy-start.3
  426.9 2.4 copy-start.5

commit v9 on v6

--- a/solution.py
+++ b/solution.py
@@ -197,22 +197,27 @@
     send_out = jnp.take(proj_out, expert_list, axis=0, mode="clip")
 
     hiddens = []
-    pending = tokens
+    pieces = [
+        jnp.take(proj_in, expert_list[:, slot], axis=0, mode="clip").transpose(0, 2, 1, 3)
+        for slot in range(slots)
+    ]
+    weight_in = lax.all_to_all(pieces[0], "dp", 0, 0, tiled=True)
     for slot in range(slots):
-        piece = jnp.take(proj_in, expert_list[:, slot], axis=0, mode="clip").transpose(0, 2, 1, 3)
-        pending, piece = lax.optimization_barrier((pending, piece))
-        weight_in = lax.all_to_all(piece, "dp", 0, 0, tiled=True).reshape(-1, width_here)
         if hiddens:
             weight_in, hiddens[-1] = lax.optimization_barrier((weight_in, hiddens[-1]))
-        partial_here = jnp.dot(weight_in, tokens.T, preferred_element_type=jnp.float32)
+        partial_here = jnp.dot(weight_in.reshape(-1, width_here), tokens.T, preferred_element_type=jnp.float32)
         partial_here = partial_here.astype(jnp.bfloat16)
+        if slot == 0:
+            partial_here, rest = lax.optimization_barrier((partial_here, pieces[1:] + [send_out]))
+            rest = lax.all_to_all(jnp.concatenate(rest, axis=1), "dp", 0, 0, tiled=True)
+            later = [rest[:, 2 * k:2 * k + 2] for k in range(slots - 1)]
+            weights_out = rest[:, 2 * (slots - 1):]
         shares = group_reduce_scatter(partial_here, collective_id=slot)
         shares = shares.reshape(n_dp // group_size, 2, ff_here, row_count)
         hidden = (token_scale[slot] * jax.nn.silu(shares[:, 0]) * shares[:, 1]).astype(jnp.bfloat16)
         hiddens.append(group_all_gather(hidden.reshape(-1, row_count), collective_id=slots + slot))
-        pending = partial_here
-    pending, send_out = lax.optimization_barrier((pending, send_out))
-    weights_out = lax.all_to_all(send_out, "dp", 0, 0, tiled=True)
+        if slot + 1 < slots:
+            weight_in = later[slot]
 
     combined = None
     for slot in range(slots):

time: 387 us -> 470 us (1.21)
  Pallas kernels: 228 us -> 282 us
  local copies, waits for them, and re-layouts: 44.1 us -> 62.5 us
  other arithmetic: 0.5 us -> 9.42 us
  waiting for transfers between devices: 70.9 us -> 79.8 us
  starting transfers between devices: 24.3 us -> 15.6 us
    pallas_call x2, Pallas kernels: 168 us -> 230 us  [group_reduce_scatter(): pl.pallas_call(_rs_kernel, out_shape=jax.ShapeDtypeStruct((r // size, c),...]
    all_to_all x3 -> x2, waiting for transfers between devices: 70.9 us -> 79.8 us  [the longest x1 66.1 us: on_device(): weight_in = lax.all_to_all(pieces[0], 'dp', 0, 0, tiled=True)]
    concatenate x0 -> x1, other arithmetic: none -> 8.92 us  [on_device(): rest = lax.all_to_all(jnp.concatenate(rest, axis=1), 'dp', 0, 0, tiled=True)]
    all_to_all x3 -> x2, starting transfers between devices: 24.3 us -> 15.6 us  [the longest x1 9.17 us: on_device(): weight_in = lax.all_to_all(pieces[0], 'dp', 0, 0, tiled=True)]
    slice x1, local copies, waits for them, and re-layouts: 2.52 us -> 11 us  [on_device(): weights_out[:, slot].reshape(-1, width_here)]
    slice x0 -> x1, local copies, waits for them, and re-layouts: none -> 8.03 us  [on_device(): later = [rest[:, 2 * k:2 * k + 2] for k in range(slots - 1)]]
    pallas_call x2, Pallas kernels: 59.7 us -> 52.7 us  [group_all_gather(): pl.pallas_call(_ag_kernel, out_shape=jax.ShapeDtypeStruct((size * n, c),...]
    optimization_barrier x0 -> x2, local copies, waits for them, and re-layouts: none -> 6.36 us  [the longest x1 3.64 us: on_device(): lax.optimization_barrier((partial_here, pieces[1:] + [send_out]))]
  transfers between devices with their start and end apart: 3 -> 2, of which waited for: 1 -> 2; matrix products, arithmetic and copies ran while one was open for 4% -> 4% of each run, Pallas kernels for 59% -> 38%
where the time goes in v9:
time: 470 us; the launch traced here: 467 us
  Pallas kernels  282 us (60%)
  waiting for transfers between devices  79.8 us (17%)
  local copies, waits for them, and re-layouts  62.5 us (13%)
  matrix products  17.4 us (4%)
  starting transfers between devices  15.6 us (3%)
  other arithmetic  9.42 us (2%)
    pallas_call x2, Pallas kernels, group_reduce_scatter(): pl.pallas_call(_rs_kernel, out_shape=jax.ShapeDtypeStruct((r // size, c),...  230 us
    all_to_all x1, waiting for transfers between devices, on_device(): weight_in = lax.all_to_all(pieces[0], 'dp', 0, 0, tiled=True)  66.1 us
    pallas_call x2, Pallas kernels, group_all_gather(): pl.pallas_call(_ag_kernel, out_shape=jax.ShapeDtypeStruct((size * n, c),...  52.7 us
    gather x2, local copies, waits for them, and re-layouts, on_device(): jnp.take(proj_in, expert_list[:, slot], axis=0, mode='clip')  23.3 us
    all_to_all x1, waiting for transfers between devices, on_device(): rest = lax.all_to_all(jnp.concatenate(rest, axis=1), 'dp', 0, 0, tiled=True)  13.7 us
    dot_general x2, matrix products, on_device(): jnp.dot(weight_in.reshape(-1, width_here), tokens.T, preferred_element_ty...  11.2 us
    slice x1, local copies, waits for them, and re-layouts, on_device(): weights_out[:, slot].reshape(-1, width_here)  11 us
  transfers between devices with their start and end apart: 2, of which 2 were waited for; matrix products, arithmetic and copies ran while one was open for 4% of the time, Pallas kernels for 38%

profile of v9, /device:TPU:24, one launch (start us, length us, event | category | flops | bytes accessed | tf_op | source)
XLA Modules:
  0.0 467.3 jit_solution(14511514751342173267)
XLA Ops:
  0.0 0.0 copy-start
  0.0 0.8 slice_bitcast_fusion
  0.8 11.6 %gather_fusion = bf16[32,32,2,896]{3,2,1,0:T(2,128)(2,1)} fusion(bf16[32,32,2,896]{3,2,1,0:T(2,128)(2,1)} %param.7, s32[1024]{0:T(1024)S(1)} %get-tuple-element.26), kind=kCustom, calls=%fused_computation | custom fusion | bytes 7340160 | tf_op jit(solution)/shard_map/jit(_take)/gather | solution.py:201
  12.5 9.2 %all-to-all-start = ((bf16[32,2,32,896]{3,1,2,0:T(2,128)(2,1)}), bf16[32,2,32,896]{3,1,2,0:T(2,128)(2,1)}, u32[]{:S(2)}, u32[]{:S(2)}) async-start(bf16[32,2,32,896]{3,1,2,0:T(2,128)(2,1)} %bitcast.79), calls=%async_computation | async-start | bytes 7340032 | tf_op jit(solution)/shard_map/all_to_all | solution.py:204
  21.7 0.0 copy-done.9
  21.7 0.1 copy.20
  21.7 11.7 %gather_fusion.1 = bf16[32,32,2,896]{3,2,1,0:T(2,128)(2,1)} fusion(bf16[32,32,2,896]{3,2,1,0:T(2,128)(2,1)} %param.7, s32[1024]{0:T(1024)S(1)} %get-tuple-element.25), kind=kCustom, calls=%fused_computation.1 | custom fusion | bytes 7340160 | tf_op jit(solution)/shard_map/jit(_take)/gather | solution.py:201
  33.4 0.1 reshape.45
  33.5 4.4 gather_fusion.2
  37.9 66.1 %all-to-all-done = bf16[32,2,32,896]{3,1,2,0:T(2,128)(2,1)} async-done(((bf16[32,2,32,896]{3,1,2,0:T(2,128)(2,1)}), bf16[32,2,32,896]{3,1,2,0:T(2,128)(2,1)}, u32[]{:S(2)}, u32[]{:S(2)}) %all-to-all-start) | async-done | bytes 3670048 | tf_op jit(solution)/shard_map/all_to_all | solution.py:204
  104.0 2.7 copy.19
  106.7 0.0 copy-done
  106.7 0.0 copy-start.6
  106.7 6.4 %convolution_convert_fusion.1.x_ref = bf16[2048,1024]{1,0:T(8,128)(2,1)} fusion(bf16[2048,896]{1,0:T(8,128)(2,1)S(1)} %bitcast.80, bf16[1024,896]{1,0:T(8,128)(2,1)S(1)} %copy-done), kind=kOutput, calls=%fused_computation.5 | convolution fusion | flops 3760193536 | bytes 9699328 | tf_op jit(solution)/shard_map/dot_general | solution.py:208
  113.1 0.0 copy-done.6
  113.1 3.6 copy.21
  116.8 0.0 copy-done.5
  116.8 8.9 %pad_maximum_fusion = bf16[32,4,32,896]{3,1,2,0:T(4,128)(2,1)} fusion(bf16[32,2,32,896]{3,1,2,0:T(2,128)(2,1)S(1)} %copy.21, bf16[32,2,32,896]{3,1,2,0:T(2,128)(2,1)S(1)} %bitcast.77), kind=kLoop, calls=%fused_computation.3 | loop fusion | flops 14680064 | bytes 14680064 | tf_op jit(solution)/shard_map/concatenate | solution.py:212
  125.7 6.4 %all-to-all-start.1 = ((bf16[32,4,32,896]{3,1,2,0:T(4,128)(2,1)}), bf16[32,4,32,896]{3,1,2,0:T(4,128)(2,1)}, u32[]{:S(2)}, u32[]{:S(2)}) async-start(bf16[32,4,32,896]{3,1,2,0:T(4,128)(2,1)} %pad_maximum_fusion), calls=%async_computation.1 | async-start | bytes 14680064 | tf_op jit(solution)/shard_map/all_to_all | solution.py:212
  132.1 0.0 copy-done.8
  132.1 0.2 convert_reduce_fusion
  132.2 0.1 broadcast_bitcast_fusion
  132.3 0.0 copy-done.7
  132.4 0.0 copy-start.2
  132.4 2.2 copy-done.2
  134.5 153.2 %shard_map.64 = f32[256,1024]{1,0:T(8,128)S(1)} custom-call(bf16[2048,1024]{1,0:T(8,128)(2,1)S(1)} %copy-done.2), custom_call_target="tpu_custom_call" | custom-call | tf_op jit(solution)/shard_map/pallas_call | solution.py:82
  287.8 0.1 fusion.12
  287.9 0.2 fusion.5.h_ref
  288.0 25.1 %shard_map.65 = bf16[1024,1024]{1,0:T(8,128)(2,1)S(1)} custom-call(bf16[128,1024]{1,0:T(8,128)(2,1)S(1)} %fusion.5.h_ref), custom_call_target="tpu_custom_call" | custom-call | tf_op jit(solution)/shard_map/pallas_call | solution.py:166
  313.2 0.0 copy-start.3
  313.2 1.3 copy-done.3
  314.5 13.7 %all-to-all-done.1 = bf16[32,4,32,896]{3,1,2,0:T(4,128)(2,1)} async-done(((bf16[32,4,32,896]{3,1,2,0:T(4,128)(2,1)}), bf16[32,4,32,896]{3,1,2,0:T(4,128)(2,1)}, u32[]{:S(2)}, u32[]{:S(2)}) %all-to-all-start.1) | async-done | bytes 7340064 | tf_op jit(solution)/shard_map/all_to_all | solution.py:212
  328.2 8.0 %slice.53 = bf16[32,2,32,896]{3,1,2,0:T(2,128)(2,1)} slice(bf16[32,4,32,896]{3,1,2,0:T(4,128)(2,1)} %all-to-all-done.1), slice={[0:32], [0:2], [0:32], [0:896]} | slice | bytes 7340032 | tf_op jit(solution)/shard_map/slice | solution.py:213
  336.2 2.7 copy.24
  338.9 4.9 %convolution_convert_fusion.x_ref = bf16[2048,1024]{1,0:T(8,128)(2,1)S(1)} fusion(bf16[2048,896]{1,0:T(8,128)(2,1)S(1)} %bitcast.81, bf16[1024,896]{1,0:T(8,128)(2,1)S(1)} %copy-done), kind=kOutput, calls=%fused_computation.4 | convolution fusion | flops 3760193536 | bytes 9699328 | tf_op jit(solution)/shard_map/dot_general | solution.py:208
  343.8 76.5 %shard_map.66 = f32[256,1024]{1,0:T(8,128)S(1)} custom-call(bf16[2048,1024]{1,0:T(8,128)(2,1)S(1)} %convolution_convert_fusion.x_ref), custom_call_target="tpu_custom_call" | custom-call | tf_op jit(solution)/shard_map/pallas_call | solution.py:82
  420.3 0.1 fusion.11
  420.4 0.2 fusion.h_ref
  420.6 27.5 %shard_map.67 = bf16[1024,1024]{1,0:T(8,128)(2,1)S(1)} custom-call(bf16[128,1024]{1,0:T(8,128)(2,1)S(1)} %fusion.h_ref), custom_call_target="tpu_custom_call" | custom-call | tf_op jit(solution)/shard_map/pallas_call | solution.py:166
  448.1 11.0 %fusion.10 = (bf16[32,1,32,896]{3,1,2,0:T(2,128)(2,1)S(1)}, bf16[32,1,32,896]{3,1,2,0:T(2,128)(2,1)S(1)}) fusion(bf16[32,4,32,896]{3,1,2,0:T(4,128)(2,1)} %all-to-all-done.1), kind=kLoop, calls=%fused_computation.31 | loop fusion | bytes 7340032 | tf_op jit(solution)/shard_map/slice | solution.py:225
  459.1 0.4 copy.27
  459.5 0.0 copy-start.4
  459.5 0.4 copy.28
  459.9 1.2 copy-done.4
  461.1 2.4 fusion.14
  463.5 0.0 copy-start.1
  463.5 3.8 add_convert_fusion
  467.3 0.0 copy-done.1
  (8 shorter events, 0.0 us)
Async XLA Ops:
  0.0 106.7 %copy-start = (bf16[1024,896]{1,0:T(8,128)(2,1)S(1)}, bf16[1024,896]{1,0:T(8,128)(2,1)}, u32[]{:S(2)}) copy-start(bf16[1024,896]{1,0:T(8,128)(2,1)} %param.6) | copy-start | bytes 5505028
  12.5 9.2 %copy-start.9 = (s32[32,2]{0,1:T(2,128)S(1)}, s32[32,2]{0,1:T(2,128)}, u32[]{:S(2)}) copy-start(s32[32,2]{0,1:T(2,128)} %param.9) | copy-start | bytes 772
  12.5 91.5 %all-to-all-start = ((bf16[32,2,32,896]{3,1,2,0:T(2,128)(2,1)}), bf16[32,2,32,896]{3,1,2,0:T(2,128)(2,1)}, u32[]{:S(2)}, u32[]{:S(2)}) async-start(bf16[32,2,32,896]{3,1,2,0:T(2,128)(2,1)} %bitcast.79), calls=%async_computation | async-start | bytes 7340032 | tf_op jit(solution)/shard_map/all_to_all | solution.py:204
  106.7 6.4 %copy-start.6 = (bf16[64,32,896]{2,1,0:T(8,128)(2,1)S(1)}, bf16[64,32,896]{2,1,0:T(8,128)(2,1)}, u32[]{:S(2)}) copy-start(bf16[64,32,896]{2,1,0:T(8,128)(2,1)} %gather_fusion.2) | copy-start | bytes 11010052
  113.1 3.7 copy-start.5
  125.7 6.4 %copy-start.8 = (s32[32,2,8]{0,2,1:T(8,128)S(1)}, s32[32,2,8]{0,2,1:T(8,128)}, u32[]{:S(2)}) copy-start(s32[32,2,8]{0,2,1:T(8,128)} %param.10) | copy-start | bytes 6148
  125.7 6.6 %copy-start.7 = (f32[1024,2]{0,1:T(2,128)S(1)}, f32[1024,2]{0,1:T(2,128)}, u32[]{:S(2)}) copy-start(f32[1024,2]{0,1:T(2,128)} %param.11) | copy-start | bytes 24580
  125.7 202.5 %all-to-all-start.1 = ((bf16[32,4,32,896]{3,1,2,0:T(4,128)(2,1)}), bf16[32,4,32,896]{3,1,2,0:T(4,128)(2,1)}, u32[]{:S(2)}, u32[]{:S(2)}) async-start(bf16[32,4,32,896]{3,1,2,0:T(4,128)(2,1)} %pad_maximum_fusion), calls=%async_computation.1 | async-start | bytes 14680064 | tf_op jit(solution)/shard_map/all_to_all | solution.py:212
  132.4 2.2 copy-start.2
  313.2 1.3 copy-start.3
  459.5 1.6 copy-start.4
  463.5 3.8 copy-start.1

commit v10 on v6

--- a/solution.py
+++ b/solution.py
@@ -214,13 +214,11 @@
     pending, send_out = lax.optimization_barrier((pending, send_out))
     weights_out = lax.all_to_all(send_out, "dp", 0, 0, tiled=True)
 
-    combined = None
-    for slot in range(slots):
-        term = lax.dot_general(
-            hiddens[slot], weights_out[:, slot].reshape(-1, width_here), (((0,), (0,)), ((), ())),
-            preferred_element_type=jnp.float32,
-        )
-        combined = term if combined is None else combined + term
+    hidden_all = jnp.stack(hiddens).reshape(slots, n_dp, ff_here, row_count)
+    combined = lax.dot_general(
+        hidden_all, weights_out, (((0, 1, 2), (1, 0, 2)), ((), ())),
+        preferred_element_type=jnp.float32,
+    )
     return combined.astype(jnp.bfloat16)
 
 

time: 387 us -> 388 us (level)
    dot_general x2 -> x1, matrix products: 6.07 us -> 9.1 us  [on_device(): lax.dot_general(hidden_all, weights_out, (((0, 1, 2), (1, 0, 2)), ((), ()...]
where the time goes in v10:
time: 388 us; the launch traced here: 387 us
  Pallas kernels  228 us (59%)
  waiting for transfers between devices  70.9 us (18%)
  local copies, waits for them, and re-layouts  41.4 us (11%)
  starting transfers between devices  24.3 us (6%)
  matrix products  21.7 us (6%)
    pallas_call x2, Pallas kernels, group_reduce_scatter(): pl.pallas_call(_rs_kernel, out_shape=jax.ShapeDtypeStruct((r // size, c),...  168 us
    all_to_all x2, waiting for transfers between devices, on_device(): lax.all_to_all(piece, 'dp', 0, 0, tiled=True).reshape(-1, width_here)  70.9 us
    pallas_call x2, Pallas kernels, group_all_gather(): pl.pallas_call(_ag_kernel, out_shape=jax.ShapeDtypeStruct((size * n, c),...  59.7 us
    gather x2, local copies, waits for them, and re-layouts, on_device(): jnp.take(proj_in, expert_list[:, slot], axis=0, mode='clip')  23.3 us
    all_to_all x2, starting transfers between devices, on_device(): lax.all_to_all(piece, 'dp', 0, 0, tiled=True).reshape(-1, width_here)  15.2 us
    dot_general x2, matrix products, on_device(): jnp.dot(weight_in, tokens.T, preferred_element_type=jnp.float32)  12.6 us
    all_to_all x1, starting transfers between devices, on_device(): weights_out = lax.all_to_all(send_out, 'dp', 0, 0, tiled=True)  9.11 us
    dot_general x1, matrix products, on_device(): lax.dot_general(hidden_all, weights_out, (((0, 1, 2), (1, 0, 2)), ((), ()...  9.1 us
  transfers between devices with their start and end apart: 3, of which 1 were waited for; matrix products, arithmetic and copies ran while one was open for 4% of the time, Pallas kernels for 59%

profile of v10, /device:TPU:24, one launch (start us, length us, event | category | flops | bytes accessed | tf_op | source)
XLA Modules:
  0.0 386.5 jit_solution(13213571963588568073)
XLA Ops:
  0.0 0.0 copy-start
  0.0 0.8 slice_bitcast_fusion
  0.8 11.7 %gather_fusion = bf16[32,32,2,896]{3,2,1,0:T(2,128)(2,1)} fusion(bf16[32,32,2,896]{3,2,1,0:T(2,128)(2,1)} %param.7, s32[1024]{0:T(1024)S(1)} %get-tuple-element.24), kind=kCustom, calls=%fused_computation | custom fusion | bytes 7340160 | tf_op jit(solution)/shard_map/jit(_take)/gather | solution.py:202
  12.5 8.9 %all-to-all-start = ((bf16[32,2,32,896]{3,1,2,0:T(2,128)(2,1)}), bf16[32,2,32,896]{3,1,2,0:T(2,128)(2,1)}, u32[]{:S(2)}, u32[]{:S(2)}) async-start(bf16[32,2,32,896]{3,1,2,0:T(2,128)(2,1)} %bitcast.81), calls=%async_computation | async-start | bytes 7340032 | tf_op jit(solution)/shard_map/all_to_all | solution.py:204
  21.4 11.6 %gather_fusion.1 = bf16[32,32,2,896]{3,2,1,0:T(2,128)(2,1)} fusion(bf16[32,32,2,896]{3,2,1,0:T(2,128)(2,1)} %param.7, s32[1024]{0:T(1024)S(1)} %get-tuple-element.23), kind=kCustom, calls=%fused_computation.1 | custom fusion | bytes 7340160 | tf_op jit(solution)/shard_map/jit(_take)/gather | solution.py:202
  33.0 70.9 %all-to-all-done = bf16[32,2,32,896]{3,1,2,0:T(2,128)(2,1)} async-done(((bf16[32,2,32,896]{3,1,2,0:T(2,128)(2,1)}), bf16[32,2,32,896]{3,1,2,0:T(2,128)(2,1)}, u32[]{:S(2)}, u32[]{:S(2)}) %all-to-all-start) | async-done | bytes 3670048 | tf_op jit(solution)/shard_map/all_to_all | solution.py:204
  103.9 2.7 copy.26
  106.6 0.0 copy-done
  106.6 6.3 %convolution_convert_fusion.1.x_ref = bf16[2048,1024]{1,0:T(8,128)(2,1)} fusion(bf16[2048,896]{1,0:T(8,128)(2,1)S(1)} %bitcast.82, bf16[1024,896]{1,0:T(8,128)(2,1)S(1)} %copy-done), kind=kOutput, calls=%fused_computation.8 | convolution fusion | flops 3760193536 | bytes 9699328 | tf_op jit(solution)/shard_map/dot_general | solution.py:207
  112.9 0.0 copy-start.7
  112.9 6.3 %all-to-all-start.1 = ((bf16[32,2,32,896]{3,1,2,0:T(2,128)(2,1)}), bf16[32,2,32,896]{3,1,2,0:T(2,128)(2,1)}, u32[]{:S(2)}, u32[]{:S(2)}) async-start(bf16[32,2,32,896]{3,1,2,0:T(2,128)(2,1)} %bitcast.80), calls=%async_computation.1 | async-start | bytes 7340032 | tf_op jit(solution)/shard_map/all_to_all | solution.py:204
  119.3 0.0 copy-done.7
  119.3 0.1 copy.32
  119.4 0.1 reshape.50
  119.5 0.0 copy-start.6
  119.5 0.0 copy-start.5
  119.5 4.2 %gather_fusion.2 = bf16[64,32,896]{2,1,0:T(8,128)(2,1)} fusion(bf16[32,32,896]{2,1,0:T(8,128)(2,1)} %param.8, s32[1024]{0:T(1024)S(1)} %pad_clamp_fusion), kind=kCustom, calls=%fused_computation.2 | custom fusion | bytes 7340288 | tf_op jit(solution)/shard_map/jit(_take)/gather | solution.py:197
  123.8 0.0 copy-done.6
  123.8 0.2 convert_reduce_fusion
  123.9 0.1 broadcast_bitcast_fusion
  124.0 0.0 copy-done.5
  124.0 0.0 copy-start.1
  124.0 2.2 copy-done.1
  126.2 82.2 %shard_map.64 = f32[256,1024]{1,0:T(8,128)S(1)} custom-call(bf16[2048,1024]{1,0:T(8,128)(2,1)S(1)} %copy-done.1), custom_call_target="tpu_custom_call" | custom-call | tf_op jit(solution)/shard_map/pallas_call | solution.py:82
  208.4 0.1 fusion.21
  208.5 0.2 fusion.14.h_ref
  208.7 29.3 %shard_map.65 = bf16[1024,1024]{1,0:T(8,128)(2,1)S(1)} custom-call(bf16[128,1024]{1,0:T(8,128)(2,1)S(1)} %fusion.14.h_ref), custom_call_target="tpu_custom_call" | custom-call | tf_op jit(solution)/shard_map/pallas_call | solution.py:166
  238.0 0.0 copy-start.3
  238.0 1.3 copy-done.3
  239.3 0.0 all-to-all-done.1
  239.3 2.7 copy.27
  242.0 6.3 %convolution_convert_fusion.x_ref = bf16[2048,1024]{1,0:T(8,128)(2,1)} fusion(bf16[2048,896]{1,0:T(8,128)(2,1)S(1)} %bitcast.83, bf16[1024,896]{1,0:T(8,128)(2,1)S(1)} %copy-done), kind=kOutput, calls=%fused_computation.7 | convolution fusion | flops 3760193536 | bytes 9699328 | tf_op jit(solution)/shard_map/dot_general | solution.py:207
  248.3 9.1 %all-to-all-start.2 = ((bf16[32,2,32,896]{3,2,1,0:T(8,128)(2,1)}), bf16[32,2,32,896]{3,2,1,0:T(8,128)(2,1)}, u32[]{:S(2)}, u32[]{:S(2)}) async-start(bf16[32,2,32,896]{3,2,1,0:T(8,128)(2,1)} %bitcast.79), calls=%async_computation.2 | async-start | bytes 7340032 | tf_op jit(solution)/shard_map/all_to_all | solution.py:215
  257.4 0.0 copy-start.2
  257.4 2.2 copy-done.2
  259.6 85.7 %shard_map.66 = f32[256,1024]{1,0:T(8,128)S(1)} custom-call(bf16[2048,1024]{1,0:T(8,128)(2,1)S(1)} %copy-done.2), custom_call_target="tpu_custom_call" | custom-call | tf_op jit(solution)/shard_map/pallas_call | solution.py:82
  345.3 0.1 fusion.20
  345.4 0.2 fusion.9.h_ref
  345.6 30.4 %shard_map.67 = bf16[1024,1024]{1,0:T(8,128)(2,1)S(1)} custom-call(bf16[128,1024]{1,0:T(8,128)(2,1)S(1)} %fusion.9.h_ref), custom_call_target="tpu_custom_call" | custom-call | tf_op jit(solution)/shard_map/pallas_call | solution.py:166
  376.0 0.0 copy-start.4
  376.0 1.4 copy-done.4
  377.4 0.0 all-to-all-done.2
  377.4 9.1 %bitcast_convert_fusion = bf16[1024,896]{1,0:T(8,128)(2,1)} fusion(bf16[32,2,32,896]{3,2,1,0:T(8,128)(2,1)} %all-to-all-done.2, bf16[1,32,32,1024]{3,2,1,0:T(8,128)(2,1)} %bitcast.78, bf16[1,32,32,1024]{3,2,1,0:T(8,128)(2,1)} %bitcast.77), kind=kOutput, calls=%fused_computation.9 | convolution fusion | flops 3761111040 | bytes 9699328 | tf_op jit(solution)/shard_map/dot_general | solution.py:218
  (4 shorter events, 0.0 us)
Async XLA Ops:
  0.0 106.6 %copy-start = (bf16[1024,896]{1,0:T(8,128)(2,1)S(1)}, bf16[1024,896]{1,0:T(8,128)(2,1)}, u32[]{:S(2)}) copy-start(bf16[1024,896]{1,0:T(8,128)(2,1)} %param.6) | copy-start | bytes 5505028
  12.5 91.4 %all-to-all-start = ((bf16[32,2,32,896]{3,1,2,0:T(2,128)(2,1)}), bf16[32,2,32,896]{3,1,2,0:T(2,128)(2,1)}, u32[]{:S(2)}, u32[]{:S(2)}) async-start(bf16[32,2,32,896]{3,1,2,0:T(2,128)(2,1)} %bitcast.81), calls=%async_computation | async-start | bytes 7340032 | tf_op jit(solution)/shard_map/all_to_all | solution.py:204
  112.9 6.4 %copy-start.7 = (s32[32,2]{0,1:T(2,128)S(1)}, s32[32,2]{0,1:T(2,128)}, u32[]{:S(2)}) copy-start(s32[32,2]{0,1:T(2,128)} %param.9) | copy-start | bytes 772
  112.9 126.4 %all-to-all-start.1 = ((bf16[32,2,32,896]{3,1,2,0:T(2,128)(2,1)}), bf16[32,2,32,896]{3,1,2,0:T(2,128)(2,1)}, u32[]{:S(2)}, u32[]{:S(2)}) async-start(bf16[32,2,32,896]{3,1,2,0:T(2,128)(2,1)} %bitcast.80), calls=%async_computation.1 | async-start | bytes 7340032 | tf_op jit(solution)/shard_map/all_to_all | solution.py:204
  119.5 4.3 %copy-start.6 = (s32[32,2,8]{0,2,1:T(8,128)S(1)}, s32[32,2,8]{0,2,1:T(8,128)}, u32[]{:S(2)}) copy-start(s32[32,2,8]{0,2,1:T(8,128)} %param.10) | copy-start | bytes 6148
  119.5 4.5 %copy-start.5 = (f32[1024,2]{0,1:T(2,128)S(1)}, f32[1024,2]{0,1:T(2,128)}, u32[]{:S(2)}) copy-start(f32[1024,2]{0,1:T(2,128)} %param.11) | copy-start | bytes 24580
  124.0 2.2 copy-start.1
  238.0 1.3 copy-start.3
  248.3 129.1 %all-to-all-start.2 = ((bf16[32,2,32,896]{3,2,1,0:T(8,128)(2,1)}), bf16[32,2,32,896]{3,2,1,0:T(8,128)(2,1)}, u32[]{:S(2)}, u32[]{:S(2)}) async-start(bf16[32,2,32,896]{3,2,1,0:T(8,128)(2,1)} %bitcast.79), calls=%async_computation.2 | async-start | bytes 7340032 | tf_op jit(solution)/shard_map/all_to_all | solution.py:215
  257.4 2.2 copy-start.2
  376.0 1.4 copy-start.4

commit v11 on v6

--- a/solution.py
+++ b/solution.py
@@ -202,6 +202,8 @@
         piece = jnp.take(proj_in, expert_list[:, slot], axis=0, mode="clip").transpose(0, 2, 1, 3)
         pending, piece = lax.optimization_barrier((pending, piece))
         weight_in = lax.all_to_all(piece, "dp", 0, 0, tiled=True).reshape(-1, width_here)
+        if not hiddens:
+            weight_in, send_out = lax.optimization_barrier((weight_in, send_out))
         if hiddens:
             weight_in, hiddens[-1] = lax.optimization_barrier((weight_in, hiddens[-1]))
         partial_here = jnp.dot(weight_in, tokens.T, preferred_element_type=jnp.float32)

time: 387 us -> 386 us (level)
  waiting for transfers between devices: 70.9 us -> 66.4 us
  Pallas kernels: 228 us -> 232 us
    all_to_all x2, waiting for transfers between devices: 70.9 us -> 66.4 us  [on_device(): lax.all_to_all(piece, 'dp', 0, 0, tiled=True).reshape(-1, width_here)]
    pallas_call x2, Pallas kernels: 168 us -> 172 us  [group_reduce_scatter(): pl.pallas_call(_rs_kernel, out_shape=jax.ShapeDtypeStruct((r // size, c),...]
  transfers between devices with their start and end apart: 3 -> 3, of which waited for: 1 -> 1; matrix products, arithmetic and copies ran while one was open for 4% -> 4% of each run, Pallas kernels for 59% -> 61%
where the time goes in v11:
time: 386 us; the launch traced here: 384 us
  Pallas kernels  232 us (60%)
  waiting for transfers between devices  66.4 us (17%)
  local copies, waits for them, and re-layouts  44.1 us (11%)
  starting transfers between devices  21.9 us (6%)
  matrix products  18.6 us (5%)
    pallas_call x2, Pallas kernels, group_reduce_scatter(): pl.pallas_call(_rs_kernel, out_shape=jax.ShapeDtypeStruct((r // size, c),...  172 us
    all_to_all x2, waiting for transfers between devices, on_device(): lax.all_to_all(piece, 'dp', 0, 0, tiled=True).reshape(-1, width_here)  66.4 us
    pallas_call x2, Pallas kernels, group_all_gather(): pl.pallas_call(_ag_kernel, out_shape=jax.ShapeDtypeStruct((size * n, c),...  60.6 us
    gather x2, local copies, waits for them, and re-layouts, on_device(): jnp.take(proj_in, expert_list[:, slot], axis=0, mode='clip')  23.3 us
    all_to_all x2, starting transfers between devices, on_device(): lax.all_to_all(piece, 'dp', 0, 0, tiled=True).reshape(-1, width_here)  15.3 us
    dot_general x2, matrix products, on_device(): jnp.dot(weight_in, tokens.T, preferred_element_type=jnp.float32)  12.6 us
  transfers between devices with their start and end apart: 3, of which 1 were waited for; matrix products, arithmetic and copies ran while one was open for 4% of the time, Pallas kernels for 61%

profile of v11, /device:TPU:24, one launch (start us, length us, event | category | flops | bytes accessed | tf_op | source)
XLA Modules:
  0.0 384.2 jit_solution(17228499385423970522)
XLA Ops:
  0.0 0.0 copy-start
  0.0 0.8 slice_bitcast_fusion
  0.8 11.6 %gather_fusion = bf16[32,32,2,896]{3,2,1,0:T(2,128)(2,1)} fusion(bf16[32,32,2,896]{3,2,1,0:T(2,128)(2,1)} %param.7, s32[1024]{0:T(1024)S(1)} %get-tuple-element.30), kind=kCustom, calls=%fused_computation | custom fusion | bytes 7340160 | tf_op jit(solution)/shard_map/jit(_take)/gather | solution.py:202
  12.5 0.0 copy-start.9
  12.5 9.0 %all-to-all-start = ((bf16[32,2,32,896]{3,1,2,0:T(2,128)(2,1)}), bf16[32,2,32,896]{3,1,2,0:T(2,128)(2,1)}, u32[]{:S(2)}, u32[]{:S(2)}) async-start(bf16[32,2,32,896]{3,1,2,0:T(2,128)(2,1)} %bitcast.79), calls=%async_computation | async-start | bytes 7340032 | tf_op jit(solution)/shard_map/all_to_all | solution.py:204
  21.5 0.0 copy-done.9
  21.5 0.1 copy.18
  21.6 0.1 reshape.37
  21.7 11.7 %gather_fusion.2 = bf16[32,32,2,896]{3,2,1,0:T(2,128)(2,1)} fusion(bf16[32,32,2,896]{3,2,1,0:T(2,128)(2,1)} %param.7, s32[1024]{0:T(1024)S(1)} %get-tuple-element.29), kind=kCustom, calls=%fused_computation.2 | custom fusion | bytes 7340160 | tf_op jit(solution)/shard_map/jit(_take)/gather | solution.py:202
  33.3 4.2 %gather_fusion.1 = bf16[64,32,896]{2,1,0:T(8,128)(2,1)} fusion(bf16[32,32,896]{2,1,0:T(8,128)(2,1)} %param.8, s32[1024]{0:T(1024)S(1)} %pad_clamp_fusion.1), kind=kCustom, calls=%fused_computation.1 | custom fusion | bytes 7340288 | tf_op jit(solution)/shard_map/jit(_take)/gather | solution.py:197
  37.6 66.4 %all-to-all-done = bf16[32,2,32,896]{3,1,2,0:T(2,128)(2,1)} async-done(((bf16[32,2,32,896]{3,1,2,0:T(2,128)(2,1)}), bf16[32,2,32,896]{3,1,2,0:T(2,128)(2,1)}, u32[]{:S(2)}, u32[]{:S(2)}) %all-to-all-start) | async-done | bytes 3670048 | tf_op jit(solution)/shard_map/all_to_all | solution.py:204
  104.0 2.7 copy.17
  106.7 0.0 copy-done
  106.7 6.3 %convolution_convert_fusion.1.x_ref = bf16[2048,1024]{1,0:T(8,128)(2,1)} fusion(bf16[2048,896]{1,0:T(8,128)(2,1)S(1)} %bitcast.80, bf16[1024,896]{1,0:T(8,128)(2,1)S(1)} %copy-done), kind=kOutput, calls=%fused_computation.4 | convolution fusion | flops 3760193536 | bytes 9699328 | tf_op jit(solution)/shard_map/dot_general | solution.py:209
  113.0 0.0 copy-start.8
  113.0 0.0 copy-start.7
  113.0 6.3 %all-to-all-start.1 = ((bf16[32,2,32,896]{3,1,2,0:T(2,128)(2,1)}), bf16[32,2,32,896]{3,1,2,0:T(2,128)(2,1)}, u32[]{:S(2)}, u32[]{:S(2)}) async-start(bf16[32,2,32,896]{3,1,2,0:T(2,128)(2,1)} %bitcast.78), calls=%async_computation.1 | async-start | bytes 7340032 | tf_op jit(solution)/shard_map/all_to_all | solution.py:204
  119.4 0.0 copy-done.8
  119.4 0.2 convert_reduce_fusion
  119.5 0.1 broadcast_bitcast_fusion
  119.6 0.0 copy-done.7
  119.7 0.0 copy-start.1
  119.7 2.2 copy-done.1
  121.8 86.9 %shard_map.64 = f32[256,1024]{1,0:T(8,128)S(1)} custom-call(bf16[2048,1024]{1,0:T(8,128)(2,1)S(1)} %copy-done.1), custom_call_target="tpu_custom_call" | custom-call | tf_op jit(solution)/shard_map/pallas_call | solution.py:82
  208.8 0.1 fusion.12
  208.9 0.2 fusion.5.h_ref
  209.1 29.3 %shard_map.65 = bf16[1024,1024]{1,0:T(8,128)(2,1)S(1)} custom-call(bf16[128,1024]{1,0:T(8,128)(2,1)S(1)} %fusion.5.h_ref), custom_call_target="tpu_custom_call" | custom-call | tf_op jit(solution)/shard_map/pallas_call | solution.py:166
  238.4 0.0 copy-start.3
  238.4 1.3 copy-done.3
  239.7 0.0 all-to-all-done.1
  239.7 2.7 copy.19
  242.4 6.3 %convolution_convert_fusion.x_ref = bf16[2048,1024]{1,0:T(8,128)(2,1)} fusion(bf16[2048,896]{1,0:T(8,128)(2,1)S(1)} %bitcast.81, bf16[1024,896]{1,0:T(8,128)(2,1)S(1)} %copy-done), kind=kOutput, calls=%fused_computation.3 | convolution fusion | flops 3760193536 | bytes 9699328 | tf_op jit(solution)/shard_map/dot_general | solution.py:209
  248.7 6.5 %all-to-all-start.2 = ((bf16[32,2,32,896]{3,2,1,0:T(8,128)(2,1)}), bf16[32,2,32,896]{3,2,1,0:T(8,128)(2,1)}, u32[]{:S(2)}, u32[]{:S(2)}) async-start(bf16[32,2,32,896]{3,2,1,0:T(8,128)(2,1)} %bitcast.77), calls=%async_computation.2 | async-start | bytes 7340032 | tf_op jit(solution)/shard_map/all_to_all | solution.py:217
  255.3 0.0 copy-start.2
  255.3 2.2 copy-done.2
  257.4 85.0 %shard_map.66 = f32[256,1024]{1,0:T(8,128)S(1)} custom-call(bf16[2048,1024]{1,0:T(8,128)(2,1)S(1)} %copy-done.2), custom_call_target="tpu_custom_call" | custom-call | tf_op jit(solution)/shard_map/pallas_call | solution.py:82
  342.4 0.1 fusion.11
  342.5 0.2 fusion.h_ref
  342.7 31.2 %shard_map.67 = bf16[1024,1024]{1,0:T(8,128)(2,1)S(1)} custom-call(bf16[128,1024]{1,0:T(8,128)(2,1)S(1)} %fusion.h_ref), custom_call_target="tpu_custom_call" | custom-call | tf_op jit(solution)/shard_map/pallas_call | solution.py:166
  373.9 0.0 copy-start.5
  373.9 1.4 copy-done.5
  375.4 0.0 all-to-all-done.2
  375.4 0.0 copy-start.4
  375.4 2.5 fusion.10
  377.9 0.2 copy-done.4
  378.1 2.4 fusion.14
  380.5 0.0 copy-done.6
  380.5 3.7 add_convert_fusion
  (5 shorter events, 0.0 us)
Async XLA Ops:
  0.0 106.7 %copy-start = (bf16[1024,896]{1,0:T(8,128)(2,1)S(1)}, bf16[1024,896]{1,0:T(8,128)(2,1)}, u32[]{:S(2)}) copy-start(bf16[1024,896]{1,0:T(8,128)(2,1)} %param.6) | copy-start | bytes 5505028
  12.5 9.0 %copy-start.9 = (s32[32,2]{0,1:T(2,128)S(1)}, s32[32,2]{0,1:T(2,128)}, u32[]{:S(2)}) copy-start(s32[32,2]{0,1:T(2,128)} %param.9) | copy-start | bytes 772
  12.5 91.5 %all-to-all-start = ((bf16[32,2,32,896]{3,1,2,0:T(2,128)(2,1)}), bf16[32,2,32,896]{3,1,2,0:T(2,128)(2,1)}, u32[]{:S(2)}, u32[]{:S(2)}) async-start(bf16[32,2,32,896]{3,1,2,0:T(2,128)(2,1)} %bitcast.79), calls=%async_computation | async-start | bytes 7340032 | tf_op jit(solution)/shard_map/all_to_all | solution.py:204
  113.0 6.4 %copy-start.8 = (s32[32,2,8]{0,2,1:T(8,128)S(1)}, s32[32,2,8]{0,2,1:T(8,128)}, u32[]{:S(2)}) copy-start(s32[32,2,8]{0,2,1:T(8,128)} %param.10) | copy-start | bytes 6148
  113.0 6.6 %copy-start.7 = (f32[1024,2]{0,1:T(2,128)S(1)}, f32[1024,2]{0,1:T(2,128)}, u32[]{:S(2)}) copy-start(f32[1024,2]{0,1:T(2,128)} %param.11) | copy-start | bytes 24580
  113.0 126.7 %all-to-all-start.1 = ((bf16[32,2,32,896]{3,1,2,0:T(2,128)(2,1)}), bf16[32,2,32,896]{3,1,2,0:T(2,128)(2,1)}, u32[]{:S(2)}, u32[]{:S(2)}) async-start(bf16[32,2,32,896]{3,1,2,0:T(2,128)(2,1)} %bitcast.78), calls=%async_computation.1 | async-start | bytes 7340032 | tf_op jit(solution)/shard_map/all_to_all | solution.py:204
  119.7 2.2 copy-start.1
  238.4 1.3 copy-start.3
  248.7 126.7 %all-to-all-start.2 = ((bf16[32,2,32,896]{3,2,1,0:T(8,128)(2,1)}), bf16[32,2,32,896]{3,2,1,0:T(8,128)(2,1)}, u32[]{:S(2)}, u32[]{:S(2)}) async-start(bf16[32,2,32,896]{3,2,1,0:T(8,128)(2,1)} %bitcast.77), calls=%async_computation.2 | async-start | bytes 7340032 | tf_op jit(solution)/shard_map/all_to_all | solution.py:217
  255.3 2.2 copy-start.2
  373.9 1.4 copy-start.5
  375.4 2.7 copy-start.4
  378.1 2.4 copy-start.6

commit v12 on v11

--- a/solution.py
+++ b/solution.py
@@ -130,21 +130,19 @@
     own_lo = pl.multiple_of(zh * n, n)
     other_lo = pl.multiple_of((1 - zh) * n, n)
     zc = remote(h_ref, pbuf, 0, partner)
-    first = [
-        remote(h_ref, ybuf.at[0, pl.ds(own_lo, n)], 1, up),
-        remote(h_ref, ybuf.at[1, pl.ds(own_lo, n)], 2, down),
-    ]
+    own_up = remote(h_ref, ybuf.at[0, pl.ds(own_lo, n)], 1, up)
+    own_down = remote(h_ref, ybuf.at[1, pl.ds(own_lo, n)], 2, down)
+    own_up.wait()
+    relay_up = remote(ybuf.at[0, pl.ds(own_lo, n)], fbuf.at[0], 5, up)
     zc.wait()
-    first += [
+    rest = [
+        own_down,
         remote(pbuf, ybuf.at[0, pl.ds(other_lo, n)], 3, up),
         remote(pbuf, ybuf.at[1, pl.ds(other_lo, n)], 4, down),
     ]
-    for c in first:
+    for c in rest:
         c.wait()
-    second = [
-        remote(ybuf.at[0, pl.ds(0, n)], fbuf.at[0], 5, up),
-        remote(ybuf.at[1, pl.ds(n, n)], fbuf.at[1], 6, down),
-    ]
+    relay_down = remote(ybuf.at[1, pl.ds(other_lo, n)], fbuf.at[1], 6, down)
     pair = 2 * n
 
     def at(dy):
@@ -154,10 +152,10 @@
     out_ref[pl.ds(at(0) + other_lo, n), :] = pbuf[...]
     out_ref[pl.ds(at(-1), pair), :] = ybuf[0]
     out_ref[pl.ds(at(1), pair), :] = ybuf[1]
-    for c in second:
-        c.wait()
-    out_ref[pl.ds(at(2), n), :] = fbuf[0]
-    out_ref[pl.ds(at(2) + n, n), :] = fbuf[1]
+    relay_up.wait()
+    relay_down.wait()
+    out_ref[pl.ds(at(2) + own_lo, n), :] = fbuf[0]
+    out_ref[pl.ds(at(2) + other_lo, n), :] = fbuf[1]
 
 
 def group_all_gather(h, collective_id=0):

time: 386 us -> 390 us (1.010)
  transfers between devices with their start and end apart: 3 -> 3, of which waited for: 1 -> 1; matrix products, arithmetic and copies ran while one was open for 4% -> 4% of each run, Pallas kernels for 61% -> 60%
where the time goes in v12:
time: 390 us; the launch traced here: 388 us
  Pallas kernels  233 us (60%)
  waiting for transfers between devices  66.5 us (17%)
  local copies, waits for them, and re-layouts  44 us (11%)
  starting transfers between devices  24.9 us (6%)
  matrix products  18.6 us (5%)
    pallas_call x2, Pallas kernels, group_reduce_scatter(): pl.pallas_call(_rs_kernel, out_shape=jax.ShapeDtypeStruct((r // size, c),...  174 us
    all_to_all x2, waiting for transfers between devices, on_device(): lax.all_to_all(piece, 'dp', 0, 0, tiled=True).reshape(-1, width_here)  66.5 us
    pallas_call x2, Pallas kernels, group_all_gather(): pl.pallas_call(_ag_kernel, out_shape=jax.ShapeDtypeStruct((size * n, c),...  58.8 us
    gather x2, local copies, waits for them, and re-layouts, on_device(): jnp.take(proj_in, expert_list[:, slot], axis=0, mode='clip')  23.3 us
    all_to_all x2, starting transfers between devices, on_device(): lax.all_to_all(piece, 'dp', 0, 0, tiled=True).reshape(-1, width_here)  15.3 us
    dot_general x2, matrix products, on_device(): jnp.dot(weight_in, tokens.T, preferred_element_type=jnp.float32)  12.6 us
    all_to_all x1, starting transfers between devices, on_device(): weights_out = lax.all_to_all(send_out, 'dp', 0, 0, tiled=True)  9.57 us
  transfers between devices with their start and end apart: 3, of which 1 were waited for; matrix products, arithmetic and copies ran while one was open for 4% of the time, Pallas kernels for 60%

profile of v12, /device:TPU:24, one launch (start us, length us, event | category | flops | bytes accessed | tf_op | source)
XLA Modules:
  0.0 387.6 jit_solution(11348767308718470806)
XLA Ops:
  0.0 0.0 copy-start
  0.0 0.8 slice_bitcast_fusion
  0.8 11.6 %gather_fusion = bf16[32,32,2,896]{3,2,1,0:T(2,128)(2,1)} fusion(bf16[32,32,2,896]{3,2,1,0:T(2,128)(2,1)} %param.7, s32[1024]{0:T(1024)S(1)} %get-tuple-element.30), kind=kCustom, calls=%fused_computation | custom fusion | bytes 7340160 | tf_op jit(solution)/shard_map/jit(_take)/gather | solution.py:200
  12.5 0.0 copy-start.9
  12.5 9.0 %all-to-all-start = ((bf16[32,2,32,896]{3,1,2,0:T(2,128)(2,1)}), bf16[32,2,32,896]{3,1,2,0:T(2,128)(2,1)}, u32[]{:S(2)}, u32[]{:S(2)}) async-start(bf16[32,2,32,896]{3,1,2,0:T(2,128)(2,1)} %bitcast.79), calls=%async_computation | async-start | bytes 7340032 | tf_op jit(solution)/shard_map/all_to_all | solution.py:202
  21.5 0.0 copy-done.9
  21.5 0.1 copy.18
  21.6 0.1 reshape.37
  21.7 11.6 %gather_fusion.2 = bf16[32,32,2,896]{3,2,1,0:T(2,128)(2,1)} fusion(bf16[32,32,2,896]{3,2,1,0:T(2,128)(2,1)} %param.7, s32[1024]{0:T(1024)S(1)} %get-tuple-element.29), kind=kCustom, calls=%fused_computation.2 | custom fusion | bytes 7340160 | tf_op jit(solution)/shard_map/jit(_take)/gather | solution.py:200
  33.3 4.2 %gather_fusion.1 = bf16[64,32,896]{2,1,0:T(8,128)(2,1)} fusion(bf16[32,32,896]{2,1,0:T(8,128)(2,1)} %param.8, s32[1024]{0:T(1024)S(1)} %pad_clamp_fusion.1), kind=kCustom, calls=%fused_computation.1 | custom fusion | bytes 7340288 | tf_op jit(solution)/shard_map/jit(_take)/gather | solution.py:195
  37.6 66.5 %all-to-all-done = bf16[32,2,32,896]{3,1,2,0:T(2,128)(2,1)} async-done(((bf16[32,2,32,896]{3,1,2,0:T(2,128)(2,1)}), bf16[32,2,32,896]{3,1,2,0:T(2,128)(2,1)}, u32[]{:S(2)}, u32[]{:S(2)}) %all-to-all-start) | async-done | bytes 3670048 | tf_op jit(solution)/shard_map/all_to_all | solution.py:202
  104.0 2.7 copy.17
  106.7 0.0 copy-done
  106.7 6.3 %convolution_convert_fusion.1.x_ref = bf16[2048,1024]{1,0:T(8,128)(2,1)} fusion(bf16[2048,896]{1,0:T(8,128)(2,1)S(1)} %bitcast.80, bf16[1024,896]{1,0:T(8,128)(2,1)S(1)} %copy-done), kind=kOutput, calls=%fused_computation.4 | convolution fusion | flops 3760193536 | bytes 9699328 | tf_op jit(solution)/shard_map/dot_general | solution.py:207
  113.0 0.0 copy-start.8
  113.0 0.0 copy-start.7
  113.0 6.3 %all-to-all-start.1 = ((bf16[32,2,32,896]{3,1,2,0:T(2,128)(2,1)}), bf16[32,2,32,896]{3,1,2,0:T(2,128)(2,1)}, u32[]{:S(2)}, u32[]{:S(2)}) async-start(bf16[32,2,32,896]{3,1,2,0:T(2,128)(2,1)} %bitcast.78), calls=%async_computation.1 | async-start | bytes 7340032 | tf_op jit(solution)/shard_map/all_to_all | solution.py:202
  119.4 0.0 copy-done.8
  119.4 0.2 convert_reduce_fusion
  119.6 0.1 broadcast_bitcast_fusion
  119.6 0.0 copy-done.7
  119.7 0.0 copy-start.1
  119.7 2.2 copy-done.1
  121.9 86.9 %shard_map.64 = f32[256,1024]{1,0:T(8,128)S(1)} custom-call(bf16[2048,1024]{1,0:T(8,128)(2,1)S(1)} %copy-done.1), custom_call_target="tpu_custom_call" | custom-call | tf_op jit(solution)/shard_map/pallas_call | solution.py:82
  208.8 0.1 fusion.12
  208.9 0.2 fusion.5.h_ref
  209.1 29.4 %shard_map.65 = bf16[1024,1024]{1,0:T(8,128)(2,1)S(1)} custom-call(bf16[128,1024]{1,0:T(8,128)(2,1)S(1)} %fusion.5.h_ref), custom_call_target="tpu_custom_call" | custom-call | tf_op jit(solution)/shard_map/pallas_call | solution.py:164
  238.5 0.0 copy-start.3
  238.5 1.3 copy-done.3
  239.8 0.0 all-to-all-done.1
  239.8 2.7 copy.19
  242.5 6.3 %convolution_convert_fusion.x_ref = bf16[2048,1024]{1,0:T(8,128)(2,1)} fusion(bf16[2048,896]{1,0:T(8,128)(2,1)S(1)} %bitcast.81, bf16[1024,896]{1,0:T(8,128)(2,1)S(1)} %copy-done), kind=kOutput, calls=%fused_computation.3 | convolution fusion | flops 3760193536 | bytes 9699328 | tf_op jit(solution)/shard_map/dot_general | solution.py:207
  248.8 9.6 %all-to-all-start.2 = ((bf16[32,2,32,896]{3,2,1,0:T(8,128)(2,1)}), bf16[32,2,32,896]{3,2,1,0:T(8,128)(2,1)}, u32[]{:S(2)}, u32[]{:S(2)}) async-start(bf16[32,2,32,896]{3,2,1,0:T(8,128)(2,1)} %bitcast.77), calls=%async_computation.2 | async-start | bytes 7340032 | tf_op jit(solution)/shard_map/all_to_all | solution.py:215
  258.4 0.0 copy-start.2
  258.4 2.2 copy-done.2
  260.6 87.1 %shard_map.66 = f32[256,1024]{1,0:T(8,128)S(1)} custom-call(bf16[2048,1024]{1,0:T(8,128)(2,1)S(1)} %copy-done.2), custom_call_target="tpu_custom_call" | custom-call | tf_op jit(solution)/shard_map/pallas_call | solution.py:82
  347.7 0.1 fusion.11
  347.8 0.2 fusion.h_ref
  347.9 29.4 %shard_map.67 = bf16[1024,1024]{1,0:T(8,128)(2,1)S(1)} custom-call(bf16[128,1024]{1,0:T(8,128)(2,1)S(1)} %fusion.h_ref), custom_call_target="tpu_custom_call" | custom-call | tf_op jit(solution)/shard_map/pallas_call | solution.py:164
  377.3 0.0 copy-start.5
  377.3 1.4 copy-done.5
  378.8 0.0 all-to-all-done.2
  378.8 0.0 copy-start.4
  378.8 2.5 fusion.10
  381.3 0.2 copy-done.4
  381.5 2.4 fusion.14
  383.9 0.0 copy-done.6
  383.9 3.7 add_convert_fusion
  (5 shorter events, 0.0 us)
Async XLA Ops:
  0.0 106.7 %copy-start = (bf16[1024,896]{1,0:T(8,128)(2,1)S(1)}, bf16[1024,896]{1,0:T(8,128)(2,1)}, u32[]{:S(2)}) copy-start(bf16[1024,896]{1,0:T(8,128)(2,1)} %param.6) | copy-start | bytes 5505028
  12.5 9.0 %copy-start.9 = (s32[32,2]{0,1:T(2,128)S(1)}, s32[32,2]{0,1:T(2,128)}, u32[]{:S(2)}) copy-start(s32[32,2]{0,1:T(2,128)} %param.9) | copy-start | bytes 772
  12.5 91.5 %all-to-all-start = ((bf16[32,2,32,896]{3,1,2,0:T(2,128)(2,1)}), bf16[32,2,32,896]{3,1,2,0:T(2,128)(2,1)}, u32[]{:S(2)}, u32[]{:S(2)}) async-start(bf16[32,2,32,896]{3,1,2,0:T(2,128)(2,1)} %bitcast.79), calls=%async_computation | async-start | bytes 7340032 | tf_op jit(solution)/shard_map/all_to_all | solution.py:202
  113.0 6.4 %copy-start.8 = (s32[32,2,8]{0,2,1:T(8,128)S(1)}, s32[32,2,8]{0,2,1:T(8,128)}, u32[]{:S(2)}) copy-start(s32[32,2,8]{0,2,1:T(8,128)} %param.10) | copy-start | bytes 6148
  113.0 6.6 %copy-start.7 = (f32[1024,2]{0,1:T(2,128)S(1)}, f32[1024,2]{0,1:T(2,128)}, u32[]{:S(2)}) copy-start(f32[1024,2]{0,1:T(2,128)} %param.11) | copy-start | bytes 24580
  113.0 126.7 %all-to-all-start.1 = ((bf16[32,2,32,896]{3,1,2,0:T(2,128)(2,1)}), bf16[32,2,32,896]{3,1,2,0:T(2,128)(2,1)}, u32[]{:S(2)}, u32[]{:S(2)}) async-start(bf16[32,2,32,896]{3,1,2,0:T(2,128)(2,1)} %bitcast.78), calls=%async_computation.1 | async-start | bytes 7340032 | tf_op jit(solution)/shard_map/all_to_all | solution.py:202
  119.7 2.2 copy-start.1
  238.5 1.3 copy-start.3
  248.8 130.0 %all-to-all-start.2 = ((bf16[32,2,32,896]{3,2,1,0:T(8,128)(2,1)}), bf16[32,2,32,896]{3,2,1,0:T(8,128)(2,1)}, u32[]{:S(2)}, u32[]{:S(2)}) async-start(bf16[32,2,32,896]{3,2,1,0:T(8,128)(2,1)} %bitcast.77), calls=%async_computation.2 | async-start | bytes 7340032 | tf_op jit(solution)/shard_map/all_to_all | solution.py:215
  258.4 2.2 copy-start.2
  377.3 1.4 copy-start.5
  378.8 2.7 copy-start.4
  381.5 2.4 copy-start.6
